TPU v7x, 32 devices: a whole 2x2x4 slice. The times are simulated.
32 devices in a mesh: gx: 4 (over z), gy: 8 (over y, x, core).
Axes of the slice: x: 2, y: 2, z: 4, core: 2. Of those that a mesh axis runs over, the one named last changes fastest.
Arguments:
- sample_field: float32 [128, 256, 256], P('gx', 'gy'), may hold values from -4 to 4
- mean_shift: float32 [128, 256, 256], P('gx', 'gy'), may hold values from -18 to 18
- class_map: int32 [128, 256, 256], P('gx', 'gy'), may hold values from 0 to 7
- noise_seed: int32 [128, 256, 256], P('gx', 'gy'), may hold values from 0 to 32703
- diffusion_table: float32 [8], replicated, may hold values from 0.5 to 4
- mass_table: float32 [8], replicated, may hold values from 0.1 to 2
Outputs:
- fine_sample: float32 [128, 256, 256], P('gx', 'gy')
- coarse_sample: float32 [16, 32, 32], P('gx', 'gy')
All inputs are finite; a program needn't handle non-finite values.
Results may differ from a plain program's by a relative error of at most 0.0001.
Values sent between devices are 32-bit elements; how exact they have to be, the bound alone decides.
No kernel may reach another device: no remote copies, remote signals or barrier semaphores. Data moves between devices by JAX's collectives and lax.ppermute only.
A program may use at most 192 MiB of HBM per device.

v0:
```python
import jax
import jax.numpy as jnp
from jax import lax
from jax.sharding import PartitionSpec as P

SWEEPS = 3
LEVELS = 4


def with_halo(x, sides, width):
    for axis, dim in sides:
        devices, length = (lax.axis_size(axis), x.shape[dim])
        up = [(i, (i + 1) % devices) for i in range(devices - 1)]
        down = [(j, i) for i, j in up]
        last = lax.slice_in_dim(x, length - width, length, axis=dim)
        leading = lax.slice_in_dim(x, 0, width, axis=dim)
        before = lax.ppermute(last, axis, up)
        after = lax.ppermute(leading, axis, down)
        x = jnp.concatenate([before, x, after], axis=dim)
    return x


def shifted(block, axis, distance):
    devices = range(lax.axis_size(axis))
    route = [(i - distance, i) for i in devices if i - distance in devices]
    return lax.ppermute(block, axis, route)


def lookup(class_map, table):
    result = jnp.zeros(class_map.shape, jnp.float32)
    for class_index in range(table.shape[0]):
        result = jnp.where(class_map == class_index, table[class_index], result)
    return result


def coarsen(values):
    rows_x, rows_y, rows_z = values.shape
    return values.reshape(rows_x // 2, 2, rows_y // 2, 2, rows_z // 2, 2).mean(axis=(1, 3, 5))


def gaussian(seed_field, tag_value):
    first_hash = (seed_field * 40503 + (tag_value + 1) * 12347) % 65521
    second_hash = (seed_field * 30011 + (tag_value + 1) * 7919) % 65519
    first_uniform = (first_hash.astype(jnp.float32) + 0.5) / 65521.0
    second_uniform = (second_hash.astype(jnp.float32) + 0.5) / 65519.0
    return jnp.sqrt(-2.0 * jnp.log(first_uniform)) * jnp.cos(6.283185307179586 * second_uniform)


def face_weights(diff_padded, mass_field, grid_scale):
    centre = diff_padded[1:-1, 1:-1]
    column = jnp.pad(centre, ((0, 0), (0, 0), (1, 1)))
    neighbours = [
        diff_padded[2:, 1:-1],
        diff_padded[:-2, 1:-1],
        diff_padded[1:-1, 2:],
        diff_padded[1:-1, :-2],
        column[:, :, 2:],
        column[:, :, :-2],
    ]
    weights = [grid_scale * 0.5 * (centre + neighbour) for neighbour in neighbours]
    diagonal = mass_field
    for weight in weights:
        diagonal = diagonal + weight
    return (weights, diagonal)


def neighbour_sum(field_padded, weights):
    centre = field_padded[1:-1, 1:-1]
    column = jnp.pad(centre, ((0, 0), (0, 0), (1, 1)))
    neighbours = [
        field_padded[2:, 1:-1],
        field_padded[:-2, 1:-1],
        field_padded[1:-1, 2:],
        field_padded[1:-1, :-2],
        column[:, :, 2:],
        column[:, :, :-2],
    ]
    running = weights[0] * neighbours[0]
    for position in range(1, 6):
        running = running + weights[position] * neighbours[position]
    return running


def heat_bath(current, diagonal, beside_sum, right_side, noise_field, chosen):
    updated = (right_side + beside_sum) / diagonal + noise_field * lax.rsqrt(diagonal)
    return jnp.where(chosen, updated, current)


def parity(block_shape, offset_x, offset_y, colour):
    index_x = lax.broadcasted_iota(jnp.int32, block_shape, 0) + offset_x
    index_y = lax.broadcasted_iota(jnp.int32, block_shape, 1) + offset_y
    index_z = lax.broadcasted_iota(jnp.int32, block_shape, 2)
    return (index_x + index_y + index_z) % 2 == colour


def restrict(residual_padded):

    def along_axis(values, axis_number):
        span_length = values.shape[axis_number] - 1
        thirds = [
            lax.slice_in_dim(values, anchor, anchor + span_length - 1, stride=2, axis=axis_number)
            for anchor in range(3)
        ]
        return 0.5 * thirds[0] + thirds[1] + 0.5 * thirds[2]

    return 0.25 * along_axis(along_axis(along_axis(residual_padded, 0), 1), 2)


def tiled_sweeps(
    current, diffusion, mass_field, right_side, noises, grid_scale, offset_x, offset_y
):
    diff_padded = with_halo(diffusion, (("gx", 0), ("gy", 1)), 1)
    weights, diagonal = face_weights(diff_padded, mass_field, grid_scale)
    for sweep_index in range(len(noises)):
        for colour in range(2):
            field_padded = with_halo(current, (("gx", 0), ("gy", 1)), 1)
            beside_sum = neighbour_sum(field_padded, weights)
            current = heat_bath(
                current,
                diagonal,
                beside_sum,
                right_side,
                noises[sweep_index],
                parity(current.shape, offset_x, offset_y, colour),
            )
    return (current, weights, diagonal)


def per_device(sample_field, mean_shift, class_map, noise_seed, diffusion_table, mass_table):
    index_x = lax.axis_index("gx")
    index_y = lax.axis_index("gy")
    diffusion = lookup(class_map, diffusion_table)
    mass_field = lookup(class_map, mass_table)
    right_side = mean_shift
    current = sample_field
    fine_sample = sample_field
    for level_index in range(LEVELS):
        grid_scale = 0.5**level_index
        factor = 2**level_index
        if level_index > 0:
            diffusion = coarsen(diffusion)
            mass_field = coarsen(mass_field)
            current = jnp.zeros_like(right_side)
        seed_field = noise_seed[::factor, ::factor, ::factor]
        rows_x, rows_y, rows_z = diffusion.shape
        offset_x = index_x * rows_x
        offset_y = index_y * rows_y
        noises = [
            gaussian(seed_field, level_index * SWEEPS + sweep_index)
            for sweep_index in range(SWEEPS)
        ]
        if level_index == LEVELS - 1:
            current, weights, diagonal = tiled_sweeps(
                current, diffusion, mass_field, right_side, noises, grid_scale, offset_x, offset_y
            )
        else:
            current, weights, diagonal = tiled_sweeps(
                current, diffusion, mass_field, right_side, noises, grid_scale, offset_x, offset_y
            )
        if level_index == 0:
            fine_sample = current
        if level_index < LEVELS - 1:
            field_padded = with_halo(current, (("gx", 0), ("gy", 1)), 1)
            beside_sum = neighbour_sum(field_padded, weights)
            residual = right_side - (diagonal * current - beside_sum)
            edge_rows = shifted(residual[-1:], "gx", 1)
            extended = jnp.concatenate([edge_rows, residual], axis=0)
            edge_cols = shifted(extended[:, -1:], "gy", 1)
            extended = jnp.concatenate([edge_cols, extended], axis=1)
            extended = jnp.pad(extended, ((0, 0), (0, 0), (1, 0)))
            right_side = restrict(extended)
    return (fine_sample, current)


def solution(mesh):
    in_specs = (
        P("gx", "gy", None),
        P("gx", "gy", None),
        P("gx", "gy", None),
        P("gx", "gy", None),
        P(),
        P(),
    )
    out_specs = (P("gx", "gy", None), P("gx", "gy", None))
    return jax.shard_map(
        per_device, mesh=mesh, in_specs=in_specs, out_specs=out_specs, check_vma=False
    )
```

profile of v0, /device:TPU:28, one launch (start us, length us, event | category | flops | bytes accessed | tf_op | source)
XLA Modules:
  0.0 805.2 jit_solution(1296313545712334381)
XLA Ops:
  2.3 8.8 %select_select_fusion.1 = (f32[32,32,256]{2,1,0:T(8,128)S(1)}, pred[32,32,256]{2,1,0:T(8,128)(4,1)S(1)}, pred[32,32,256]{2,1,0:T(8,128)(4,1)}, pred[32,32,256]{2...) fusion(f32[]{:T(128)} %bitcast.7, f32[]{:T(128)} %bitcast.6, ...), kind=kLoop, calls=%fused_computation.252 | loop fusion | flops 4194304 | bytes 4194336 | tf_op jit(solution)/shard_map/jit(_where)/select_n | solution.py:32
  16.7 5.8 collective-permute-start.1
  39.8 16.7 %fusion.50 = (f32[32,32,256]{2,1,0:T(8,128)S(1)}, f32[32,32,256]{2,1,0:T(8,128)S(1)}, f32[32,32,256]{2,1,0:T(8,128)S(1)}, f32[32,32,256]{2,1,0:T(8,128)S(1)}) fusion(f32[32,32,256]{2,1,0:T(8,128)S(1)} %copy-done.10, f32[32,32,256]{2,1,0:T(8,128)S(1)} %copy-done, f32[34,32,256]{2,1,0:T(8,128)S(1)} %constant_dynamic-update-slice_fusion, ...), kind=kLoop, calls=%fused_computation.77 | loop fusion | flops 24117248 | bytes 11870496 | tf_op jit(solution)/shard_map/jit(_where)/select_n | solution.py:86
  73.8 9.2 %fusion.58 = f32[32,32,256]{2,1,0:T(8,128)S(1)} fusion(f32[32,32,256]{2,1,0:T(8,128)S(1)} %get-tuple-element.18, f32[32,32,256]{2,1,0:T(8,128)S(1)} %copy-done, f32[32,32,256]{2,1,0:T(8,128)S(1)} %get-tuple-element.21, f32[32,32,256]{2,1,0:T(8,128)S(1)} %get-tuple-element.20, f32[34,1,256]{2,1,0:T(1,128)S(1)} %collective-permute-done.11, ...), kind=kLoop, calls=%fused_computation.85 | loop fusion | flops 22020096 | bytes 8659200 | tf_op jit(solution)/shard_map/jit(_where)/select_n | solution.py:86
  99.9 9.2 %fusion.66 = f32[32,32,256]{2,1,0:T(8,128)S(1)} fusion(f32[32,32,256]{2,1,0:T(8,128)S(1)} %fusion.58, f32[32,32,256]{2,1,0:T(8,128)S(1)} %copy-done, f32[32,32,256]{2,1,0:T(8,128)S(1)} %get-tuple-element.21, f32[32,32,256]{2,1,0:T(8,128)S(1)} %get-tuple-element.20, f32[34,1,256]{2,1,0:T(1,128)S(1)} %collective-permute-done.15, ...), kind=kLoop, calls=%fused_computation.93 | loop fusion | flops 22020096 | bytes 8659200 | tf_op jit(solution)/shard_map/jit(_where)/select_n | solution.py:86
  125.0 9.2 %fusion.74 = f32[32,32,256]{2,1,0:T(8,128)S(1)} fusion(f32[32,32,256]{2,1,0:T(8,128)S(1)} %fusion.66, f32[32,32,256]{2,1,0:T(8,128)S(1)} %copy-done, f32[32,32,256]{2,1,0:T(8,128)S(1)} %get-tuple-element.21, f32[32,32,256]{2,1,0:T(8,128)S(1)} %get-tuple-element.20, f32[34,1,256]{2,1,0:T(1,128)S(1)} %collective-permute-done.19, ...), kind=kLoop, calls=%fused_computation.101 | loop fusion | flops 22020096 | bytes 8659200 | tf_op jit(solution)/shard_map/jit(_where)/select_n | solution.py:86
  150.1 9.2 %fusion.82 = f32[32,32,256]{2,1,0:T(8,128)S(1)} fusion(f32[32,32,256]{2,1,0:T(8,128)S(1)} %fusion.74, f32[32,32,256]{2,1,0:T(8,128)S(1)} %copy-done, f32[32,32,256]{2,1,0:T(8,128)S(1)} %get-tuple-element.21, f32[32,32,256]{2,1,0:T(8,128)S(1)} %get-tuple-element.20, f32[34,1,256]{2,1,0:T(1,128)S(1)} %collective-permute-done.23, ...), kind=kLoop, calls=%fused_computation.109 | loop fusion | flops 22020096 | bytes 8659200 | tf_op jit(solution)/shard_map/jit(_where)/select_n | solution.py:86
  164.1 5.1 collective-permute-start.38
  170.5 68.4 %reshape.27 = f32[16,2,16,2,128,2]{5,4,3,2,1,0:T(8,128)} reshape(f32[32,32,256]{2,1,0:T(8,128)S(1)} %get-tuple-element.22) | data formatting | bytes 2097152 | tf_op jit(solution)/shard_map/reshape | solution.py:38
  238.9 20.8 %reduce_sum.55 = f32[16,16,128]{2,1,0:T(8,128)S(1)} reduce(f32[16,2,16,2,128,2]{5,4,3,2,1,0:T(8,128)} %reshape.27, f32[]{:T(128)} %constant.329.clone.1), dimensions={1,3,5}, to_apply=%region_1.2 | reduce | flops 229376 | bytes 1179652 | tf_op jit(solution)/shard_map/reduce_sum | solution.py:38
  269.0 12.0 %fusion.90 = f32[32,32,256]{2,1,0:T(8,128)S(1)} fusion(f32[32,32,256]{2,1,0:T(8,128)} %copy-done.6, f32[32,32,256]{2,1,0:T(8,128)S(1)} %copy-done, f32[32,32,256]{2,1,0:T(8,128)} %copy-done.3, f32[32,32,256]{2,1,0:T(8,128)S(1)} %copy-done.2, f32[34,1,256]{2,1,0:T(1,128)S(1)} %collective-permute-done.27, f32[1,32,256]{2,1,0:T(8,128)} %copy-done.16, ...), kind=kLoop, calls=%fused_computation.117 | loop fusion | flops 22020096 | bytes 8659200 | tf_op jit(solution)/shard_map/jit(_where)/select_n | solution.py:86
  299.7 9.8 %slice.1317 = s32[16,16,128]{2,1,0:T(8,128)S(1)} slice(s32[32,32,256]{2,1,0:T(8,128)} %param.9), slice={[0:32:2], [0:32:2], [0:256:2]} | slice | bytes 262144 | tf_op jit(solution)/shard_map/slice | solution.py:144
  311.0 7.6 fusion.96
  336.4 68.4 %reshape.26 = f32[16,2,16,2,128,2]{5,4,3,2,1,0:T(8,128)} reshape(f32[32,32,256]{2,1,0:T(8,128)S(1)} %get-tuple-element.19) | data formatting | bytes 2097152 | tf_op jit(solution)/shard_map/reshape | solution.py:38
  404.8 20.8 %reduce_sum.54 = f32[16,16,128]{2,1,0:T(8,128)S(1)} reduce(f32[16,2,16,2,128,2]{5,4,3,2,1,0:T(8,128)} %reshape.26, f32[]{:T(128)} %constant.329.clone.1), dimensions={1,3,5}, to_apply=%region_0.1 | reduce | flops 229376 | bytes 1179652 | tf_op jit(solution)/shard_map/reduce_sum | solution.py:38
  443.3 4.9 collective-permute-start.42
  515.5 9.7 %div.168 = f32[8,2,8,2,64,2]{5,4,3,2,1,0:T(8,128)} reshape(f32[16,16,128]{2,1,0:T(8,128)S(1)} %broadcast_multiply_fusion) | data formatting | bytes 262144 | tf_op jit(solution)/shard_map/div | solution.py:38
  530.9 4.5 collective-permute-start.58
  573.0 4.5 collective-permute-start.74
  581.7 9.7 %div.166 = f32[8,2,8,2,64,2]{5,4,3,2,1,0:T(8,128)} reshape(f32[16,16,128]{2,1,0:T(8,128)S(1)} %broadcast_multiply_fusion.1) | data formatting | bytes 262144 | tf_op jit(solution)/shard_map/div | solution.py:38
  598.0 5.5 collective-permute-start.76
  669.4 4.5 collective-permute-start.92
  707.3 4.5 collective-permute-start.107
  720.5 5.3 collective-permute-start.110
  (433 shorter events, 467.1 us)
Async XLA Ops:
  160.3 99.4 %collective-permute-start.24 = (f32[1,32,256]{2,1,0:T(8,128)S(1)}, f32[1,32,256]{2,1,0:T(8,128)S(1)}, u32[]{:S(2)}, u32[]{:S(2)}) collective-permute-start(f32[1,32,256]{2,1,0:T(8,128)S(1)} %get-tuple-element.50), channel_id=1, source_target_pairs={{8,0},{16,8},{24,16},{9,1},{17,9},{25,17},{10,2},{18,10},{26,18},{... | collective-permute-start | bytes 98312 | tf_op jit(solution)/shard_map/ppermute | solution.py:18
  162.2 97.5 %collective-permute-start.25 = (f32[1,32,256]{2,1,0:T(8,128)S(1)}, f32[1,32,256]{2,1,0:T(8,128)S(1)}, u32[]{:S(2)}, u32[]{:S(2)}) collective-permute-start(f32[1,32,256]{2,1,0:T(8,128)S(1)} %get-tuple-element.49), channel_id=1, source_target_pairs={{0,8},{8,16},{16,24},{1,9},{9,17},{17,25},{2,10},{10,18},{18,26},{... | collective-permute-start | bytes 98312 | tf_op jit(solution)/shard_map/ppermute | solution.py:17
  164.1 164.5 %collective-permute-start.38 = (f32[1,16,128]{2,1,0:T(8,128)}, f32[1,16,128]{2,1,0:T(8,128)}, u32[]{:S(2)}, u32[]{:S(2)}) collective-permute-start(f32[1,16,128]{2,1,0:T(8,128)} %broadcast.373), channel_id=1, source_target_pairs={{8,0},{16,8},{24,16},{9,1},{17,9},{25,17},{10,2},{18,10},{26,18},{... | collective-permute-start | bytes 24584 | tf_op jit(solution)/shard_map/ppermute | solution.py:18
  169.2 159.4 %collective-permute-start.39 = (f32[1,16,128]{2,1,0:T(8,128)}, f32[1,16,128]{2,1,0:T(8,128)}, u32[]{:S(2)}, u32[]{:S(2)}) collective-permute-start(f32[1,16,128]{2,1,0:T(8,128)} %broadcast.373), channel_id=1, source_target_pairs={{0,8},{8,16},{16,24},{1,9},{9,17},{17,25},{2,10},{10,18},{18,26},{... | collective-permute-start | bytes 24584 | tf_op jit(solution)/shard_map/ppermute | solution.py:17
  288.5 31.5 %collective-permute-start.34 = (f32[1,16,128]{2,1,0:T(8,128)}, f32[1,16,128]{2,1,0:T(8,128)S(1)}, u32[]{:S(2)}, u32[]{:S(2)}) collective-permute-start(f32[1,16,128]{2,1,0:T(8,128)} %get-tuple-element.92), channel_id=1, source_target_pairs={{8,0},{16,8},{24,16},{9,1},{17,9},{25,17},{10,2},{18,10},{26,18},{... | collective-permute-start | bytes 24584 | tf_op jit(solution)/shard_map/ppermute | solution.py:18
  320.6 120.9 %collective-permute-start.36 = (f32[18,1,128]{2,1,0:T(1,128)}, f32[18,1,128]{2,1,0:T(1,128)}, u32[]{:S(2)}, u32[]{:S(2)}) collective-permute-start(f32[18,1,128]{2,1,0:T(1,128)} %get-tuple-element.76), channel_id=1, source_target_pairs={{1,0},{2,1},{3,2},{4,3},{5,4},{6,5},{7,6},{9,8},{10,9},{11,10},{12... | collective-permute-start | bytes 27656 | tf_op jit(solution)/shard_map/ppermute | solution.py:18
  324.6 116.8 %collective-permute-start.37 = (f32[18,1,128]{2,1,0:T(1,128)}, f32[18,1,128]{2,1,0:T(1,128)}, u32[]{:S(2)}, u32[]{:S(2)}) collective-permute-start(f32[18,1,128]{2,1,0:T(1,128)} %get-tuple-element.75), channel_id=1, source_target_pairs={{0,1},{1,2},{2,3},{3,4},{4,5},{5,6},{6,7},{8,9},{9,10},{10,11},{11... | collective-permute-start | bytes 27656 | tf_op jit(solution)/shard_map/ppermute | solution.py:17
  326.6 99.0 %collective-permute-start.33 = (f32[33,1,256]{2,1,0:T(1,128)S(1)}, f32[33,1,256]{2,1,0:T(1,128)S(1)}, u32[]{:S(2)}, u32[]{:S(2)}) collective-permute-start(f32[33,1,256]{2,1,0:T(1,128)S(1)} %pad_maximum_fusion.143), channel_id=1, source_target_pairs={{0,1},{1,2},{2,3},{3,4},{4,5},{5,6},{6,7},{8,9},{9,10},{10,11},{11... | collective-permute-start | bytes 101384 | tf_op jit(solution)/shard_map/ppermute | solution.py:26
  329.9 111.6 %collective-permute-start.40 = (f32[18,1,128]{2,1,0:T(1,128)}, f32[18,1,128]{2,1,0:T(1,128)}, u32[]{:S(2)}, u32[]{:S(2)}) collective-permute-start(f32[18,1,128]{2,1,0:T(1,128)} %get-tuple-element.77), channel_id=1, source_target_pairs={{1,0},{2,1},{3,2},{4,3},{5,4},{6,5},{7,6},{9,8},{10,9},{11,10},{12... | collective-permute-start | bytes 27656 | tf_op jit(solution)/shard_map/ppermute | solution.py:18
  334.5 107.0 %collective-permute-start.41 = (f32[18,1,128]{2,1,0:T(1,128)}, f32[18,1,128]{2,1,0:T(1,128)}, u32[]{:S(2)}, u32[]{:S(2)}) collective-permute-start(f32[18,1,128]{2,1,0:T(1,128)} %get-tuple-element.78), channel_id=1, source_target_pairs={{0,1},{1,2},{2,3},{3,4},{4,5},{5,6},{6,7},{8,9},{9,10},{10,11},{11... | collective-permute-start | bytes 27656 | tf_op jit(solution)/shard_map/ppermute | solution.py:17
  507.9 21.3 %collective-permute-start.56 = (f32[18,1,128]{2,1,0:T(1,128)S(1)}, f32[18,1,128]{2,1,0:T(1,128)S(1)}, u32[]{:S(2)}, u32[]{:S(2)}) collective-permute-start(f32[18,1,128]{2,1,0:T(1,128)S(1)} %get-tuple-element.67), channel_id=1, source_target_pairs={{1,0},{2,1},{3,2},{4,3},{5,4},{6,5},{7,6},{9,8},{10,9},{11,10},{12... | collective-permute-start | bytes 27656 | tf_op jit(solution)/shard_map/ppermute | solution.py:18
  509.9 19.4 %collective-permute-start.57 = (f32[18,1,128]{2,1,0:T(1,128)S(1)}, f32[18,1,128]{2,1,0:T(1,128)S(1)}, u32[]{:S(2)}, u32[]{:S(2)}) collective-permute-start(f32[18,1,128]{2,1,0:T(1,128)S(1)} %get-tuple-element.68), channel_id=1, source_target_pairs={{0,1},{1,2},{2,3},{3,4},{4,5},{5,6},{6,7},{8,9},{9,10},{10,11},{11... | collective-permute-start | bytes 27656 | tf_op jit(solution)/shard_map/ppermute | solution.py:17
  512.3 60.6 %collective-permute-start.72 = (f32[1,8,64]{2,1,0:T(8,128)S(1)}, f32[1,8,64]{2,1,0:T(8,128)S(1)}, u32[]{:S(2)}, u32[]{:S(2)}) collective-permute-start(f32[1,8,64]{2,1,0:T(8,128)S(1)} %broadcast.383), channel_id=1, source_target_pairs={{8,0},{16,8},{24,16},{9,1},{17,9},{25,17},{10,2},{18,10},{26,18},{... | collective-permute-start | bytes 6152 | tf_op jit(solution)/shard_map/ppermute | solution.py:18
  514.2 58.7 %collective-permute-start.73 = (f32[1,8,64]{2,1,0:T(8,128)S(1)}, f32[1,8,64]{2,1,0:T(8,128)S(1)}, u32[]{:S(2)}, u32[]{:S(2)}) collective-permute-start(f32[1,8,64]{2,1,0:T(8,128)S(1)} %broadcast.383), channel_id=1, source_target_pairs={{0,8},{8,16},{16,24},{1,9},{9,17},{17,25},{2,10},{10,18},{18,26},{... | collective-permute-start | bytes 6152 | tf_op jit(solution)/shard_map/ppermute | solution.py:17
  545.4 16.8 %collective-permute-start.68 = (f32[1,8,64]{2,1,0:T(8,128)S(1)}, f32[1,8,64]{2,1,0:T(8,128)S(1)}, u32[]{:S(2)}, u32[]{:S(2)}) collective-permute-start(f32[1,8,64]{2,1,0:T(8,128)S(1)} %get-tuple-element.122), channel_id=1, source_target_pairs={{8,0},{16,8},{24,16},{9,1},{17,9},{25,17},{10,2},{18,10},{26,18},{... | collective-permute-start | bytes 6152 | tf_op jit(solution)/shard_map/ppermute | solution.py:18
  564.8 32.9 %collective-permute-start.70 = (f32[10,1,64]{2,1,0:T(1,128)S(1)}, f32[10,1,64]{2,1,0:T(1,128)S(1)}, u32[]{:S(2)}, u32[]{:S(2)}) collective-permute-start(f32[10,1,64]{2,1,0:T(1,128)S(1)} %get-tuple-element.106), channel_id=1, source_target_pairs={{1,0},{2,1},{3,2},{4,3},{5,4},{6,5},{7,6},{9,8},{10,9},{11,10},{12... | collective-permute-start | bytes 7688 | tf_op jit(solution)/shard_map/ppermute | solution.py:18
  568.8 28.9 %collective-permute-start.71 = (f32[10,1,64]{2,1,0:T(1,128)S(1)}, f32[10,1,64]{2,1,0:T(1,128)S(1)}, u32[]{:S(2)}, u32[]{:S(2)}) collective-permute-start(f32[10,1,64]{2,1,0:T(1,128)S(1)} %get-tuple-element.105), channel_id=1, source_target_pairs={{0,1},{1,2},{2,3},{3,4},{4,5},{5,6},{6,7},{8,9},{9,10},{10,11},{11... | collective-permute-start | bytes 7688 | tf_op jit(solution)/shard_map/ppermute | solution.py:17
  573.0 24.7 %collective-permute-start.74 = (f32[10,1,64]{2,1,0:T(1,128)S(1)}, f32[10,1,64]{2,1,0:T(1,128)S(1)}, u32[]{:S(2)}, u32[]{:S(2)}) collective-permute-start(f32[10,1,64]{2,1,0:T(1,128)S(1)} %get-tuple-element.107), channel_id=1, source_target_pairs={{1,0},{2,1},{3,2},{4,3},{5,4},{6,5},{7,6},{9,8},{10,9},{11,10},{12... | collective-permute-start | bytes 7688 | tf_op jit(solution)/shard_map/ppermute | solution.py:18
  577.5 20.2 %collective-permute-start.75 = (f32[10,1,64]{2,1,0:T(1,128)S(1)}, f32[10,1,64]{2,1,0:T(1,128)S(1)}, u32[]{:S(2)}, u32[]{:S(2)}) collective-permute-start(f32[10,1,64]{2,1,0:T(1,128)S(1)} %get-tuple-element.108), channel_id=1, source_target_pairs={{0,1},{1,2},{2,3},{3,4},{4,5},{5,6},{6,7},{8,9},{9,10},{10,11},{11... | collective-permute-start | bytes 7688 | tf_op jit(solution)/shard_map/ppermute | solution.py:17
  579.5 15.9 %collective-permute-start.67 = (f32[17,1,128]{2,1,0:T(1,128)S(1)}, f32[17,1,128]{2,1,0:T(1,128)S(1)}, u32[]{:S(2)}, u32[]{:S(2)}) collective-permute-start(f32[17,1,128]{2,1,0:T(1,128)S(1)} %pad_maximum_fusion.230), channel_id=1, source_target_pairs={{0,1},{1,2},{2,3},{3,4},{4,5},{5,6},{6,7},{8,9},{9,10},{10,11},{11... | collective-permute-start | bytes 26120 | tf_op jit(solution)/shard_map/ppermute | solution.py:26
  664.7 42.5 %collective-permute-start.103 = (f32[1,4,32]{2,1,0:T(4,128)S(1)}, f32[1,4,32]{2,1,0:T(4,128)S(1)}, u32[]{:S(2)}, u32[]{:S(2)}) collective-permute-start(f32[1,4,32]{2,1,0:T(4,128)S(1)} %broadcast.393), channel_id=1, source_target_pairs={{8,0},{16,8},{24,16},{9,1},{17,9},{25,17},{10,2},{18,10},{26,18},{... | collective-permute-start | bytes 1544 | tf_op jit(solution)/shard_map/ppermute | solution.py:18
  666.6 40.6 %collective-permute-start.105 = (f32[1,4,32]{2,1,0:T(4,128)S(1)}, f32[1,4,32]{2,1,0:T(4,128)S(1)}, u32[]{:S(2)}, u32[]{:S(2)}) collective-permute-start(f32[1,4,32]{2,1,0:T(4,128)S(1)} %broadcast.393), channel_id=1, source_target_pairs={{0,8},{8,16},{16,24},{1,9},{9,17},{17,25},{2,10},{10,18},{18,26},{... | collective-permute-start | bytes 1544 | tf_op jit(solution)/shard_map/ppermute | solution.py:17
  699.8 20.5 %collective-permute-start.106 = (f32[6,1,32]{2,1,0:T(1,128)S(1)}, f32[6,1,32]{2,1,0:T(1,128)S(1)}, u32[]{:S(2)}, u32[]{:S(2)}) collective-permute-start(f32[6,1,32]{2,1,0:T(1,128)S(1)} %get-tuple-element.134), channel_id=1, source_target_pairs={{1,0},{2,1},{3,2},{4,3},{5,4},{6,5},{7,6},{9,8},{10,9},{11,10},{12... | collective-permute-start | bytes 2312 | tf_op jit(solution)/shard_map/ppermute | solution.py:18
  703.9 16.4 %collective-permute-start.108 = (f32[6,1,32]{2,1,0:T(1,128)S(1)}, f32[6,1,32]{2,1,0:T(1,128)S(1)}, u32[]{:S(2)}, u32[]{:S(2)}) collective-permute-start(f32[6,1,32]{2,1,0:T(1,128)S(1)} %get-tuple-element.133), channel_id=1, source_target_pairs={{0,1},{1,2},{2,3},{3,4},{4,5},{5,6},{6,7},{8,9},{9,10},{10,11},{11... | collective-permute-start | bytes 2312 | tf_op jit(solution)/shard_map/ppermute | solution.py:17
  (127 other events, 1073.5 us)
where the time goes:
time: 817 us; the launch traced here: 805 us
  starting transfers between devices  299 us (37%)
  local copies, waits for them, and re-layouts  200 us (24%)
  other arithmetic  153 us (19%)
  waiting for transfers between devices  149 us (18%)
    ppermute x62, starting transfers between devices, with_halo(): after = lax.ppermute(leading, axis, down)  179 us
    ppermute x62, waiting for transfers between devices, with_halo(): before = lax.ppermute(last, axis, up)  145 us
    reshape x2, local copies, waits for them, and re-layouts, coarsen(): values.reshape(rows_x // 2, 2, rows_y // 2, 2, rows_z // 2, 2)  137 us
    ppermute x62, starting transfers between devices, with_halo(): before = lax.ppermute(last, axis, up)  110 us
    select_n x24, other arithmetic, heat_bath(): return jnp.where(chosen, updated, current)  78.6 us
    reduce_sum x6, other arithmetic, coarsen(): values.reshape(rows_x // 2, 2, rows_y // 2, 2, rows_z // 2, 2)  50 us
    div x4, local copies, waits for them, and re-layouts, coarsen(): values.reshape(rows_x // 2, 2, rows_y // 2, 2, rows_z // 2, 2)  21.5 us
    slice x18, local copies, waits for them, and re-layouts, along_axis(): lax.slice_in_dim(values, anchor, anchor + span_length - 1, stride=2, axis...  17.2 us
  transfers between devices with their start and end apart: 130, of which 45 were waited for; matrix products, arithmetic and copies ran while one was open for 34% of the time, Pallas kernels for 0%

commit v1 on v0

v1 whole, which is shorter than its diff:
```python
import functools

import jax
import jax.numpy as jnp
import numpy as np
from jax import lax
from jax.experimental import pallas as pl
from jax.experimental.pallas import tpu as pltpu
from jax.sharding import PartitionSpec as P

SWEEPS = 3
LEVELS = 4
LANES = 128
HALO = 8
PRIMES = (65521, 65519)
FACTORS = (40503, 30011)
STEPS = (12347, 7919)


def sine_terms(count):
    nodes = 0.25 * np.cos(np.pi * (np.arange(64) + 0.5) / 64)
    design = np.stack([nodes ** (2 * n + 1) for n in range(count)], axis=1)
    fit = np.linalg.lstsq(design, np.sin(2 * np.pi * nodes), rcond=None)[0]
    return [float(c) for c in fit]


SINE = sine_terms(6)


def hash_base(seed, which):
    gap = 65536 - PRIMES[which]
    v = seed * FACTORS[which]
    v = (v >> 16) * gap + (v & 65535)
    v = (v >> 16) * gap + (v & 65535)
    v = jnp.where(v >= PRIMES[which], v - PRIMES[which], v)
    return v.astype(jnp.float32)


def hash_step(base, which, tag):
    prime = float(PRIMES[which])
    h = base + float(((tag + 1) * STEPS[which]) % PRIMES[which])
    return jnp.where(h >= prime, h - prime, h)


def scaled_noise(base1, base2, tag, minus_two_inverse):
    h1 = hash_step(base1, 0, tag)
    h2 = hash_step(base2, 1, tag)
    u1 = h1 * (1.0 / PRIMES[0]) + 0.5 / PRIMES[0]
    v = jnp.log(u1) * minus_two_inverse
    radius = v * lax.rsqrt(jnp.maximum(v, 1e-30))
    z = jnp.abs(h2 - float(PRIMES[1] // 2)) * (1.0 / PRIMES[1]) - 0.25
    zz = z * z
    poly = jnp.full_like(zz, SINE[-1])
    for term in SINE[-2::-1]:
        poly = poly * zz + term
    return radius * (poly * z)


def dot32(a, b):
    return jnp.dot(a, b, preferred_element_type=jnp.float32, precision=lax.Precision.HIGHEST)


def lane_matrix(rows, kind):
    k = lax.broadcasted_iota(jnp.int32, (rows, LANES), 0)
    half = 2 * lax.broadcasted_iota(jnp.int32, (rows, LANES), 1)
    if kind == "pick":
        return (k == half).astype(jnp.float32)
    if kind == "pair":
        return ((k == half) | (k == half + 1)).astype(jnp.float32)
    near = (k == half - 1) | (k == half + 1)
    return jnp.where(k == half, 0.25, jnp.where(near, 0.125, 0.0))


def table_lookup(classes, table_ref, row, count):
    result = jnp.zeros(classes.shape, jnp.float32)
    for n in range(count):
        result = jnp.where(classes == n, table_ref[row, n], result)
    return result


def statics_kernel(shapes, classes, tab_ref, cls_ref, seed_ref, *refs):
    outs, (t_ref, u_ref) = refs[: 3 * (LEVELS - 1)], refs[3 * (LEVELS - 1) :]
    for level in range(1, LEVELS):
        ni, nj, nk = shapes[level - 1]
        rows = ni // 2 * nj
        width = max(nk, LANES)
        for what in range(3):
            for q in range(ni // 2):
                if level == 1:
                    if what < 2:
                        a = table_lookup(cls_ref[2 * q], tab_ref, what, classes)
                        a = a + table_lookup(cls_ref[2 * q + 1], tab_ref, what, classes)
                    else:
                        a = seed_ref[2 * q].astype(jnp.float32)
                else:
                    prev = outs[3 * (level - 2) + what]
                    a = prev[2 * q]
                    if what < 2:
                        a = a + prev[2 * q + 1]
                t_ref[pl.ds(q * nj, nj), :width] = a
            matrix = lane_matrix(width, "pair" if what < 2 else "pick")
            u_ref[pl.ds(0, rows), :] = dot32(t_ref[pl.ds(0, rows), :width], matrix)
            even = u_ref[pl.ds(0, rows // 2, stride=2), :]
            if what < 2:
                even = 0.125 * (even + u_ref[pl.ds(1, rows // 2, stride=2), :])
            outs[3 * (level - 1) + what][...] = even.reshape(ni // 2, nj // 2, LANES)


def coarse_statics(table, class_map, noise_seed):
    ni, nj, nk = class_map.shape
    shapes = [(ni >> n, nj >> n, nk >> n) for n in range(LEVELS)]
    outs = []
    for level in range(1, LEVELS):
        outs += [jax.ShapeDtypeStruct((*shapes[level][:2], LANES), jnp.float32)] * 3
    vmem = pl.BlockSpec(memory_space=pltpu.VMEM)
    got = pl.pallas_call(
        functools.partial(statics_kernel, shapes, table.shape[1]),
        out_shape=tuple(outs),
        in_specs=[pl.BlockSpec(memory_space=pltpu.SMEM), vmem, vmem],
        out_specs=tuple([vmem] * len(outs)),
        scratch_shapes=[
            pltpu.VMEM((ni // 2 * nj, nk), jnp.float32),
            pltpu.VMEM((ni // 2 * nj, LANES), jnp.float32),
        ],
        name="coarse_statics",
    )(table, class_map, noise_seed)
    return [got[3 * n : 3 * n + 3] for n in range(LEVELS - 1)]


def level_kernel(level, dims, classes, *refs):
    ni, nj, nk, w = dims
    first, last = level == 0, level == LEVELS - 1
    count_i, count_j = ni + 2 * w, nj + 2 * w
    pairs = count_i // 2
    refs = list(refs)
    tab_ref = refs.pop(0) if first else None
    arrays = 4 if not first else 4
    own = [refs.pop(0) for _ in range(arrays)]
    if w:
        x_lo, x_hi, y_lo, y_hi = [refs.pop(0) for _ in range(4)]
    outs = [refs.pop(0) for _ in range(2 if first else 1)]
    d_ref, m_ref, s_ref, r_ref, w_ref, x_ref = refs[:6]
    t_ref, u_ref = refs[6:] if not last else (None, None)

    shape = (count_j, nk)
    lane = lax.broadcasted_iota(jnp.int32, shape, 1)
    row = lax.broadcasted_iota(jnp.int32, shape, 0)
    even = ((lane + row) & 1) == 0
    scale = 0.5 * 0.5**level

    def plane(a, e, where):
        if where == 0:
            mid = x_lo[a * w + e]
        elif where == 1:
            mid = own[a][e - w]
        else:
            mid = x_hi[a * w + e - (w + ni)]
        if not w:
            return mid
        at = a * count_i + e
        mid = mid.astype(jnp.float32)
        return jnp.concatenate([mid, y_hi[at], y_lo[at]], axis=0)

    def half_plane(q, where):
        a, h = 3, w // 2
        if where == 0:
            mid = x_lo[a * w + q]
        elif where == 1:
            both = (own[a][2 * q - w], own[a][2 * q - w + 1])
            own_even = even[:nj]
            mid = jnp.where(own_even, both[1], both[0])
        else:
            mid = x_hi[a * w + q - (h + ni // 2)]
        at = a * count_i + q
        return jnp.concatenate([mid, y_hi[at], y_lo[at]], axis=0)

    zero = jnp.zeros(shape, jnp.float32)
    for c in range(2):
        for g in (0, pairs + 1):
            d_ref[c, g] = zero
            x_ref[c, g] = zero

    def split(q, where):
        def put(ref, slot, values):
            ref[0, q + slot] = jnp.where(even, values[0], values[1])
            ref[1, q + slot] = jnp.where(even, values[1], values[0])

        e = (2 * q, 2 * q + 1)
        if first:
            cls = [plane(0, n, where).astype(jnp.int32) for n in e]
            for c in range(2):
                here = jnp.where(even, cls[c], cls[1 - c])
                d_ref[c, q + 1] = table_lookup(here, tab_ref, 0, classes)
                m_ref[c, q] = table_lookup(here, tab_ref, 1, classes)
            put(s_ref, 0, [plane(1, n, where) for n in e])
            put(r_ref.at[0], 0, [plane(2, n, where) for n in e])
            x_ref[1, q + 1] = half_plane(q, where)
        else:
            put(d_ref, 1, [plane(0, n, where) for n in e])
            put(m_ref, 0, [plane(1, n, where) for n in e])
            put(s_ref, 0, [plane(2, n, where) for n in e])
            put(r_ref.at[0], 0, [plane(3, n, where) for n in e])
            x_ref[1, q + 1] = zero

    def loop(start, stop, body):
        def step(q, carry):
            body(q)
            return carry

        lax.fori_loop(start, stop, step, 0)

    h = w // 2
    if w:
        loop(0, h, lambda q: split(q, 0))
    loop(h, h + ni // 2, lambda q: split(q, 1))
    if w:
        loop(h + ni // 2, pairs, lambda q: split(q, 2))

    def around(ref, c, q):
        other = 1 - c
        mid = ref[other, q + 1]
        above, below = ref[other, q + 2], ref[other, q]
        beside = jnp.where(even, below, above) if c == 0 else jnp.where(even, above, below)
        return [
            mid,
            beside,
            pltpu.roll(mid, count_j - 1, 0),
            pltpu.roll(mid, 1, 0),
            pltpu.roll(mid, nk - 1, 1),
            pltpu.roll(mid, 1, 1),
        ]

    def prepare(q):
        for c in range(2):
            d = d_ref[c, q + 1]
            near = around(d_ref, c, q)
            near[4] = jnp.where(lane == nk - 1, 0.0, near[4])
            near[5] = jnp.where(lane == 0, 0.0, near[5])
            total = 6.0 * d
            for v in near:
                total = total + v
            diagonal = jnp.where(d > 0.0, m_ref[c, q] + scale * total, 0.0)
            inverse = jnp.where(d > 0.0, 1.0 / diagonal, 0.0)
            m_ref[c, q] = diagonal
            part = scale * inverse
            near[4] = jnp.where(lane == nk - 1, -d, near[4])
            near[5] = jnp.where(lane == 0, -d, near[5])
            for n in range(6):
                w_ref[n, c, q] = part * (d + near[n])
            r_ref[1, c, q] = inverse

    loop(0, pairs, prepare)

    step = 16 if count_j % 16 == 0 else 8

    def noises(q):
        for c in range(2):
            for at in range(0, count_j, step):
                rows = pl.ds(at, step)
                seed = s_ref[c, q, rows].astype(jnp.int32)
                base1, base2 = hash_base(seed, 0), hash_base(seed, 1)
                inverse = r_ref[1, c, q, rows]
                minus_two = -2.0 * inverse
                b = r_ref[0, c, q, rows] * inverse
                for t in range(SWEEPS):
                    noise = scaled_noise(base1, base2, level * SWEEPS + t, minus_two)
                    r_ref[t, c, q, rows] = b + noise
                s_ref[c, q, rows] = noise

    loop(0, pairs, noises)

    def gathered(c, q):
        total = None
        for n, v in enumerate(around(x_ref, c, q)):
            term = w_ref[n, c, q] * v
            total = term if total is None else total + term
        return total

    for half in range(2 * SWEEPS):
        t, c = half // 2, half % 2

        def update(q, t=t, c=c):
            x_ref[c, q + 1] = r_ref[t, c, q] + gathered(c, q)

        if w:
            loop(half // 2, (ni + w + 2 * SWEEPS - half) // 2 + 1, update)
        else:
            loop(0, pairs, update)

    if last:
        own_even = even[:nj]

        def write(q):
            red, black = x_ref[0, q + 1], x_ref[1, q + 1]
            outs[0][2 * q] = jnp.where(even, red, black)
            outs[0][2 * q + 1] = jnp.where(even, black, red)

        loop(0, pairs, write)
        return

    if first:

        def write(q):
            red, black = x_ref[0, q + h + 1, :nj], x_ref[1, q + h + 1, :nj]
            outs[0][2 * q] = jnp.where(even[:nj], red, black)
            outs[0][2 * q + 1] = jnp.where(even[:nj], black, red)

        loop(0, ni // 2, write)

    def residual(q):
        red = r_ref[SWEEPS - 1, 0, q] - s_ref[0, q] + gathered(0, q) - x_ref[0, q + 1]
        r_ref[0, 0, q] = m_ref[0, q] * red
        r_ref[0, 1, q] = -m_ref[1, q] * s_ref[1, q]

    loop(h - 1, h + ni // 2, residual)

    def restrict(q):
        p = q + h
        red, black = r_ref[0, 0, p], r_ref[0, 1, p]
        red_before, black_before = r_ref[0, 0, p - 1], r_ref[0, 1, p - 1]
        at = jnp.where(even, red, black)
        sides = jnp.where(even, black, red) + jnp.where(even, black_before, red_before)
        v = at + 0.5 * sides
        v = v + 0.5 * (pltpu.roll(v, count_j - 1, 0) + pltpu.roll(v, 1, 0))
        t_ref[pl.ds(pl.multiple_of(q * count_j, 8), count_j), :] = v

    loop(0, ni // 2, restrict)
    u_ref[...] = dot32(t_ref[...], lane_matrix(nk, "restrict"))
    size = ni // 2 * count_j // 2
    coarse = u_ref[pl.ds(0, size, stride=2), :].reshape(ni // 2, count_j // 2, LANES)
    outs[-1][...] = coarse[:, : nj // 2, :]


def run_level(level, own, halos, table=None):
    ni, nj, nk = own[0].shape
    w = HALO if halos else 0
    first, last = level == 0, level == LEVELS - 1
    count_i, count_j = ni + 2 * w, nj + 2 * w
    pairs = count_i // 2
    outs = []
    if first or last:
        outs.append(jax.ShapeDtypeStruct((ni, nj, nk), jnp.float32))
    if not last:
        outs.append(jax.ShapeDtypeStruct((ni // 2, nj // 2, LANES), jnp.float32))
    scratch = [
        pltpu.VMEM((2, pairs + 2, count_j, nk), jnp.float32),
        pltpu.VMEM((2, pairs, count_j, nk), jnp.float32),
        pltpu.VMEM((2, pairs, count_j, nk), jnp.float32),
        pltpu.VMEM((SWEEPS, 2, pairs, count_j, nk), jnp.float32),
        pltpu.VMEM((6, 2, pairs, count_j, nk), jnp.float32),
        pltpu.VMEM((2, pairs + 2, count_j, nk), jnp.float32),
    ]
    if not last:
        scratch += [
            pltpu.VMEM((ni // 2 * count_j, nk), jnp.float32),
            pltpu.VMEM((ni // 2 * count_j, LANES), jnp.float32),
        ]
    vmem = pl.BlockSpec(memory_space=pltpu.VMEM)
    args = list(own) + list(halos)
    specs = [vmem] * len(args)
    if first:
        args = [table] + args
        specs = [pl.BlockSpec(memory_space=pltpu.SMEM)] + specs
    classes = table.shape[1] if first else 0
    got = pl.pallas_call(
        functools.partial(level_kernel, level, (ni, nj, nk, w), classes),
        out_shape=tuple(outs),
        in_specs=specs,
        out_specs=tuple([vmem] * len(outs)),
        scratch_shapes=scratch,
        compiler_params=pltpu.CompilerParams(vmem_limit_bytes=60 * 1024 * 1024),
        name=f"level_{level}",
    )(*args)
    return got


def both_ways(to_next, to_previous, axis):
    size = lax.axis_size(axis)
    up = [(i, i + 1) for i in range(size - 1)]
    down = [(j, i) for i, j in up]
    return lax.ppermute(to_next, axis, up), lax.ppermute(to_previous, axis, down)


def halo_exchange(arrays, black=None):
    w = HALO
    ni, nj, nk = arrays[0].shape
    low = [a[:w] for a in arrays]
    high = [a[ni - w :] for a in arrays]
    if black is not None:
        low.append(black[: w // 2])
        high.append(black[ni // 2 - w // 2 :])
    from_low, from_high = both_ways(jnp.concatenate(high), jnp.concatenate(low), "gx")
    low_rows, high_rows = [], []
    sizes = [w] * len(arrays)
    mids = list(arrays)
    if black is not None:
        sizes.append(w // 2)
        mids.append(black)
    at = 0
    for mid, size in zip(mids, sizes):
        part = slice(at, at + size)
        at += size
        for rows, where in ((slice(0, w), low_rows), (slice(nj - w, nj), high_rows)):
            where += [from_low[part, rows], mid[:, rows], from_high[part, rows]]
    left, right = both_ways(jnp.concatenate(high_rows), jnp.concatenate(low_rows), "gy")
    return (from_low, from_high, left, right)


def per_device(sample_field, mean_shift, class_map, noise_seed, diffusion_table, mass_table):
    zero = jnp.zeros((1,), jnp.float32)
    table = jnp.stack(
        [
            jnp.concatenate([zero, diffusion_table]),
            jnp.concatenate([zero, mass_table]),
        ]
    )
    ni, nj, nk = class_map.shape
    statics = coarse_statics(table[:, 1:], class_map, noise_seed)
    index = lax.broadcasted_iota(jnp.int32, (ni // 2, nj, nk), 1)
    index = index + lax.broadcasted_iota(jnp.int32, (ni // 2, nj, nk), 2)
    planes = sample_field.reshape(ni // 2, 2, nj, nk)
    black = jnp.where((index & 1) == 0, planes[:, 1], planes[:, 0])
    cls = (class_map + 1).astype(jnp.float32)
    seed = noise_seed.astype(jnp.float32)
    arrays = [cls, seed, mean_shift]
    halos = halo_exchange(arrays, black)
    fine, rhs = run_level(0, arrays + [sample_field], halos, table)
    for level in range(1, LEVELS - 1):
        arrays = list(statics[level - 1]) + [rhs]
        (rhs,) = run_level(level, arrays, halo_exchange(arrays))
    lanes = nk >> (LEVELS - 1)
    arrays = list(statics[-1]) + [rhs]
    packed = jnp.concatenate([a[:, :, :lanes] for a in arrays], axis=2)
    gx, gy = lax.axis_size("gx"), lax.axis_size("gy")
    mi, mj, mk = packed.shape
    spread = jnp.broadcast_to(packed[None], (gx * gy, mi, mj, mk))
    all_blocks = lax.all_to_all(spread, ("gx", "gy"), 0, 0, tiled=True)
    grid = all_blocks.reshape(gx, gy, mi, mj, mk).transpose(0, 2, 1, 3, 4)
    grid = grid.reshape(gx * mi, gy * mj, mk)
    pad = ((0, 0), (0, 8), (0, LANES - lanes))
    whole = [jnp.pad(grid[:, :, n * lanes : (n + 1) * lanes], pad) for n in range(4)]
    (coarse,) = run_level(LEVELS - 1, whole, ())
    start = (lax.axis_index("gx") * mi, lax.axis_index("gy") * mj, 0)
    return fine, lax.dynamic_slice(coarse, start, (mi, mj, lanes))


def solution(mesh):
    spec = P("gx", "gy", None)
    return jax.shard_map(
        per_device,
        mesh=mesh,
        in_specs=(spec, spec, spec, spec, P(), P()),
        out_specs=(spec, spec),
        check_vma=False,
    )
```

time: 817 us -> 221 us (0.27)
  the two profiles are of different devices: /device:TPU:28 before, /device:TPU:0 now
where the time goes in v1:
time: 221 us; the launch traced here: 220 us
  Pallas kernels  76.3 us (35%)
  starting transfers between devices  60.3 us (27%)
  waiting for transfers between devices  52.7 us (24%)
  local copies, waits for them, and re-layouts  25.6 us (12%)
  other arithmetic  3.41 us (2%)
    pallas_call x4, Pallas kernels, run_level(): pl.pallas_call(functools.partial(level_kernel, level, (ni, nj, nk, w), cl...  70.6 us
    ppermute x6, starting transfers between devices, both_ways(): lax.ppermute(to_next, axis, up)  45.6 us
    ppermute x6, waiting for transfers between devices, both_ways(): lax.ppermute(to_next, axis, up)  22.1 us
    ppermute x6, waiting for transfers between devices, both_ways(): lax.ppermute(to_previous, axis, down)  20 us
    unnamed x93, local copies, waits for them, and re-layouts  14.9 us
    all_to_all x1, waiting for transfers between devices, per_device(): all_blocks = lax.all_to_all(spread, ('gx', 'gy'), 0, 0, tiled=True)  10.6 us
    ppermute x6, starting transfers between devices, both_ways(): lax.ppermute(to_previous, axis, down)  7.75 us
    all_to_all x1, starting transfers between devices, per_device(): all_blocks = lax.all_to_all(spread, ('gx', 'gy'), 0, 0, tiled=True)  6.95 us
  transfers between devices with their start and end apart: 13, of which 10 were waited for; matrix products, arithmetic and copies ran while one was open for 2% of the time, Pallas kernels for 3%

profile of v1, /device:TPU:0, one launch (start us, length us, event | category | flops | bytes accessed | tf_op | source)
XLA Modules:
  0.0 219.5 jit_solution(1813124920016913680)
XLA Ops:
  0.6 1.4 add_convert_fusion.refs_1_
  2.3 1.9 copy-done.3
  4.7 5.0 %collective-permute-start = (f32[28,32,256]{2,1,0:T(8,128)S(1)}, f32[28,32,256]{2,1,0:T(8,128)S(1)}, u32[]{:S(2)}, u32[]{:S(2)}) collective-permute-start(f32[28,32,256]{2,1,0:T(8,128)S(1)} %pad_maximum_fusion), channel_id=1, source_target_pairs={{0,8},{8,16},{16,24},{1,9},{9,17},{17,25},{2,10},{10,18},{18,26},{... | collective-permute-start | bytes 2752520 | tf_op jit(solution)/shard_map/ppermute | solution.py:381
  11.1 18.1 %collective-permute-done.refs_5_ = f32[28,32,256]{2,1,0:T(8,128)S(1)} collective-permute-done((f32[28,32,256]{2,1,0:T(8,128)S(1)}, f32[28,32,256]{2,1,0:T(8,128)S(1)}, u32[]{:S(2)}, u32[]{:S(2)}) %collective-permute-start) | collective-permute-done | bytes 917536 | tf_op jit(solution)/shard_map/ppermute | solution.py:381
  30.9 2.7 %collective-permute-done.1.refs_6_ = f32[28,32,256]{2,1,0:T(8,128)S(1)} collective-permute-done((f32[28,32,256]{2,1,0:T(8,128)S(1)}, f32[28,32,256]{2,1,0:T(8,128)S(1)}, u32[]{:S(2)}, u32[]{:S(2)}) %collective-permute-start.1) | collective-permute-done | bytes 917536 | tf_op jit(solution)/shard_map/ppermute | solution.py:381
  40.6 1.4 collective-permute-start.2
  44.1 5.7 %coarse_statics.1 = (f32[16,16,128]{2,1,0:T(8,128)}, f32[16,16,128]{2,1,0:T(8,128)}, f32[16,16,128]{2,1,0:T(8,128)}, f32[8,8,128]{2,1,0:T(8,128)}, f32[8,8,128]{...) custom-call(f32[2,8]{1,0:T(2,128)} %slice.291.tab_ref, ...), custom_call_target="tpu_custom_call" | custom-call | tf_op jit(solution)/shard_map/coarse_statics/pallas_call | solution.py:116
  54.6 38.2 %level_0.1 = (f32[32,32,256]{2,1,0:T(8,128)}, f32[16,16,128]{2,1,0:T(8,128)}) custom-call(f32[2,9]{1,0:T(2,128)} %copy-done.24, f32[32,32,256]{2,1,0:T(8,128)} %copy-done, f32[32,32,256]{2,1,0:T(8,128)} %copy-done.1, f32[32,32,256]{2,1,0:T(8,128)} %refs_3_.1, f32[32,32,256]{2,1,0:T(8,128)} %refs_4_.1, f32[28,32,256]{2,1,0:T(8,128)} %copy-done.5, ...), custom_call_target="tpu_custom_call" | custom-call | tf_op jit(solution)/shard_map/level_0/pallas_call | solution.py:365
  93.8 3.6 %collective-permute-start.4 = (f32[32,16,128]{2,1,0:T(8,128)S(1)}, f32[32,16,128]{2,1,0:T(8,128)S(1)}, u32[]{:S(2)}, u32[]{:S(2)}) collective-permute-start(f32[32,16,128]{2,1,0:T(8,128)S(1)} %pad_maximum_fusion.2), channel_id=1, source_target_pairs={{0,8},{8,16},{16,24},{1,9},{9,17},{17,25},{2,10},{10,18},{18,26},{... | collective-permute-start | bytes 786440 | tf_op jit(solution)/shard_map/ppermute | solution.py:381
  98.7 2.5 %collective-permute-done.4.refs_4_ = f32[32,16,128]{2,1,0:T(8,128)S(1)} collective-permute-done((f32[32,16,128]{2,1,0:T(8,128)S(1)}, f32[32,16,128]{2,1,0:T(8,128)S(1)}, u32[]{:S(2)}, u32[]{:S(2)}) %collective-permute-start.4) | collective-permute-done | bytes 262176 | tf_op jit(solution)/shard_map/ppermute | solution.py:381
  101.2 4.4 %collective-permute-done.5.refs_5_ = f32[32,16,128]{2,1,0:T(8,128)S(1)} collective-permute-done((f32[32,16,128]{2,1,0:T(8,128)S(1)}, f32[32,16,128]{2,1,0:T(8,128)S(1)}, u32[]{:S(2)}, u32[]{:S(2)}) %collective-permute-start.5) | collective-permute-done | bytes 262176 | tf_op jit(solution)/shard_map/ppermute | solution.py:381
  105.9 23.0 %collective-permute-start.6 = (f32[128,8,128]{2,1,0:T(8,128)S(1)}, f32[128,8,128]{2,1,0:T(8,128)S(1)}, u32[]{:S(2)}, u32[]{:S(2)}) collective-permute-start(f32[128,8,128]{2,1,0:T(8,128)S(1)} %get-tuple-element.61), channel_id=1, source_target_pairs={{0,1},{1,2},{2,3},{3,4},{4,5},{5,6},{6,7},{8,9},{9,10},{10,11},{11... | collective-permute-start | bytes 1572872 | tf_op jit(solution)/shard_map/ppermute | solution.py:381
  130.4 5.5 %collective-permute-done.7.refs_7_ = f32[128,8,128]{2,1,0:T(8,128)S(1)} collective-permute-done((f32[128,8,128]{2,1,0:T(8,128)S(1)}, f32[128,8,128]{2,1,0:T(8,128)S(1)}, u32[]{:S(2)}, u32[]{:S(2)}) %collective-permute-start.7) | collective-permute-done | bytes 524320 | tf_op jit(solution)/shard_map/ppermute | solution.py:381
  136.7 14.1 %level_1.1.refs_3_ = f32[8,8,128]{2,1,0:T(8,128)} custom-call(f32[16,16,128]{2,1,0:T(8,128)} %get-tuple-element.20.refs_0_, f32[16,16,128]{2,1,0:T(8,128)} %get-tuple-element.21.refs_1_, f32[16,16,128]{2,1,0:T(8,128)} %get-tuple-element.22.refs_2_, f32[16,16,128]{2,1,0:T(8,128)} %get-tuple-element.23.refs_3_, f32[32,16,128]{2,1,0:T(8,128)} %copy-done.13, ...), custom_call_target="tpu_custom_call" | custom-call | tf_op jit(solution)/shard_map/level_1/pallas_call | solution.py:365
  151.7 3.5 %collective-permute-start.8 = (f32[32,8,128]{2,1,0:T(8,128)S(1)}, f32[32,8,128]{2,1,0:T(8,128)S(1)}, u32[]{:S(2)}, u32[]{:S(2)}) collective-permute-start(f32[32,8,128]{2,1,0:T(8,128)S(1)} %pad_maximum_fusion.4), channel_id=1, source_target_pairs={{0,8},{8,16},{16,24},{1,9},{9,17},{17,25},{2,10},{10,18},{18,26},{... | collective-permute-start | bytes 393224 | tf_op jit(solution)/shard_map/ppermute | solution.py:381
  155.2 1.3 collective-permute-start.9
  157.7 4.4 %collective-permute-done.9.refs_5_ = f32[32,8,128]{2,1,0:T(8,128)S(1)} collective-permute-done((f32[32,8,128]{2,1,0:T(8,128)S(1)}, f32[32,8,128]{2,1,0:T(8,128)S(1)}, u32[]{:S(2)}, u32[]{:S(2)}) %collective-permute-start.9) | collective-permute-done | bytes 131104 | tf_op jit(solution)/shard_map/ppermute | solution.py:381
  162.9 9.2 %collective-permute-start.10 = (f32[96,8,128]{2,1,0:T(8,128)S(1)}, f32[96,8,128]{2,1,0:T(8,128)S(1)}, u32[]{:S(2)}, u32[]{:S(2)}) collective-permute-start(f32[96,8,128]{2,1,0:T(8,128)S(1)} %constant_dynamic-update-slice_fusion.40), channel_id=1, source_target_pairs={{0,1},{1,2},{2,3},{3,4},{4,5},{5,6},{6,7},{8,9},{9,10},{10,11},{11... | collective-permute-start | bytes 1179656 | tf_op jit(solution)/shard_map/ppermute | solution.py:381
  173.4 3.1 %collective-permute-done.11.refs_7_ = f32[96,8,128]{2,1,0:T(8,128)S(1)} collective-permute-done((f32[96,8,128]{2,1,0:T(8,128)S(1)}, f32[96,8,128]{2,1,0:T(8,128)S(1)}, u32[]{:S(2)}, u32[]{:S(2)}) %collective-permute-start.11) | collective-permute-done | bytes 393248 | tf_op jit(solution)/shard_map/ppermute | solution.py:381
  177.2 9.7 %level_2.1 = f32[4,4,128]{2,1,0:T(4,128)} custom-call(f32[8,8,128]{2,1,0:T(8,128)} %get-tuple-element.17.refs_0_, f32[8,8,128]{2,1,0:T(8,128)} %get-tuple-element.18.refs_1_, f32[8,8,128]{2,1,0:T(8,128)} %get-tuple-element.19.refs_2_, f32[8,8,128]{2,1,0:T(8,128)} %level_1.1.refs_3_, f32[32,8,128]{2,1,0:T(8,128)} %copy-done.15, f32[32,8,128]{2,1,0:T(8,128)} %copy-done.16, ...), custom_call_target="tpu_custom_call" | custom-call | tf_op jit(solution)/shard_map/level_2/pallas_call | solution.py:365
  188.5 6.9 %all-to-all-start = ((f32[32,4,4,128]{3,2,1,0:T(4,128)}), f32[32,4,4,128]{3,2,1,0:T(4,128)S(1)}, u32[]{:S(2)}, u32[]{:S(2)}) async-start(f32[32,4,4,128]{3,2,1,0:T(4,128)} %broadcast_in_dim.2), calls=%async_computation | async-start | bytes 524288 | tf_op jit(solution)/shard_map/all_to_all | solution.py:437
  195.5 10.6 %all-to-all-done = f32[32,4,4,128]{3,2,1,0:T(4,128)S(1)} async-done(((f32[32,4,4,128]{3,2,1,0:T(4,128)}), f32[32,4,4,128]{3,2,1,0:T(4,128)S(1)}, u32[]{:S(2)}, u32[]{:S(2)}) %all-to-all-start) | async-done | bytes 262176 | tf_op jit(solution)/shard_map/all_to_all | solution.py:437
  209.6 8.6 %level_3.1 = f32[16,40,128]{2,1,0:T(8,128)} custom-call(f32[16,40,128]{2,1,0:T(8,128)} %pad.13.refs_0_, f32[16,40,128]{2,1,0:T(8,128)} %pad.14.refs_1_, f32[16,40,128]{2,1,0:T(8,128)} %pad.15.refs_2_, f32[16,40,128]{2,1,0:T(8,128)} %pad.16.refs_3_), custom_call_target="tpu_custom_call" | custom-call | tf_op jit(solution)/shard_map/level_3/pallas_call | solution.py:365
  218.2 1.3 constant_dynamic-slice_fusion
  (131 shorter events, 32.2 us)
Async XLA Ops:
  2.2 27.8 %copy-start = (f32[32,32,256]{2,1,0:T(8,128)}, f32[32,32,256]{2,1,0:T(8,128)S(1)}, u32[]{:S(2)}) copy-start(f32[32,32,256]{2,1,0:T(8,128)S(1)} %add_convert_fusion.refs_1_) | copy-start | bytes 3145732
  2.3 32.6 %copy-start.1 = (f32[32,32,256]{2,1,0:T(8,128)}, f32[32,32,256]{2,1,0:T(8,128)S(1)}, u32[]{:S(2)}) copy-start(f32[32,32,256]{2,1,0:T(8,128)S(1)} %convert_element_type.12.refs_2_) | copy-start | bytes 3145732
  4.7 24.6 %collective-permute-start = (f32[28,32,256]{2,1,0:T(8,128)S(1)}, f32[28,32,256]{2,1,0:T(8,128)S(1)}, u32[]{:S(2)}, u32[]{:S(2)}) collective-permute-start(f32[28,32,256]{2,1,0:T(8,128)S(1)} %pad_maximum_fusion), channel_id=1, source_target_pairs={{0,8},{8,16},{16,24},{1,9},{9,17},{17,25},{2,10},{10,18},{18,26},{... | collective-permute-start | bytes 2752520 | tf_op jit(solution)/shard_map/ppermute | solution.py:381
  9.8 23.7 %collective-permute-start.1 = (f32[28,32,256]{2,1,0:T(8,128)S(1)}, f32[28,32,256]{2,1,0:T(8,128)S(1)}, u32[]{:S(2)}, u32[]{:S(2)}) collective-permute-start(f32[28,32,256]{2,1,0:T(8,128)S(1)} %pad_maximum_fusion.1), channel_id=1, source_target_pairs={{8,0},{16,8},{24,16},{9,1},{17,9},{25,17},{10,2},{18,10},{26,18},{... | collective-permute-start | bytes 2752520 | tf_op jit(solution)/shard_map/ppermute | solution.py:381
  40.6 11.7 %collective-permute-start.2 = (f32[168,8,256]{2,1,0:T(8,128)}, f32[168,8,256]{2,1,0:T(8,128)S(1)}, u32[]{:S(2)}, u32[]{:S(2)}) collective-permute-start(f32[168,8,256]{2,1,0:T(8,128)} %get-tuple-element.37), channel_id=1, source_target_pairs={{0,1},{1,2},{2,3},{3,4},{4,5},{5,6},{6,7},{8,9},{9,10},{10,11},{11... | collective-permute-start | bytes 4128776 | tf_op jit(solution)/shard_map/ppermute | solution.py:381
  42.0 10.4 %collective-permute-start.3 = (f32[168,8,256]{2,1,0:T(8,128)}, f32[168,8,256]{2,1,0:T(8,128)S(1)}, u32[]{:S(2)}, u32[]{:S(2)}) collective-permute-start(f32[168,8,256]{2,1,0:T(8,128)} %get-tuple-element.36), channel_id=1, source_target_pairs={{1,0},{2,1},{3,2},{4,3},{5,4},{6,5},{7,6},{9,8},{10,9},{11,10},{12... | collective-permute-start | bytes 4128776 | tf_op jit(solution)/shard_map/ppermute | solution.py:381
  93.8 7.4 %collective-permute-start.4 = (f32[32,16,128]{2,1,0:T(8,128)S(1)}, f32[32,16,128]{2,1,0:T(8,128)S(1)}, u32[]{:S(2)}, u32[]{:S(2)}) collective-permute-start(f32[32,16,128]{2,1,0:T(8,128)S(1)} %pad_maximum_fusion.2), channel_id=1, source_target_pairs={{0,8},{8,16},{16,24},{1,9},{9,17},{17,25},{2,10},{10,18},{18,26},{... | collective-permute-start | bytes 786440 | tf_op jit(solution)/shard_map/ppermute | solution.py:381
  97.4 8.3 %collective-permute-start.5 = (f32[32,16,128]{2,1,0:T(8,128)S(1)}, f32[32,16,128]{2,1,0:T(8,128)S(1)}, u32[]{:S(2)}, u32[]{:S(2)}) collective-permute-start(f32[32,16,128]{2,1,0:T(8,128)S(1)} %pad_maximum_fusion.3), channel_id=1, source_target_pairs={{8,0},{16,8},{24,16},{9,1},{17,9},{25,17},{10,2},{18,10},{26,18},{... | collective-permute-start | bytes 786440 | tf_op jit(solution)/shard_map/ppermute | solution.py:381
  101.2 34.7 %copy-start.13 = (f32[32,16,128]{2,1,0:T(8,128)}, f32[32,16,128]{2,1,0:T(8,128)S(1)}, u32[]{:S(2)}) copy-start(f32[32,16,128]{2,1,0:T(8,128)S(1)} %collective-permute-done.4.refs_4_) | copy-start | bytes 786436
  105.6 30.3 %copy-start.14 = (f32[32,16,128]{2,1,0:T(8,128)}, f32[32,16,128]{2,1,0:T(8,128)S(1)}, u32[]{:S(2)}) copy-start(f32[32,16,128]{2,1,0:T(8,128)S(1)} %collective-permute-done.5.refs_5_) | copy-start | bytes 786436
  105.8 45.1 %copy-start.21 = (f32[8,8,128]{2,1,0:T(8,128)S(1)}, f32[8,8,128]{2,1,0:T(8,128)}, u32[]{:S(2)}) copy-start(f32[8,8,128]{2,1,0:T(8,128)} %get-tuple-element.17.refs_0_) | copy-start | bytes 98308
  105.8 45.1 %copy-start.22 = (f32[8,8,128]{2,1,0:T(8,128)S(1)}, f32[8,8,128]{2,1,0:T(8,128)}, u32[]{:S(2)}) copy-start(f32[8,8,128]{2,1,0:T(8,128)} %get-tuple-element.18.refs_1_) | copy-start | bytes 98308
  105.8 45.1 %copy-start.23 = (f32[8,8,128]{2,1,0:T(8,128)S(1)}, f32[8,8,128]{2,1,0:T(8,128)}, u32[]{:S(2)}) copy-start(f32[8,8,128]{2,1,0:T(8,128)} %get-tuple-element.19.refs_2_) | copy-start | bytes 98308
  105.9 24.5 %collective-permute-start.6 = (f32[128,8,128]{2,1,0:T(8,128)S(1)}, f32[128,8,128]{2,1,0:T(8,128)S(1)}, u32[]{:S(2)}, u32[]{:S(2)}) collective-permute-start(f32[128,8,128]{2,1,0:T(8,128)S(1)} %get-tuple-element.61), channel_id=1, source_target_pairs={{0,1},{1,2},{2,3},{3,4},{4,5},{5,6},{6,7},{8,9},{9,10},{10,11},{11... | collective-permute-start | bytes 1572872 | tf_op jit(solution)/shard_map/ppermute | solution.py:381
  128.9 7.0 %collective-permute-start.7 = (f32[128,8,128]{2,1,0:T(8,128)S(1)}, f32[128,8,128]{2,1,0:T(8,128)S(1)}, u32[]{:S(2)}, u32[]{:S(2)}) collective-permute-start(f32[128,8,128]{2,1,0:T(8,128)S(1)} %get-tuple-element.60), channel_id=1, source_target_pairs={{1,0},{2,1},{3,2},{4,3},{5,4},{6,5},{7,6},{9,8},{10,9},{11,10},{12... | collective-permute-start | bytes 1572872 | tf_op jit(solution)/shard_map/ppermute | solution.py:381
  150.9 36.1 %copy-start.25 = (f32[4,4,128]{2,1,0:T(4,128)S(1)}, f32[4,4,128]{2,1,0:T(4,128)}, u32[]{:S(2)}) copy-start(f32[4,4,128]{2,1,0:T(4,128)} %get-tuple-element.14) | copy-start | bytes 24580
  150.9 36.1 %copy-start.26 = (f32[4,4,128]{2,1,0:T(4,128)S(1)}, f32[4,4,128]{2,1,0:T(4,128)}, u32[]{:S(2)}) copy-start(f32[4,4,128]{2,1,0:T(4,128)} %get-tuple-element.15) | copy-start | bytes 24580
  150.9 36.1 %copy-start.27 = (f32[4,4,128]{2,1,0:T(4,128)S(1)}, f32[4,4,128]{2,1,0:T(4,128)}, u32[]{:S(2)}) copy-start(f32[4,4,128]{2,1,0:T(4,128)} %get-tuple-element.16) | copy-start | bytes 24580
  151.7 6.0 %collective-permute-start.8 = (f32[32,8,128]{2,1,0:T(8,128)S(1)}, f32[32,8,128]{2,1,0:T(8,128)S(1)}, u32[]{:S(2)}, u32[]{:S(2)}) collective-permute-start(f32[32,8,128]{2,1,0:T(8,128)S(1)} %pad_maximum_fusion.4), channel_id=1, source_target_pairs={{0,8},{8,16},{16,24},{1,9},{9,17},{17,25},{2,10},{10,18},{18,26},{... | collective-permute-start | bytes 393224 | tf_op jit(solution)/shard_map/ppermute | solution.py:381
  155.2 6.9 %collective-permute-start.9 = (f32[32,8,128]{2,1,0:T(8,128)S(1)}, f32[32,8,128]{2,1,0:T(8,128)S(1)}, u32[]{:S(2)}, u32[]{:S(2)}) collective-permute-start(f32[32,8,128]{2,1,0:T(8,128)S(1)} %pad_maximum_fusion.4), channel_id=1, source_target_pairs={{8,0},{16,8},{24,16},{9,1},{17,9},{25,17},{10,2},{18,10},{26,18},{... | collective-permute-start | bytes 393224 | tf_op jit(solution)/shard_map/ppermute | solution.py:381
  157.7 18.8 %copy-start.15 = (f32[32,8,128]{2,1,0:T(8,128)}, f32[32,8,128]{2,1,0:T(8,128)S(1)}, u32[]{:S(2)}) copy-start(f32[32,8,128]{2,1,0:T(8,128)S(1)} %collective-permute-done.8.refs_4_) | copy-start | bytes 393220
  162.9 10.5 %collective-permute-start.10 = (f32[96,8,128]{2,1,0:T(8,128)S(1)}, f32[96,8,128]{2,1,0:T(8,128)S(1)}, u32[]{:S(2)}, u32[]{:S(2)}) collective-permute-start(f32[96,8,128]{2,1,0:T(8,128)S(1)} %constant_dynamic-update-slice_fusion.40), channel_id=1, source_target_pairs={{0,1},{1,2},{2,3},{3,4},{4,5},{5,6},{6,7},{8,9},{9,10},{10,11},{11... | collective-permute-start | bytes 1179656 | tf_op jit(solution)/shard_map/ppermute | solution.py:381
  172.1 4.4 %collective-permute-start.11 = (f32[96,8,128]{2,1,0:T(8,128)S(1)}, f32[96,8,128]{2,1,0:T(8,128)S(1)}, u32[]{:S(2)}, u32[]{:S(2)}) collective-permute-start(f32[96,8,128]{2,1,0:T(8,128)S(1)} %constant_dynamic-update-slice_fusion.40), channel_id=1, source_target_pairs={{1,0},{2,1},{3,2},{4,3},{5,4},{6,5},{7,6},{9,8},{10,9},{11,10},{12... | collective-permute-start | bytes 1179656 | tf_op jit(solution)/shard_map/ppermute | solution.py:381
  188.5 17.5 %all-to-all-start = ((f32[32,4,4,128]{3,2,1,0:T(4,128)}), f32[32,4,4,128]{3,2,1,0:T(4,128)S(1)}, u32[]{:S(2)}, u32[]{:S(2)}) async-start(f32[32,4,4,128]{3,2,1,0:T(4,128)} %broadcast_in_dim.2), calls=%async_computation | async-start | bytes 524288 | tf_op jit(solution)/shard_map/all_to_all | solution.py:437
  (19 other events, 118.8 us)

commit v2 on v0

v2 whole, which is shorter than its diff:
```python
import functools

import jax
import jax.numpy as jnp
import numpy as np
from jax import lax
from jax.experimental import pallas as pl
from jax.experimental.pallas import tpu as pltpu
from jax.sharding import PartitionSpec as P

SWEEPS = 3
LEVELS = 4
LANES = 128
FINE_HALO = 4
FINE_LIMIT = 40
HALO = 8
PRIMES = (65521, 65519)
FACTORS = (40503, 30011)
STEPS = (12347, 7919)


def sine_terms(count):
    nodes = 0.25 * np.cos(np.pi * (np.arange(64) + 0.5) / 64)
    design = np.stack([nodes ** (2 * n + 1) for n in range(count)], axis=1)
    fit = np.linalg.lstsq(design, np.sin(2 * np.pi * nodes), rcond=None)[0]
    return [float(c) for c in fit]


SINE = sine_terms(6)


def hash_base(seed, which):
    gap = 65536 - PRIMES[which]
    v = seed * FACTORS[which]
    v = (v >> 16) * gap + (v & 65535)
    v = (v >> 16) * gap + (v & 65535)
    v = jnp.where(v >= PRIMES[which], v - PRIMES[which], v)
    return v.astype(jnp.float32)


def hash_step(base, which, tag):
    prime = float(PRIMES[which])
    h = base + float(((tag + 1) * STEPS[which]) % PRIMES[which])
    return jnp.where(h >= prime, h - prime, h)


def raw_noise(base1, base2, tag):
    h1 = hash_step(base1, 0, tag)
    h2 = hash_step(base2, 1, tag)
    u1 = h1 * (1.0 / PRIMES[0]) + 0.5 / PRIMES[0]
    v = -2.0 * jnp.log(u1)
    radius = v * lax.rsqrt(v)
    z = jnp.abs(h2 - float(PRIMES[1] // 2)) * (1.0 / PRIMES[1]) - 0.25
    zz = z * z
    poly = jnp.full_like(zz, SINE[-1])
    for term in SINE[-2::-1]:
        poly = poly * zz + term
    return radius * (poly * z)


def raw_noises(seed, level):
    base1, base2 = hash_base(seed, 0), hash_base(seed, 1)
    return [raw_noise(base1, base2, level * SWEEPS + t) for t in range(SWEEPS)]


def dot32(a, b):
    return jnp.dot(a, b, preferred_element_type=jnp.float32, precision=lax.Precision.HIGHEST)


def lane_matrix(rows, kind):
    k = lax.broadcasted_iota(jnp.int32, (rows, LANES), 0)
    half = 2 * lax.broadcasted_iota(jnp.int32, (rows, LANES), 1)
    if kind == "pick":
        return (k == half).astype(jnp.float32)
    if kind == "pair":
        return ((k == half) | (k == half + 1)).astype(jnp.float32)
    near = (k == half - 1) | (k == half + 1)
    return jnp.where(k == half, 0.25, jnp.where(near, 0.125, 0.0))


def lookups(numbers, tables):
    results = [jnp.zeros(numbers.shape, jnp.float32) for _ in tables]
    for n in range(tables[0].shape[0]):
        hit = numbers == n + 1
        results = [jnp.where(hit, table[n], result) for table, result in zip(tables, results)]
    return results


def loop(start, stop, body, unroll=1):
    if stop - start <= unroll:
        for q in range(start, stop):
            body(q)
        return

    def step(n, carry):
        for u in range(unroll):
            body(start + n * unroll + u)
        return carry

    whole = (stop - start) // unroll
    lax.fori_loop(0, whole, step, 0)
    for q in range(start + whole * unroll, stop):
        body(q)


def checker(shape):
    return ((lax.broadcasted_iota(jnp.int32, shape, 0) + lax.broadcasted_iota(jnp.int32, shape, 1)) & 1) == 0


def has_neighbours(axis):
    at = lax.axis_index(axis)
    last = lax.axis_size(axis) - 1
    return (at > 0).astype(jnp.float32), (at < last).astype(jnp.float32)


VMEM = pl.BlockSpec(memory_space=pltpu.VMEM)
SMEM = pl.BlockSpec(memory_space=pltpu.SMEM)


def f32(*shape):
    return jax.ShapeDtypeStruct(shape, jnp.float32)


def call(kernel, name, outs, args, specs=None, scratch=(), limit=None):
    return pl.pallas_call(
        kernel,
        out_shape=tuple(outs),
        in_specs=specs or [VMEM] * len(args),
        out_specs=tuple([VMEM] * len(outs)),
        scratch_shapes=list(scratch),
        compiler_params=pltpu.CompilerParams(vmem_limit_bytes=(limit or 24) * 1024 * 1024),
        name=name,
    )(*args)


def pack_planes(class_map, noise_seed, mean_shift, sample_field):
    ni, nj, nk = class_map.shape
    w = FINE_HALO
    arrays = (class_map, noise_seed, mean_shift, sample_field)

    def kernel(*refs):
        even = checker((nj, nk))
        for out, ins in ((refs[9], refs[0:8:2]), (refs[8], refs[1:8:2])):
            for e in range(w):
                out[e] = (ins[0][e] + 1).astype(jnp.float32)
                out[w + e] = ins[1][e].astype(jnp.float32)
                out[2 * w + e] = ins[2][e]
            for q in range(w // 2):
                out[3 * w + q] = jnp.where(even, ins[3][2 * q + 1], ins[3][2 * q])

    first = pl.BlockSpec((w, nj, nk), lambda n: (0, 0, 0))
    last = pl.BlockSpec((w, nj, nk), lambda n: (ni // w - 1, 0, 0))
    whole = pl.BlockSpec((3 * w + w // 2, nj, nk), lambda n: (0, 0, 0))
    return pl.pallas_call(
        kernel,
        grid=(1,),
        out_shape=(f32(3 * w + w // 2, nj, nk),) * 2,
        in_specs=[first, last] * 4,
        out_specs=(whole, whole),
        name="pack_planes",
    )(*[a for a in arrays for _ in range(2)])


def edge_specs(shape):
    n, nj, nk = shape
    low = pl.BlockSpec((n, 8, nk), lambda g: (0, 0, 0))
    high = pl.BlockSpec((n, 8, nk), lambda g: (0, nj // 8 - 1, 0))
    return [low, high]


def pack_rows_fine(from_low, from_high, class_map, noise_seed, mean_shift, sample_field):
    ni, nj, nk = class_map.shape
    w = FINE_HALO
    count = ni + 2 * w
    arrays = (from_low, from_high, class_map, noise_seed, mean_shift, sample_field)

    def kernel(*refs):
        to_next, to_previous = refs[12:]
        even = checker((8, nk))
        for out, ins, rows in (
            (to_previous, refs[0:12:2], slice(0, w)),
            (to_next, refs[1:12:2], slice(8 - w, 8)),
        ):
            low, high, own = ins[0], ins[1], ins[2:]
            for a in range(3):
                for e in range(w):
                    out[a * count + e] = low[a * w + e, rows]
                    out[a * count + ni + w + e] = high[a * w + e, rows]
                for e in range(ni):
                    if a == 0:
                        v = (own[0][e, rows] + 1).astype(jnp.float32)
                    else:
                        v = own[a][e, rows].astype(jnp.float32)
                    out[a * count + w + e] = v
            base = 3 * count
            for q in range(w // 2):
                out[base + q] = low[3 * w + q, rows]
                out[base + (ni + w) // 2 + q] = high[3 * w + q, rows]
            for q in range(ni // 2):
                v = jnp.where(even, own[3][2 * q + 1], own[3][2 * q])
                out[base + w // 2 + q] = v[rows]

    total = 3 * count + count // 2
    whole = pl.BlockSpec((total, w, nk), lambda g: (0, 0, 0))
    return pl.pallas_call(
        kernel,
        grid=(1,),
        out_shape=(f32(total, w, nk),) * 2,
        in_specs=[s for a in arrays for s in edge_specs(a.shape)],
        out_specs=(whole, whole),
        name="pack_rows_fine",
    )(*[a for a in arrays for _ in range(2)])


def pack_rows(triples, w, name):
    parts = [a for triple in triples for a in triple]
    nk = parts[0].shape[2]
    total = sum(p.shape[0] for p in parts)

    def kernel(*refs):
        to_next, to_previous = refs[-2:]
        at = 0
        for n, part in enumerate(parts):
            size = part.shape[0]
            for e in range(size):
                to_previous[at + e] = refs[2 * n][e, slice(0, w)]
                to_next[at + e] = refs[2 * n + 1][e, slice(8 - w, 8)]
            at += size

    whole = pl.BlockSpec((total, w, nk), lambda g: (0, 0, 0))
    return pl.pallas_call(
        kernel,
        grid=(1,),
        out_shape=(f32(total, w, nk),) * 2,
        in_specs=[s for a in parts for s in edge_specs(a.shape)],
        out_specs=(whole, whole),
        name=name,
    )(*[a for a in parts for _ in range(2)])


def pack_static_rows(static_planes, statics1, statics2):
    w = HALO
    h = w // 2
    sizes = (statics1[0].shape, statics2[0].shape)
    total = 3 * sum(s[0] + 2 * w for s in sizes)

    def kernel(low, high, *refs):
        to_next, to_previous = refs[-2:]
        at = 0
        for level in range(2):
            ni, nj, _ = sizes[level]
            for a in range(3):
                own = refs[3 * level + a]
                for out, start in ((to_previous, 0), (to_next, nj - w)):
                    for src, base in ((low, 0), (high, w + ni)):
                        for e in range(w):
                            if level == 0:
                                v = src[a * w + e, pl.ds(start, w)]
                            else:
                                v = src[3 * w + a * h + e // 2, pl.ds(e % 2 * nj + start, w)]
                            out[at + base + e] = v
                    for e in range(ni):
                        out[at + w + e] = own[e, pl.ds(start, w)]
                at += ni + 2 * w

    args = (*static_planes, *statics1, *statics2)
    return call(kernel, "pack_rows_static", [f32(total, w, LANES)] * 2, args)


def coarse_statics(tables, class_map, noise_seed):
    ni, nj, nk = class_map.shape
    shapes = [(ni >> n, nj >> n, nk >> n) for n in range(LEVELS)]
    w = HALO

    def kernel(d_tab, m_tab, cls_ref, seed_ref, *refs):
        outs, (to_next, to_previous, packed), (t_ref, u_ref) = refs[:6], refs[6:9], refs[9:]
        for level in range(1, LEVELS):
            mi, mj, mk = shapes[level - 1]
            rows = mi // 2 * mj
            width = max(mk, LANES)
            for what in range(3):

                def gather(q):
                    if level == 1:
                        if what < 2:
                            tab = (d_tab, m_tab)[what]
                            (a,) = lookups(cls_ref[2 * q] + 1, [tab])
                            (b,) = lookups(cls_ref[2 * q + 1] + 1, [tab])
                            a = a + b
                        else:
                            a = seed_ref[2 * q].astype(jnp.float32)
                    else:
                        prev = outs[3 * (level - 2) + what]
                        a = prev[2 * q]
                        if what < 2:
                            a = a + prev[2 * q + 1]
                    t_ref[pl.ds(q * mj, mj), :width] = a

                for q in range(mi // 2):
                    gather(q)
                matrix = lane_matrix(width, "pair" if what < 2 else "pick")
                u_ref[pl.ds(0, rows), :] = dot32(t_ref[pl.ds(0, rows), :width], matrix)
                even = u_ref[pl.ds(0, rows // 2, stride=2), :]
                if what < 2:
                    even = 0.125 * (even + u_ref[pl.ds(1, rows // 2, stride=2), :])
                if level < LEVELS - 1:
                    outs[3 * (level - 1) + what][...] = even.reshape(mi // 2, mj // 2, LANES)
                else:
                    lanes = mk // 2
                    if what:
                        even = pltpu.roll(even, what * lanes, 1)
                    total = even if what == 0 else total + even
        packed[...] = total.reshape(shapes[-1][0], shapes[-1][1], LANES)
        mj = shapes[1][1]
        for what in range(3):
            one, two = outs[what], outs[3 + what]
            for e in range(w):
                to_previous[what * w + e] = one[e]
                to_next[what * w + e] = one[shapes[1][0] - w + e]
                n = what * w + e
                at = (3 * w + n // 2, pl.ds(n % 2 * (mj // 2), mj // 2))
                to_previous[at] = two[e]
                to_next[at] = two[shapes[2][0] - w + e]

    outs = []
    for level in range(1, LEVELS - 1):
        outs += [f32(*shapes[level][:2], LANES)] * 3
    outs += [f32(3 * w + 3 * w // 2, shapes[1][1], LANES)] * 2
    outs += [f32(*shapes[-1][:2], LANES)]
    scratch = [
        pltpu.VMEM((ni // 2 * nj, nk), jnp.float32),
        pltpu.VMEM((ni // 2 * nj, LANES), jnp.float32),
    ]
    args = (*tables, class_map, noise_seed)
    got = call(kernel, "coarse_statics", outs, args, [SMEM, SMEM, VMEM, VMEM], scratch)
    return got[:3], got[3:6], got[6], got[7], got[8]


def around(red_black, c, q, even, roll_rows, roll_lanes):
    ref = red_black[1 - c]
    mid, above, below = ref[q + 1], ref[q + 2], ref[q]
    beside = jnp.where(even, below, above) if c == 0 else jnp.where(even, above, below)
    return [
        mid,
        beside,
        pltpu.roll(mid, roll_rows - 1, 0),
        pltpu.roll(mid, 1, 0),
        pltpu.roll(mid, roll_lanes - 1, 1),
        pltpu.roll(mid, 1, 1),
    ]


class Stencil:
    def __init__(self, level, shape):
        self.rows, self.lanes = shape
        self.scale = 0.5 * 0.5**level
        self.lane = lax.broadcasted_iota(jnp.int32, shape, 1)
        self.even = checker(shape)

    def around(self, refs, c, q):
        return around(refs, c, q, self.even, self.rows, self.lanes)

    def weights(self, d_refs, mass, c, q):
        d = d_refs[c][q + 1]
        near = self.around(d_refs, c, q)
        at_end, at_start = self.lane == self.lanes - 1, self.lane == 0
        near[4] = jnp.where(at_end, 0.0, near[4])
        near[5] = jnp.where(at_start, 0.0, near[5])
        total = 6.0 * d
        for v in near:
            total = total + v
        inside = d > 0.0
        diagonal = jnp.where(inside, mass + self.scale * total, 0.0)
        inverse = jnp.where(inside, 1.0 / diagonal, 0.0)
        part = self.scale * inverse
        near[4] = jnp.where(at_end, -d, near[4])
        near[5] = jnp.where(at_start, -d, near[5])
        return diagonal, inverse, [part * (d + v) for v in near]

    def gathered(self, x_refs, w_ref, c, q):
        total = None
        for n, v in enumerate(self.around(x_refs, c, q)):
            term = w_ref[n, c, q] * v
            total = term if total is None else total + term
        return total

    def whole(self, red, black):
        return jnp.where(self.even, red, black), jnp.where(self.even, black, red)


def restricted(st, res_ref, first_pair, ni, nj, t_ref, u_ref, unroll):
    def gather(q):
        p = q + first_pair
        at, after = st.whole(res_ref[0, p], res_ref[1, p])
        _, before = st.whole(res_ref[0, p - 1], res_ref[1, p - 1])
        v = at + 0.5 * (before + after)
        v = v + 0.5 * (pltpu.roll(v, st.rows - 1, 0) + pltpu.roll(v, 1, 0))
        t_ref[pl.ds(pl.multiple_of(q * st.rows, 8), st.rows), :] = v

    loop(0, ni // 2, gather, unroll)
    u_ref[...] = dot32(t_ref[...], lane_matrix(st.lanes, "restrict"))
    size = ni // 2 * st.rows // 2
    coarse = u_ref[pl.ds(0, size, stride=2), :].reshape(ni // 2, st.rows // 2, LANES)
    return coarse[:, : nj // 2, :]


def restrict_scratch(ni, st_rows, nk):
    return [
        pltpu.VMEM((ni // 2 * st_rows, nk), jnp.float32),
        pltpu.VMEM((ni // 2 * st_rows, LANES), jnp.float32),
    ]


def own_noise(noise_seed):
    ni, nj, nk = noise_seed.shape

    def kernel(seed_ref, out):
        even = checker((nj, nk))

        def body(q):
            for c in range(2):
                for at in range(0, nj, 16):
                    rows = pl.ds(at, 16)
                    mask = even[at : at + 16]
                    seeds = (seed_ref[2 * q, rows], seed_ref[2 * q + 1, rows])
                    seed = jnp.where(mask, seeds[c], seeds[1 - c])
                    for t, g in enumerate(raw_noises(seed, 0)):
                        out[t, c, q, rows] = g

        loop(0, ni // 2, body)

    (out,) = call(kernel, "own_noise", [f32(SWEEPS, 2, ni // 2, nj, nk)], (noise_seed,))
    return out


def halo_noise(from_low, from_high):
    w = FINE_HALO
    nj, nk = from_low.shape[1:]

    def kernel(low, high, out_low, out_high):
        even = checker((nj, nk))
        for src, out in ((low, out_low), (high, out_high)):

            def body(q):
                for c in range(2):
                    for at in range(0, nj, 16):
                        rows = pl.ds(at, 16)
                        mask = even[at : at + 16]
                        seeds = (src[w + 2 * q, rows], src[w + 2 * q + 1, rows])
                        seed = jnp.where(mask, seeds[c], seeds[1 - c]).astype(jnp.int32)
                        for t, g in enumerate(raw_noises(seed, 0)):
                            out[t, c, q, rows] = g

            loop(0, w // 2, body)

    return call(kernel, "halo_noise", [f32(SWEEPS, 2, w // 2, nj, nk)] * 2, (from_low, from_high))


def fine_start(tables, own, noise, planes, plane_noise, rows):
    class_map, mean_shift, sample_field = own
    ni, nj, nk = class_map.shape
    w = FINE_HALO
    h = w // 2
    count = ni + 2 * w
    pairs = count // 2
    count_j = nj + 2 * w

    def kernel(d_tab, m_tab, cls_ref, b_ref, sample, g_own, x_lo, x_hi, g_lo, g_hi, y_lo, y_hi, *refs):
        w_ref, r3_ref, n3_ref, m_ref, xb_ref, to_next, to_previous = refs[:7]
        d0, d1, r_ref, x0, x1 = refs[7:]
        d_refs, x_refs = (d0, d1), (x0, x1)
        shape = (count_j, nk)
        st = Stencil(0, shape)
        even, own_even = st.even, st.even[:nj]
        edge_even = st.even[nj:]
        has_low, has_high = has_neighbours("gy")
        zero = jnp.zeros(shape, jnp.float32)
        for g in (0, pairs + 1):
            for ref in (*d_refs, *x_refs):
                ref[g] = zero

        def edge(at, mask=False):
            hi, lo = y_hi[at], y_lo[at]
            if mask:
                hi, lo = hi * has_high, lo * has_low
            return jnp.concatenate([hi, lo], axis=0)

        def split(q, where):
            e = (2 * q, 2 * q + 1)
            if where == 1:
                mids = [(cls_ref[n - w] + 1).astype(jnp.float32) for n in e]
                bs = [b_ref[n - w] for n in e]
                x = jnp.where(own_even, sample[e[1] - w], sample[e[0] - w])
                g_ref, g_at = g_own, q - h
            else:
                src, g_ref = ((x_lo, g_lo) if where == 0 else (x_hi, g_hi))
                off = 0 if where == 0 else -(w + ni)
                mids = [src[n + off] for n in e]
                bs = [src[2 * w + n + off] for n in e]
                g_at = q + off // 2
                x = src[3 * w + g_at]
            cls = [jnp.concatenate([mids[c], edge(e[c], True)], axis=0) for c in range(2)]
            b = [jnp.concatenate([bs[c], edge(2 * count + e[c])], axis=0) for c in range(2)]
            x1[q + 1] = jnp.concatenate([x, edge(3 * count + q, True)], axis=0)
            seeds = [edge(count + e[c]) for c in range(2)]
            for c in range(2):
                number = jnp.where(even, cls[c], cls[1 - c]).astype(jnp.int32)
                d, m = lookups(number, [d_tab, m_tab])
                d_refs[c][q + 1] = d
                m_ref[c, q] = m
                r_ref[0, c, q] = jnp.where(even, b[c], b[1 - c])
                seed = jnp.where(edge_even, seeds[c], seeds[1 - c]).astype(jnp.int32)
                for t, g in enumerate(raw_noises(seed, 0)):
                    out = n3_ref if t == SWEEPS - 1 else r_ref.at[t + 1]
                    out[c, q] = jnp.concatenate([g_ref[t, c, g_at], g], axis=0)

        loop(0, h, lambda q: split(q, 0))
        loop(h, h + ni // 2, lambda q: split(q, 1))
        loop(h + ni // 2, pairs, lambda q: split(q, 2))

        def prepare(q):
            for c in range(2):
                diagonal, inverse, weights = st.weights(d_refs, m_ref[c, q], c, q)
                m_ref[c, q] = diagonal
                for n in range(6):
                    w_ref[n, c, q] = weights[n]
                root = jnp.where(inverse > 0.0, lax.rsqrt(diagonal), 0.0)
                b = r_ref[0, c, q] * inverse
                noise = n3_ref[c, q] * root
                n3_ref[c, q] = noise
                r3_ref[c, q] = b + noise
                r_ref[0, c, q] = b + r_ref[1, c, q] * root
                r_ref[1, c, q] = b + r_ref[2, c, q] * root

        loop(0, pairs, prepare)

        for half in range(2 * SWEEPS - 2):
            t, c = half // 2, half % 2

            def update(q, t=t, c=c):
                x_refs[c][q + 1] = r_ref[t, c, q] + st.gathered(x_refs, w_ref, c, q)

            loop((half + 1) // 2, pairs - (half + 1) // 2, update)

        def write(q):
            xb_ref[q] = x1[q + h + 1, :nj]

        loop(0, ni // 2, write, 4)
        for q in range(h):
            to_previous[q] = x1[q + h + 1, :nj]
            to_next[q] = x1[ni // 2 + q + 1, :nj]

    state = f32(2, pairs, count_j, nk)
    outs = [f32(6, 2, pairs, count_j, nk), state, state, state]
    outs += [f32(ni // 2, nj, nk), f32(h, nj, nk), f32(h, nj, nk)]
    scratch = [
        pltpu.VMEM((pairs + 2, count_j, nk), jnp.float32),
        pltpu.VMEM((pairs + 2, count_j, nk), jnp.float32),
        pltpu.VMEM((SWEEPS, 2, pairs, count_j, nk), jnp.float32),
        pltpu.VMEM((pairs + 2, count_j, nk), jnp.float32),
        pltpu.VMEM((pairs + 2, count_j, nk), jnp.float32),
    ]
    args = (*tables, class_map, mean_shift, sample_field, noise, *planes, *plane_noise, *rows)
    specs = [SMEM, SMEM] + [VMEM] * (len(args) - 2)
    return call(kernel, "fine_start", outs, args, specs, scratch, FINE_LIMIT)


def fine_finish(state, black, planes, rows):
    ni, nj, nk = black.shape[0] * 2, black.shape[1], black.shape[2]
    w = FINE_HALO
    h = w // 2
    pairs = (ni + 2 * w) // 2
    count_j = nj + 2 * w
    halo = HALO

    def kernel(w_ref, r3_ref, n3_ref, m_ref, xb_ref, x_lo, x_hi, y_lo, y_hi, *refs):
        fine, rhs, to_next, to_previous = refs[:4]
        x0, x1, res_ref, t_ref, u_ref = refs[4:]
        x_refs = (x0, x1)
        shape = (count_j, nk)
        st = Stencil(0, shape)
        has_low, has_high = has_neighbours("gy")
        zero = jnp.zeros(shape, jnp.float32)
        for g in (0, pairs + 1):
            for ref in x_refs:
                ref[g] = zero

        def join(q, mid):
            x1[q + 1] = jnp.concatenate([mid, y_hi[q] * has_high, y_lo[q] * has_low], axis=0)

        for q in range(h):
            join(q, x_lo[q])
            join(h + ni // 2 + q, x_hi[q])
        loop(0, ni // 2, lambda q: join(h + q, xb_ref[q]), 4)

        for c, (start, stop) in enumerate(((0, pairs - 1), (1, pairs - 1))):

            def update(q, c=c):
                x_refs[c][q + 1] = r3_ref[c, q] + st.gathered(x_refs, w_ref, c, q)

            loop(start, stop, update)

        def residual(q):
            red = r3_ref[0, q] - n3_ref[0, q] + st.gathered(x_refs, w_ref, 0, q) - x0[q + 1]
            res_ref[0, q] = m_ref[0, q] * red
            res_ref[1, q] = -m_ref[1, q] * n3_ref[1, q]

        loop(h - 1, h + ni // 2, residual)

        def write(q):
            both = st.whole(x0[q + h + 1], x1[q + h + 1])
            fine[2 * q] = both[0][:nj]
            fine[2 * q + 1] = both[1][:nj]

        loop(0, ni // 2, write, 4)
        coarse = restricted(st, res_ref, h, ni, nj, t_ref, u_ref, 2)
        rhs[...] = coarse
        to_previous[...] = coarse[:halo]
        to_next[...] = coarse[ni // 2 - halo :]

    outs = [f32(ni, nj, nk), f32(ni // 2, nj // 2, LANES)] + [f32(halo, nj // 2, LANES)] * 2
    scratch = [
        pltpu.VMEM((pairs + 2, count_j, nk), jnp.float32),
        pltpu.VMEM((pairs + 2, count_j, nk), jnp.float32),
        pltpu.VMEM((2, pairs, count_j, nk), jnp.float32),
    ] + restrict_scratch(ni, count_j, nk)
    args = (*state, black, *planes, *rows)
    return call(kernel, "fine_finish", outs, args, None, scratch, FINE_LIMIT)


def level_sweeps(st, level, pairs, d_refs, m_ref, s_ref, r_ref, w_ref, x_refs, bounds, unroll):
    def prepare(q):
        for c in range(2):
            diagonal, inverse, weights = st.weights(d_refs, m_ref[c, q], c, q)
            m_ref[c, q] = diagonal
            for n in range(6):
                w_ref[n, c, q] = weights[n]
            root = jnp.where(inverse > 0.0, lax.rsqrt(diagonal), 0.0)
            b = r_ref[0, c, q] * inverse
            for t, g in enumerate(raw_noises(s_ref[c, q].astype(jnp.int32), level)):
                noise = g * root
                r_ref[t, c, q] = b + noise
            s_ref[c, q] = noise

    loop(0, pairs, prepare, min(unroll, 2))
    for half in range(2 * SWEEPS):
        t, c = half // 2, half % 2

        def update(q, t=t, c=c, half=half):
            if half == 0:
                x_refs[c][q + 1] = r_ref[t, c, q]
            else:
                x_refs[c][q + 1] = r_ref[t, c, q] + st.gathered(x_refs, w_ref, c, q)

        loop(*bounds(half), update, unroll)


def level_scratch(pairs, rows, lanes):
    guarded = pltpu.VMEM((pairs + 2, rows, lanes), jnp.float32)
    return [
        guarded,
        guarded,
        pltpu.VMEM((2, pairs, rows, lanes), jnp.float32),
        pltpu.VMEM((2, pairs, rows, lanes), jnp.float32),
        pltpu.VMEM((SWEEPS, 2, pairs, rows, lanes), jnp.float32),
        pltpu.VMEM((6, 2, pairs, rows, lanes), jnp.float32),
        guarded,
        guarded,
    ]


def middle_level(level, statics, static_planes, static_rows, rhs, rhs_planes, rhs_rows, tail=None):
    ni, nj, nk = rhs.shape
    w = HALO
    h = w // 2
    count, count_j = ni + 2 * w, nj + 2 * w
    pairs = count // 2
    to_coarsest = level == LEVELS - 2
    plane_base = 0 if level == 1 else 3 * w
    row_base = 0 if level == 1 else 3 * (2 * ni + 2 * w)
    members = lax.axis_size("gx") * lax.axis_size("gy")

    def kernel(*refs):
        refs = list(refs)
        own = refs[:4]
        sx_lo, sx_hi, sy_lo, sy_hi, bx_lo, bx_hi, by_lo, by_hi = refs[4:12]
        at = 12
        if to_coarsest:
            tail_ref, spread = refs[12:14]
            at = 14
        else:
            out, to_next, to_previous = refs[12:15]
            at = 15
        d0, d1, m_ref, s_ref, r_ref, w_ref, x0, x1, t_ref, u_ref = refs[at:]
        d_refs, x_refs = (d0, d1), (x0, x1)
        shape = (count_j, nk)
        st = Stencil(level, shape)
        x_has = has_neighbours("gx")
        y_has = has_neighbours("gy")
        zero = jnp.zeros(shape, jnp.float32)
        for g in (0, pairs + 1):
            for ref in (*d_refs, *x_refs):
                ref[g] = zero

        def static_plane(src, a, q, k):
            if level == 1:
                return src[a * w + 2 * q + k]
            return src[plane_base + a * h + q, pl.ds(k * nj, nj)]

        def fields(a, q, k, where):
            e = 2 * q + k
            if where == 1:
                mid = own[a][e - w]
            else:
                p = q if where == 0 else q - h - ni // 2
                if a < 3:
                    mid = static_plane((sx_lo, sx_hi)[where // 2], a, p, k)
                else:
                    mid = (bx_lo, bx_hi)[where // 2][2 * p + k]
                if a == 0:
                    mid = mid * x_has[where // 2]
            if a < 3:
                r = row_base + a * count + e
                hi, lo = sy_hi[r], sy_lo[r]
            else:
                hi, lo = by_hi[e], by_lo[e]
            if a == 0:
                hi, lo = hi * y_has[1], lo * y_has[0]
                if where != 1:
                    hi, lo = hi * x_has[where // 2], lo * x_has[where // 2]
            return jnp.concatenate([mid, hi, lo], axis=0)

        def split(q, where):
            for a in range(4):
                v = st.whole(fields(a, q, 0, where), fields(a, q, 1, where))
                for c in range(2):
                    if a == 0:
                        d_refs[c][q + 1] = v[c]
                    else:
                        (m_ref, s_ref, r_ref.at[0])[a - 1][c, q] = v[c]

        loop(0, h, lambda q: split(q, 0), 4)
        loop(h, h + ni // 2, lambda q: split(q, 1), 4)
        loop(h + ni // 2, pairs, lambda q: split(q, 2), 4)

        def bounds(half):
            return half // 2, (ni + w + 2 * SWEEPS - half) // 2 + 1

        level_sweeps(st, level, pairs, d_refs, m_ref, s_ref, r_ref, w_ref, x_refs, bounds, 4)

        def residual(q):
            red = r_ref[SWEEPS - 1, 0, q] - s_ref[0, q] + st.gathered(x_refs, w_ref, 0, q) - x0[q + 1]
            r_ref[0, 0, q] = m_ref[0, q] * red
            r_ref[0, 1, q] = -m_ref[1, q] * s_ref[1, q]

        loop(h - 1, h + ni // 2, residual, 4)
        coarse = restricted(st, r_ref.at[0], h, ni, nj, t_ref, u_ref, 4)
        if to_coarsest:
            lanes = nk // 4
            coarse = jnp.where(lax.broadcasted_iota(jnp.int32, coarse.shape, 2) < lanes, coarse, 0.0)
            block = tail_ref[...] + pltpu.roll(coarse, 3 * lanes, 2)
            for n in range(members):
                spread[n] = block
        else:
            out[...] = coarse
            to_previous[...] = coarse[:w]
            to_next[...] = coarse[ni // 2 - w :]

    args = [*statics, rhs, *static_planes, *static_rows, *rhs_planes, *rhs_rows]
    if to_coarsest:
        args.append(tail)
        outs = [f32(members, ni // 2, nj // 2, LANES)]
    else:
        outs = [f32(ni // 2, nj // 2, LANES)] + [f32(w, nj // 2, LANES)] * 2
    scratch = level_scratch(pairs, count_j, nk) + restrict_scratch(ni, count_j, nk)
    return call(kernel, f"level_{level}", outs, args, None, scratch)


def coarsest_level(blocks, lanes):
    members, mi, mj, _ = blocks.shape
    gx, gy = lax.axis_size("gx"), lax.axis_size("gy")
    pairs = gx * mi // 2
    nj = gy * mj
    count_j = nj + 8
    level = LEVELS - 1

    def kernel(blocks_ref, out, d0, d1, m_ref, s_ref, r_ref, w_ref, x0, x1, t_ref):
        d_refs, x_refs = (d0, d1), (x0, x1)
        shape = (count_j, LANES)
        st = Stencil(level, shape)
        zero = jnp.zeros(shape, jnp.float32)
        for g in (0, pairs + 1):
            for ref in (*d_refs, *x_refs):
                ref[g] = zero
        for i in range(gx * mi):
            for g in range(gy):
                t_ref[i, pl.ds(g * mj, mj), :] = blocks_ref[i // mi * gy + g, i % mi]
            t_ref[i, pl.ds(nj, 8), :] = jnp.zeros((8, LANES), jnp.float32)
        inside = st.lane < lanes

        def split(q):
            both = st.whole(t_ref[2 * q], t_ref[2 * q + 1])
            for a in range(4):
                for c in range(2):
                    v = both[c] if a == 0 else pltpu.roll(both[c], LANES - a * lanes, 1)
                    v = jnp.where(inside, v, 0.0)
                    if a == 0:
                        d_refs[c][q + 1] = v
                    else:
                        (m_ref, s_ref, r_ref.at[0])[a - 1][c, q] = v

        loop(0, pairs, split, 8)
        level_sweeps(
            st, level, pairs, d_refs, m_ref, s_ref, r_ref, w_ref, x_refs, lambda half: (0, pairs), 8
        )
        at_x, at_y = lax.axis_index("gx"), lax.axis_index("gy")
        for n in range(mi // 2):
            p = at_x * (mi // 2) + n + 1
            for k, v in enumerate(st.whole(x0[p], x1[p])):
                out[2 * n + k] = pltpu.roll(v, count_j - at_y * mj, 0)[:mj, :lanes]

    scratch = level_scratch(pairs, count_j, LANES)
    scratch += [pltpu.VMEM((gx * mi, count_j, LANES), jnp.float32)]
    (out,) = call(kernel, f"level_{level}", [f32(mi, mj, lanes)], (blocks,), None, scratch)
    return out


def both_ways(to_next, to_previous, axis, ring=True):
    size = lax.axis_size(axis)
    up = [(i, (i + 1) % size) for i in range(size if ring else size - 1)]
    down = [(j, i) for i, j in up]
    return lax.ppermute(to_next, axis, up), lax.ppermute(to_previous, axis, down)


def tied(first, *others):
    return lax.optimization_barrier((first, *others))[0]


def per_device(sample_field, mean_shift, class_map, noise_seed, diffusion_table, mass_table):
    tables = (diffusion_table, mass_table)
    nk = class_map.shape[2]
    arrays = (class_map, noise_seed, mean_shift, sample_field)

    planes = both_ways(*pack_planes(*arrays), "gx", False)
    noise = own_noise(noise_seed)
    statics1, statics2, static_next, static_previous, tail = coarse_statics(
        tables, class_map, noise_seed
    )
    planes = lax.optimization_barrier((*planes, noise, static_next))[:2]

    rows = both_ways(*pack_rows_fine(*planes, *arrays), "gy")
    plane_noise = halo_noise(*planes)
    rows = lax.optimization_barrier((*rows, *plane_noise))[:2]

    *state, black, to_next, to_previous = fine_start(
        tables, (class_map, mean_shift, sample_field), noise, planes, plane_noise, rows
    )
    planes = both_ways(to_next, to_previous, "gx", False)
    static_planes = both_ways(static_next, static_previous, "gx")
    rows = both_ways(*pack_rows([(planes[0], black, planes[1])], FINE_HALO, "pack_rows_black"), "gy")
    static_rows = both_ways(*pack_static_rows(static_planes, statics1, statics2), "gy")

    fine, rhs, to_next, to_previous = fine_finish(state, black, planes, rows)
    for level in range(1, LEVELS - 1):
        planes = both_ways(to_next, to_previous, "gx")
        rows = both_ways(*pack_rows([(planes[0], rhs, planes[1])], HALO, f"pack_rows_{level}"), "gy")
        statics = (statics1, statics2)[level - 1]
        last = level == LEVELS - 2
        got = middle_level(
            level, statics, static_planes, static_rows, rhs, planes, rows, tail if last else None
        )
        if not last:
            rhs, to_next, to_previous = got
    blocks = lax.all_to_all(got[0], ("gx", "gy"), 0, 0, tiled=True)
    return fine, coarsest_level(blocks, nk >> (LEVELS - 1))


def solution(mesh):
    spec = P("gx", "gy", None)
    return jax.shard_map(
        per_device,
        mesh=mesh,
        in_specs=(spec, spec, spec, spec, P(), P()),
        out_specs=(spec, spec),
        check_vma=False,
    )
```

time: 817 us -> 176 us (0.22)
  the two profiles are of different devices: /device:TPU:28 before, /device:TPU:0 now
where the time goes in v2:
time: 176 us; the launch traced here: 175 us
  Pallas kernels  67.5 us (38%)
  starting transfers between devices  38.7 us (22%)
  local copies, waits for them, and re-layouts  28.9 us (16%)
  waiting for transfers between devices  22.6 us (13%)
  blocking collectives  16.6 us (9%)
    pallas_call x9, Pallas kernels, call(): pl.pallas_call(kernel, out_shape=tuple(outs), in_specs=specs or [VMEM] *...  57.1 us
    unnamed x100, local copies, waits for them, and re-layouts  28.9 us
    ppermute x10, starting transfers between devices, both_ways(): lax.ppermute(to_previous, axis, down)  25 us
    all_to_all x1, blocking collectives, per_device(): blocks = lax.all_to_all(got[0], ('gx', 'gy'), 0, 0, tiled=True)  16.6 us
    ppermute x10, waiting for transfers between devices, both_ways(): lax.ppermute(to_next, axis, up)  14.8 us
    ppermute x10, starting transfers between devices, both_ways(): lax.ppermute(to_next, axis, up)  13.7 us
    ppermute x10, waiting for transfers between devices, both_ways(): lax.ppermute(to_previous, axis, down)  7.78 us
    pallas_call x3, Pallas kernels, pack_rows(): pl.pallas_call(kernel, grid=(1,), out_shape=(f32(total, w, nk),) * 2, in_...  4.99 us
  transfers between devices with their start and end apart: 20, of which 10 were waited for; matrix products, arithmetic and copies ran while one was open for 0% of the time, Pallas kernels for 28%

profile of v2, /device:TPU:0, one launch (start us, length us, event | category | flops | bytes accessed | tf_op | source)
XLA Modules:
  0.0 175.1 jit_solution(16777693964192187450)
XLA Ops:
  3.1 5.0 %collective-permute-start = (f32[14,32,256]{2,1,0:T(8,128)}, f32[14,32,256]{2,1,0:T(8,128)S(1)}, u32[]{:S(2)}, u32[]{:S(2)}) collective-permute-start(f32[14,32,256]{2,1,0:T(8,128)} %get-tuple-element.43), channel_id=1, source_target_pairs={{0,8},{8,16},{16,24},{1,9},{9,17},{17,25},{2,10},{10,18},{18,26},{... | collective-permute-start | bytes 1376264 | tf_op jit(solution)/shard_map/ppermute | solution.py:832
  9.4 4.5 %coarse_statics.1 = (f32[16,16,128]{2,1,0:T(8,128)S(1)}, f32[16,16,128]{2,1,0:T(8,128)S(1)}, f32[16,16,128]{2,1,0:T(8,128)S(1)}, f32[8,8,128]{2,1,0:T(8,128)S(1)...) custom-call(f32[8]{0:T(128)S(1)} %copy-done.48, ...), custom_call_target="tpu_custom_call" | custom-call | tf_op jit(solution)/shard_map/coarse_statics/pallas_call | solution.py:125
  15.1 2.6 %collective-permute-start.8 = (f32[36,16,128]{2,1,0:T(8,128)}, f32[36,16,128]{2,1,0:T(8,128)S(1)}, u32[]{:S(2)}, u32[]{:S(2)}) collective-permute-start(f32[36,16,128]{2,1,0:T(8,128)} %get-tuple-element.45), channel_id=1, source_target_pairs={{0,8},{8,16},{16,24},{24,0},{1,9},{9,17},{17,25},{25,1},{2,10},{10... | collective-permute-start | bytes 884744 | tf_op jit(solution)/shard_map/ppermute | solution.py:832
  19.8 4.5 %own_noise.1.g_own = f32[3,2,16,32,256]{4,3,2,1,0:T(8,128)S(1)} custom-call(s32[32,32,256]{2,1,0:T(8,128)S(1)} %copy-done.2), custom_call_target="tpu_custom_call" | custom-call | tf_op jit(solution)/shard_map/own_noise/pallas_call | solution.py:125
  27.6 3.0 %pack_rows_fine.1 = (f32[140,4,256]{2,1,0:T(4,128)}, f32[140,4,256]{2,1,0:T(4,128)}) custom-call(f32[14,32,256]{2,1,0:T(8,128)} %copy-done.6, f32[14,32,256]{2,1,0:T(8,128)} %copy-done.6, f32[14,32,256]{2,1,0:T(8,128)} %copy-done.9, f32[14,32,256]{2,1,0:T(8,128)} %copy-done.9, s32[32,32,256]{2,1,0:T(8,128)} %cls_ref.3, s32[32,32,256]{2,1,0:T(8,128)} %cls_ref.3, ...), custom_call_target="tpu_custom_call" | custom-call | tf_op jit(solution)/shard_map/pack_rows_fine/pallas_call | solution.py:205
  30.6 2.6 %collective-permute-start.3 = (f32[140,4,256]{2,1,0:T(4,128)}, f32[140,4,256]{2,1,0:T(4,128)S(1)}, u32[]{:S(2)}, u32[]{:S(2)}) collective-permute-start(f32[140,4,256]{2,1,0:T(4,128)} %get-tuple-element.51), channel_id=1, source_target_pairs={{1,0},{2,1},{3,2},{4,3},{5,4},{6,5},{7,6},{0,7},{9,8},{10,9},{11,1... | collective-permute-start | bytes 1720328 | tf_op jit(solution)/shard_map/ppermute | solution.py:832
  38.8 2.6 %collective-permute-start.11 = (f32[168,8,128]{2,1,0:T(8,128)}, f32[168,8,128]{2,1,0:T(8,128)S(1)}, u32[]{:S(2)}, u32[]{:S(2)}) collective-permute-start(f32[168,8,128]{2,1,0:T(8,128)} %get-tuple-element.73), channel_id=1, source_target_pairs={{1,0},{2,1},{3,2},{4,3},{5,4},{6,5},{7,6},{0,7},{9,8},{10,9},{11,1... | collective-permute-start | bytes 2064392 | tf_op jit(solution)/shard_map/ppermute | solution.py:832
  48.9 20.2 %fine_start.1 = (f32[6,2,20,40,256]{4,3,2,1,0:T(8,128)}, f32[2,20,40,256]{3,2,1,0:T(8,128)S(1)}, f32[2,20,40,256]{3,2,1,0:T(8,128)S(1)}, f32[2,20,40,256]{3,2,1,...) custom-call(f32[8]{0:T(128)S(1)} %copy-done.48, ...), custom_call_target="tpu_custom_call" | custom-call | tf_op jit(solution)/shard_map/fine_start/pallas_call | solution.py:125
  73.5 5.6 %collective-permute-start.4 = (f32[2,32,256]{2,1,0:T(8,128)S(1)}, f32[2,32,256]{2,1,0:T(8,128)S(1)}, u32[]{:S(2)}, u32[]{:S(2)}) collective-permute-start(f32[2,32,256]{2,1,0:T(8,128)S(1)} %get-tuple-element.59), channel_id=1, source_target_pairs={{0,8},{8,16},{16,24},{1,9},{9,17},{17,25},{2,10},{10,18},{18,26},{... | collective-permute-start | bytes 196616 | tf_op jit(solution)/shard_map/ppermute | solution.py:832
  81.5 4.3 %collective-permute-done.5.refs_4_.refs_5_.x_hi = f32[2,32,256]{2,1,0:T(8,128)S(1)} collective-permute-done((f32[2,32,256]{2,1,0:T(8,128)S(1)}, f32[2,32,256]{2,1,0:T(8,128)S(1)}, u32[]{:S(2)}, u32[]{:S(2)}) %collective-permute-start.5) | collective-permute-done | bytes 65568 | tf_op jit(solution)/shard_map/ppermute | solution.py:832
  88.1 2.6 %collective-permute-start.7 = (f32[20,4,256]{2,1,0:T(4,128)}, f32[20,4,256]{2,1,0:T(4,128)S(1)}, u32[]{:S(2)}, u32[]{:S(2)}) collective-permute-start(f32[20,4,256]{2,1,0:T(4,128)} %get-tuple-element.62), channel_id=1, source_target_pairs={{1,0},{2,1},{3,2},{4,3},{5,4},{6,5},{7,6},{0,7},{9,8},{10,9},{11,1... | collective-permute-start | bytes 245768 | tf_op jit(solution)/shard_map/ppermute | solution.py:832
  90.7 2.4 %collective-permute-done.6.y_lo = f32[20,4,256]{2,1,0:T(4,128)S(1)} collective-permute-done((f32[20,4,256]{2,1,0:T(4,128)}, f32[20,4,256]{2,1,0:T(4,128)S(1)}, u32[]{:S(2)}, u32[]{:S(2)}) %collective-permute-start.6) | collective-permute-done | bytes 81952 | tf_op jit(solution)/shard_map/ppermute | solution.py:832
  99.1 10.4 %fine_finish.1 = (f32[32,32,256]{2,1,0:T(8,128)}, f32[16,16,128]{2,1,0:T(8,128)S(1)}, f32[8,16,128]{2,1,0:T(8,128)S(1)}, f32[8,16,128]{2,1,0:T(8,128)S(1)}) custom-call(f32[6,2,20,40,256]{4,3,2,1,0:T(8,128)} %get-tuple-element.54.w_ref, f32[2,20,40,256]{3,2,1,0:T(8,128)S(1)} %copy-done.17, f32[2,20,40,256]{3,2,1,0:T(8,128)S(1)} %copy-done.19, ...), custom_call_target="tpu_custom_call" | custom-call | tf_op jit(solution)/shard_map/fine_finish/pallas_call | solution.py:125
  110.7 3.3 %collective-permute-start.13 = (f32[8,16,128]{2,1,0:T(8,128)S(1)}, f32[8,16,128]{2,1,0:T(8,128)S(1)}, u32[]{:S(2)}, u32[]{:S(2)}) collective-permute-start(f32[8,16,128]{2,1,0:T(8,128)S(1)} %get-tuple-element.75), channel_id=1, source_target_pairs={{8,0},{16,8},{24,16},{0,24},{9,1},{17,9},{25,17},{1,25},{10,2},{18... | collective-permute-start | bytes 196616 | tf_op jit(solution)/shard_map/ppermute | solution.py:832
  114.0 2.5 %collective-permute-done.12.refs_0_.refs_1_.refs_8_ = f32[8,16,128]{2,1,0:T(8,128)S(1)} collective-permute-done((f32[8,16,128]{2,1,0:T(8,128)S(1)}, f32[8,16,128]{2,1,0:T(8,128)S(1)}, u32[]{:S(2)}, u32[]{:S(2)}) %collective-permute-start.12) | collective-permute-done | bytes 65568 | tf_op jit(solution)/shard_map/ppermute | solution.py:832
  118.8 2.6 %collective-permute-start.15 = (f32[32,8,128]{2,1,0:T(8,128)}, f32[32,8,128]{2,1,0:T(8,128)S(1)}, u32[]{:S(2)}, u32[]{:S(2)}) collective-permute-start(f32[32,8,128]{2,1,0:T(8,128)} %get-tuple-element.77), channel_id=1, source_target_pairs={{1,0},{2,1},{3,2},{4,3},{5,4},{6,5},{7,6},{0,7},{9,8},{10,9},{11,1... | collective-permute-start | bytes 393224 | tf_op jit(solution)/shard_map/ppermute | solution.py:832
  121.5 4.0 %collective-permute-done.14.refs_10_ = f32[32,8,128]{2,1,0:T(8,128)S(1)} collective-permute-done((f32[32,8,128]{2,1,0:T(8,128)}, f32[32,8,128]{2,1,0:T(8,128)S(1)}, u32[]{:S(2)}, u32[]{:S(2)}) %collective-permute-start.14) | collective-permute-done | bytes 131104 | tf_op jit(solution)/shard_map/ppermute | solution.py:832
  128.1 6.6 %level_1.1 = (f32[8,8,128]{2,1,0:T(8,128)S(1)}, f32[8,8,128]{2,1,0:T(8,128)S(1)}, f32[8,8,128]{2,1,0:T(8,128)S(1)}) custom-call(f32[16,16,128]{2,1,0:T(8,128)S(1)} %copy-done.33, f32[16,16,128]{2,1,0:T(8,128)S(1)} %copy-done.36, f32[16,16,128]{2,1,0:T(8,128)S(1)} %copy-done.39, f32[16,16,128]{2,1,0:T(8,128)S(1)} %copy-done.23, ...), custom_call_target="tpu_custom_call" | custom-call | tf_op jit(solution)/shard_map/level_1/pallas_call | solution.py:125
  135.3 3.8 %collective-permute-start.17 = (f32[8,8,128]{2,1,0:T(8,128)S(1)}, f32[8,8,128]{2,1,0:T(8,128)S(1)}, u32[]{:S(2)}, u32[]{:S(2)}) collective-permute-start(f32[8,8,128]{2,1,0:T(8,128)S(1)} %get-tuple-element.80), channel_id=1, source_target_pairs={{8,0},{16,8},{24,16},{0,24},{9,1},{17,9},{25,17},{1,25},{10,2},{18... | collective-permute-start | bytes 98312 | tf_op jit(solution)/shard_map/ppermute | solution.py:832
  143.3 2.6 %collective-permute-start.19 = (f32[24,8,128]{2,1,0:T(8,128)}, f32[24,8,128]{2,1,0:T(8,128)S(1)}, u32[]{:S(2)}, u32[]{:S(2)}) collective-permute-start(f32[24,8,128]{2,1,0:T(8,128)} %get-tuple-element.82), channel_id=1, source_target_pairs={{1,0},{2,1},{3,2},{4,3},{5,4},{6,5},{7,6},{0,7},{9,8},{10,9},{11,1... | collective-permute-start | bytes 294920 | tf_op jit(solution)/shard_map/ppermute | solution.py:832
  146.0 2.5 %collective-permute-done.18.refs_10_ = f32[24,8,128]{2,1,0:T(8,128)S(1)} collective-permute-done((f32[24,8,128]{2,1,0:T(8,128)}, f32[24,8,128]{2,1,0:T(8,128)S(1)}, u32[]{:S(2)}, u32[]{:S(2)}) %collective-permute-start.18) | collective-permute-done | bytes 98336 | tf_op jit(solution)/shard_map/ppermute | solution.py:832
  150.8 4.3 %level_2.1 = f32[32,4,4,128]{3,2,1,0:T(4,128)S(1)} custom-call(f32[8,8,128]{2,1,0:T(8,128)S(1)} %get-tuple-element.64.refs_3_.refs_0_, f32[8,8,128]{2,1,0:T(8,128)S(1)} %get-tuple-element.65.refs_4_.refs_1_, f32[8,8,128]{2,1,0:T(8,128)S(1)} %copy-done.47, f32[8,8,128]{2,1,0:T(8,128)S(1)} %copy-done.41, f32[36,16,128]{2,1,0:T(8,128)S(1)} %copy-done.15, ...), custom_call_target="tpu_custom_call" | custom-call | tf_op jit(solution)/shard_map/level_2/pallas_call | solution.py:125
  155.0 16.6 %all_to_all.5.blocks_ref = f32[32,4,4,128]{3,2,1,0:T(4,128)S(1)} all-to-all(f32[32,4,4,128]{3,2,1,0:T(4,128)S(1)} %level_2.1), channel_id=1, replica_groups=mesh['gx'=4,'gy'=8] {'gx','gy'}, dimensions={0} | all-to-all | bytes 524288 | tf_op jit(solution)/shard_map/all_to_all | solution.py:874
  171.7 3.4 %level_3.1 = f32[4,4,32]{2,1,0:T(4,128)} custom-call(f32[32,4,4,128]{3,2,1,0:T(4,128)S(1)} %all_to_all.5.blocks_ref), custom_call_target="tpu_custom_call" | custom-call | tf_op jit(solution)/shard_map/level_3/pallas_call | solution.py:125
  (131 shorter events, 51.5 us)
Async XLA Ops:
  3.1 23.0 %collective-permute-start = (f32[14,32,256]{2,1,0:T(8,128)}, f32[14,32,256]{2,1,0:T(8,128)S(1)}, u32[]{:S(2)}, u32[]{:S(2)}) collective-permute-start(f32[14,32,256]{2,1,0:T(8,128)} %get-tuple-element.43), channel_id=1, source_target_pairs={{0,8},{8,16},{16,24},{1,9},{9,17},{17,25},{2,10},{10,18},{18,26},{... | collective-permute-start | bytes 1376264 | tf_op jit(solution)/shard_map/ppermute | solution.py:832
  8.0 18.0 %collective-permute-start.1 = (f32[14,32,256]{2,1,0:T(8,128)}, f32[14,32,256]{2,1,0:T(8,128)S(1)}, u32[]{:S(2)}, u32[]{:S(2)}) collective-permute-start(f32[14,32,256]{2,1,0:T(8,128)} %get-tuple-element.44), channel_id=1, source_target_pairs={{8,0},{16,8},{24,16},{9,1},{17,9},{25,17},{10,2},{18,10},{26,18},{... | collective-permute-start | bytes 1376264 | tf_op jit(solution)/shard_map/ppermute | solution.py:832
  15.1 18.1 %collective-permute-start.8 = (f32[36,16,128]{2,1,0:T(8,128)}, f32[36,16,128]{2,1,0:T(8,128)S(1)}, u32[]{:S(2)}, u32[]{:S(2)}) collective-permute-start(f32[36,16,128]{2,1,0:T(8,128)} %get-tuple-element.45), channel_id=1, source_target_pairs={{0,8},{8,16},{16,24},{24,0},{1,9},{9,17},{17,25},{25,1},{2,10},{10... | collective-permute-start | bytes 884744 | tf_op jit(solution)/shard_map/ppermute | solution.py:832
  17.8 17.1 %collective-permute-start.9 = (f32[36,16,128]{2,1,0:T(8,128)}, f32[36,16,128]{2,1,0:T(8,128)}, u32[]{:S(2)}, u32[]{:S(2)}) collective-permute-start(f32[36,16,128]{2,1,0:T(8,128)} %get-tuple-element.71), channel_id=1, source_target_pairs={{8,0},{16,8},{24,16},{0,24},{9,1},{17,9},{25,17},{1,25},{10,2},{18... | collective-permute-start | bytes 884744 | tf_op jit(solution)/shard_map/ppermute | solution.py:832
  30.6 14.5 %collective-permute-start.2 = (f32[140,4,256]{2,1,0:T(4,128)}, f32[140,4,256]{2,1,0:T(4,128)S(1)}, u32[]{:S(2)}, u32[]{:S(2)}) collective-permute-start(f32[140,4,256]{2,1,0:T(4,128)} %get-tuple-element.50), channel_id=1, source_target_pairs={{0,1},{1,2},{2,3},{3,4},{4,5},{5,6},{6,7},{7,0},{8,9},{9,10},{10,1... | collective-permute-start | bytes 1720328 | tf_op jit(solution)/shard_map/ppermute | solution.py:832
  30.6 16.3 %collective-permute-start.3 = (f32[140,4,256]{2,1,0:T(4,128)}, f32[140,4,256]{2,1,0:T(4,128)S(1)}, u32[]{:S(2)}, u32[]{:S(2)}) collective-permute-start(f32[140,4,256]{2,1,0:T(4,128)} %get-tuple-element.51), channel_id=1, source_target_pairs={{1,0},{2,1},{3,2},{4,3},{5,4},{6,5},{7,6},{0,7},{9,8},{10,9},{11,1... | collective-permute-start | bytes 1720328 | tf_op jit(solution)/shard_map/ppermute | solution.py:832
  38.8 82.6 %collective-permute-start.10 = (f32[168,8,128]{2,1,0:T(8,128)}, f32[168,8,128]{2,1,0:T(8,128)S(1)}, u32[]{:S(2)}, u32[]{:S(2)}) collective-permute-start(f32[168,8,128]{2,1,0:T(8,128)} %get-tuple-element.72), channel_id=1, source_target_pairs={{0,1},{1,2},{2,3},{3,4},{4,5},{5,6},{6,7},{7,0},{8,9},{9,10},{10,1... | collective-permute-start | bytes 2064392 | tf_op jit(solution)/shard_map/ppermute | solution.py:832
  38.8 82.6 %collective-permute-start.11 = (f32[168,8,128]{2,1,0:T(8,128)}, f32[168,8,128]{2,1,0:T(8,128)S(1)}, u32[]{:S(2)}, u32[]{:S(2)}) collective-permute-start(f32[168,8,128]{2,1,0:T(8,128)} %get-tuple-element.73), channel_id=1, source_target_pairs={{1,0},{2,1},{3,2},{4,3},{5,4},{6,5},{7,6},{0,7},{9,8},{10,9},{11,1... | collective-permute-start | bytes 2064392 | tf_op jit(solution)/shard_map/ppermute | solution.py:832
  73.5 7.9 %collective-permute-start.4 = (f32[2,32,256]{2,1,0:T(8,128)S(1)}, f32[2,32,256]{2,1,0:T(8,128)S(1)}, u32[]{:S(2)}, u32[]{:S(2)}) collective-permute-start(f32[2,32,256]{2,1,0:T(8,128)S(1)} %get-tuple-element.59), channel_id=1, source_target_pairs={{0,8},{8,16},{16,24},{1,9},{9,17},{17,25},{2,10},{10,18},{18,26},{... | collective-permute-start | bytes 196616 | tf_op jit(solution)/shard_map/ppermute | solution.py:832
  79.1 6.7 %collective-permute-start.5 = (f32[2,32,256]{2,1,0:T(8,128)S(1)}, f32[2,32,256]{2,1,0:T(8,128)S(1)}, u32[]{:S(2)}, u32[]{:S(2)}) collective-permute-start(f32[2,32,256]{2,1,0:T(8,128)S(1)} %get-tuple-element.60), channel_id=1, source_target_pairs={{8,0},{16,8},{24,16},{9,1},{17,9},{25,17},{10,2},{18,10},{26,18},{... | collective-permute-start | bytes 196616 | tf_op jit(solution)/shard_map/ppermute | solution.py:832
  88.1 5.0 %collective-permute-start.6 = (f32[20,4,256]{2,1,0:T(4,128)}, f32[20,4,256]{2,1,0:T(4,128)S(1)}, u32[]{:S(2)}, u32[]{:S(2)}) collective-permute-start(f32[20,4,256]{2,1,0:T(4,128)} %get-tuple-element.61), channel_id=1, source_target_pairs={{0,1},{1,2},{2,3},{3,4},{4,5},{5,6},{6,7},{7,0},{8,9},{9,10},{10,1... | collective-permute-start | bytes 245768 | tf_op jit(solution)/shard_map/ppermute | solution.py:832
  88.1 5.0 %collective-permute-start.7 = (f32[20,4,256]{2,1,0:T(4,128)}, f32[20,4,256]{2,1,0:T(4,128)S(1)}, u32[]{:S(2)}, u32[]{:S(2)}) collective-permute-start(f32[20,4,256]{2,1,0:T(4,128)} %get-tuple-element.62), channel_id=1, source_target_pairs={{1,0},{2,1},{3,2},{4,3},{5,4},{6,5},{7,6},{0,7},{9,8},{10,9},{11,1... | collective-permute-start | bytes 245768 | tf_op jit(solution)/shard_map/ppermute | solution.py:832
  99.1 26.4 %copy-start.33 = (f32[16,16,128]{2,1,0:T(8,128)S(1)}, f32[16,16,128]{2,1,0:T(8,128)}, u32[]{:S(2)}) copy-start(f32[16,16,128]{2,1,0:T(8,128)} %copy-done.32) | copy-start | bytes 393220
  99.1 26.4 %copy-start.36 = (f32[16,16,128]{2,1,0:T(8,128)S(1)}, f32[16,16,128]{2,1,0:T(8,128)}, u32[]{:S(2)}) copy-start(f32[16,16,128]{2,1,0:T(8,128)} %copy-done.34) | copy-start | bytes 393220
  99.1 26.4 %copy-start.39 = (f32[16,16,128]{2,1,0:T(8,128)S(1)}, f32[16,16,128]{2,1,0:T(8,128)}, u32[]{:S(2)}) copy-start(f32[16,16,128]{2,1,0:T(8,128)} %copy-done.37) | copy-start | bytes 393220
  110.2 6.3 %collective-permute-start.12 = (f32[8,16,128]{2,1,0:T(8,128)S(1)}, f32[8,16,128]{2,1,0:T(8,128)S(1)}, u32[]{:S(2)}, u32[]{:S(2)}) collective-permute-start(f32[8,16,128]{2,1,0:T(8,128)S(1)} %get-tuple-element.74), channel_id=1, source_target_pairs={{0,8},{8,16},{16,24},{24,0},{1,9},{9,17},{17,25},{25,1},{2,10},{10... | collective-permute-start | bytes 196616 | tf_op jit(solution)/shard_map/ppermute | solution.py:832
  110.7 5.8 %collective-permute-start.13 = (f32[8,16,128]{2,1,0:T(8,128)S(1)}, f32[8,16,128]{2,1,0:T(8,128)S(1)}, u32[]{:S(2)}, u32[]{:S(2)}) collective-permute-start(f32[8,16,128]{2,1,0:T(8,128)S(1)} %get-tuple-element.75), channel_id=1, source_target_pairs={{8,0},{16,8},{24,16},{0,24},{9,1},{17,9},{25,17},{1,25},{10,2},{18... | collective-permute-start | bytes 196616 | tf_op jit(solution)/shard_map/ppermute | solution.py:832
  117.2 31.3 %copy-start.47 = (f32[8,8,128]{2,1,0:T(8,128)S(1)}, f32[8,8,128]{2,1,0:T(8,128)}, u32[]{:S(2)}) copy-start(f32[8,8,128]{2,1,0:T(8,128)} %copy-done.46) | copy-start | bytes 98308
  118.8 6.7 %collective-permute-start.14 = (f32[32,8,128]{2,1,0:T(8,128)}, f32[32,8,128]{2,1,0:T(8,128)S(1)}, u32[]{:S(2)}, u32[]{:S(2)}) collective-permute-start(f32[32,8,128]{2,1,0:T(8,128)} %get-tuple-element.76), channel_id=1, source_target_pairs={{0,1},{1,2},{2,3},{3,4},{4,5},{5,6},{6,7},{7,0},{8,9},{9,10},{10,1... | collective-permute-start | bytes 393224 | tf_op jit(solution)/shard_map/ppermute | solution.py:832
  118.8 6.7 %collective-permute-start.15 = (f32[32,8,128]{2,1,0:T(8,128)}, f32[32,8,128]{2,1,0:T(8,128)S(1)}, u32[]{:S(2)}, u32[]{:S(2)}) collective-permute-start(f32[32,8,128]{2,1,0:T(8,128)} %get-tuple-element.77), channel_id=1, source_target_pairs={{1,0},{2,1},{3,2},{4,3},{5,4},{6,5},{7,6},{0,7},{9,8},{10,9},{11,1... | collective-permute-start | bytes 393224 | tf_op jit(solution)/shard_map/ppermute | solution.py:832
  135.3 5.7 %collective-permute-start.16 = (f32[8,8,128]{2,1,0:T(8,128)S(1)}, f32[8,8,128]{2,1,0:T(8,128)S(1)}, u32[]{:S(2)}, u32[]{:S(2)}) collective-permute-start(f32[8,8,128]{2,1,0:T(8,128)S(1)} %get-tuple-element.79), channel_id=1, source_target_pairs={{0,8},{8,16},{16,24},{24,0},{1,9},{9,17},{17,25},{25,1},{2,10},{10... | collective-permute-start | bytes 98312 | tf_op jit(solution)/shard_map/ppermute | solution.py:832
  135.3 5.7 %collective-permute-start.17 = (f32[8,8,128]{2,1,0:T(8,128)S(1)}, f32[8,8,128]{2,1,0:T(8,128)S(1)}, u32[]{:S(2)}, u32[]{:S(2)}) collective-permute-start(f32[8,8,128]{2,1,0:T(8,128)S(1)} %get-tuple-element.80), channel_id=1, source_target_pairs={{8,0},{16,8},{24,16},{0,24},{9,1},{17,9},{25,17},{1,25},{10,2},{18... | collective-permute-start | bytes 98312 | tf_op jit(solution)/shard_map/ppermute | solution.py:832
  143.3 5.2 %collective-permute-start.18 = (f32[24,8,128]{2,1,0:T(8,128)}, f32[24,8,128]{2,1,0:T(8,128)S(1)}, u32[]{:S(2)}, u32[]{:S(2)}) collective-permute-start(f32[24,8,128]{2,1,0:T(8,128)} %get-tuple-element.81), channel_id=1, source_target_pairs={{0,1},{1,2},{2,3},{3,4},{4,5},{5,6},{6,7},{7,0},{8,9},{9,10},{10,1... | collective-permute-start | bytes 294920 | tf_op jit(solution)/shard_map/ppermute | solution.py:832
  143.3 5.2 %collective-permute-start.19 = (f32[24,8,128]{2,1,0:T(8,128)}, f32[24,8,128]{2,1,0:T(8,128)S(1)}, u32[]{:S(2)}, u32[]{:S(2)}) collective-permute-start(f32[24,8,128]{2,1,0:T(8,128)} %get-tuple-element.82), channel_id=1, source_target_pairs={{1,0},{2,1},{3,2},{4,3},{5,4},{6,5},{7,6},{0,7},{9,8},{10,9},{11,1... | collective-permute-start | bytes 294920 | tf_op jit(solution)/shard_map/ppermute | solution.py:832
  (46 other events, 215.3 us)

commit v3 on v2

--- a/solution.py
+++ b/solution.py
@@ -12,7 +12,9 @@
 LEVELS = 4
 LANES = 128
 FINE_HALO = 4
-FINE_LIMIT = 40
+START_LIMIT = 14
+FINISH_LIMIT = 8
+LEVEL_LIMIT = 12
 HALO = 8
 PRIMES = (65521, 65519)
 FACTORS = (40503, 30011)
@@ -128,7 +130,7 @@
         in_specs=specs or [VMEM] * len(args),
         out_specs=tuple([VMEM] * len(outs)),
         scratch_shapes=list(scratch),
-        compiler_params=pltpu.CompilerParams(vmem_limit_bytes=(limit or 24) * 1024 * 1024),
+        compiler_params=pltpu.CompilerParams(vmem_limit_bytes=(limit or 4) * 1024 * 1024),
         name=name,
     )(*args)
 
@@ -157,15 +159,9 @@
         out_shape=(f32(3 * w + w // 2, nj, nk),) * 2,
         in_specs=[first, last] * 4,
         out_specs=(whole, whole),
+        compiler_params=pltpu.CompilerParams(vmem_limit_bytes=8 * 1024 * 1024),
         name="pack_planes",
     )(*[a for a in arrays for _ in range(2)])
-
-
-def edge_specs(shape):
-    n, nj, nk = shape
-    low = pl.BlockSpec((n, 8, nk), lambda g: (0, 0, 0))
-    high = pl.BlockSpec((n, 8, nk), lambda g: (0, nj // 8 - 1, 0))
-    return [low, high]
 
 
 def pack_rows_fine(from_low, from_high, class_map, noise_seed, mean_shift, sample_field):
@@ -175,13 +171,12 @@
     arrays = (from_low, from_high, class_map, noise_seed, mean_shift, sample_field)
 
     def kernel(*refs):
-        to_next, to_previous = refs[12:]
-        even = checker((8, nk))
-        for out, ins, rows in (
-            (to_previous, refs[0:12:2], slice(0, w)),
-            (to_next, refs[1:12:2], slice(8 - w, 8)),
-        ):
-            low, high, own = ins[0], ins[1], ins[2:]
+        low, high, *own = refs[:6]
+        to_next, to_previous = refs[6:]
+        even = checker((nj, nk))
+        for out, start in ((to_previous, 0), (to_next, nj - w)):
+            rows = pl.ds(start, w)
+            mask = even[start : start + w]
             for a in range(3):
                 for e in range(w):
                     out[a * count + e] = low[a * w + e, rows]
@@ -197,19 +192,11 @@
                 out[base + q] = low[3 * w + q, rows]
                 out[base + (ni + w) // 2 + q] = high[3 * w + q, rows]
             for q in range(ni // 2):
-                v = jnp.where(even, own[3][2 * q + 1], own[3][2 * q])
-                out[base + w // 2 + q] = v[rows]
+                v = jnp.where(mask, own[3][2 * q + 1, rows], own[3][2 * q, rows])
+                out[base + w // 2 + q] = v
 
     total = 3 * count + count // 2
-    whole = pl.BlockSpec((total, w, nk), lambda g: (0, 0, 0))
-    return pl.pallas_call(
-        kernel,
-        grid=(1,),
-        out_shape=(f32(total, w, nk),) * 2,
-        in_specs=[s for a in arrays for s in edge_specs(a.shape)],
-        out_specs=(whole, whole),
-        name="pack_rows_fine",
-    )(*[a for a in arrays for _ in range(2)])
+    return call(kernel, "pack_rows_fine", [f32(total, w, nk)] * 2, arrays)
 
 
 def pack_rows(triples, w, name):
@@ -221,21 +208,12 @@
         to_next, to_previous = refs[-2:]
         at = 0
         for n, part in enumerate(parts):
-            size = part.shape[0]
-            for e in range(size):
-                to_previous[at + e] = refs[2 * n][e, slice(0, w)]
-                to_next[at + e] = refs[2 * n + 1][e, slice(8 - w, 8)]
+            size, nj, _ = part.shape
+            to_previous[pl.ds(at, size)] = refs[n][:, pl.ds(0, w)]
+            to_next[pl.ds(at, size)] = refs[n][:, pl.ds(nj - w, w)]
             at += size
 
-    whole = pl.BlockSpec((total, w, nk), lambda g: (0, 0, 0))
-    return pl.pallas_call(
-        kernel,
-        grid=(1,),
-        out_shape=(f32(total, w, nk),) * 2,
-        in_specs=[s for a in parts for s in edge_specs(a.shape)],
-        out_specs=(whole, whole),
-        name=name,
-    )(*[a for a in parts for _ in range(2)])
+    return call(kernel, name, [f32(total, w, nk)] * 2, parts)
 
 
 def pack_static_rows(static_planes, statics1, statics2):
@@ -562,7 +540,7 @@
     ]
     args = (*tables, class_map, mean_shift, sample_field, noise, *planes, *plane_noise, *rows)
     specs = [SMEM, SMEM] + [VMEM] * (len(args) - 2)
-    return call(kernel, "fine_start", outs, args, specs, scratch, FINE_LIMIT)
+    return call(kernel, "fine_start", outs, args, specs, scratch, START_LIMIT)
 
 
 def fine_finish(state, black, planes, rows):
@@ -625,7 +603,7 @@
         pltpu.VMEM((2, pairs, count_j, nk), jnp.float32),
     ] + restrict_scratch(ni, count_j, nk)
     args = (*state, black, *planes, *rows)
-    return call(kernel, "fine_finish", outs, args, None, scratch, FINE_LIMIT)
+    return call(kernel, "fine_finish", outs, args, None, scratch, FINISH_LIMIT)
 
 
 def level_sweeps(st, level, pairs, d_refs, m_ref, s_ref, r_ref, w_ref, x_refs, bounds, unroll):
@@ -678,7 +656,6 @@
     to_coarsest = level == LEVELS - 2
     plane_base = 0 if level == 1 else 3 * w
     row_base = 0 if level == 1 else 3 * (2 * ni + 2 * w)
-    members = lax.axis_size("gx") * lax.axis_size("gy")
 
     def kernel(*refs):
         refs = list(refs)
@@ -686,7 +663,7 @@
         sx_lo, sx_hi, sy_lo, sy_hi, bx_lo, bx_hi, by_lo, by_hi = refs[4:12]
         at = 12
         if to_coarsest:
-            tail_ref, spread = refs[12:14]
+            tail_ref, out = refs[12:14]
             at = 14
         else:
             out, to_next, to_previous = refs[12:15]
@@ -758,9 +735,7 @@
         if to_coarsest:
             lanes = nk // 4
             coarse = jnp.where(lax.broadcasted_iota(jnp.int32, coarse.shape, 2) < lanes, coarse, 0.0)
-            block = tail_ref[...] + pltpu.roll(coarse, 3 * lanes, 2)
-            for n in range(members):
-                spread[n] = block
+            out[...] = tail_ref[...] + pltpu.roll(coarse, 3 * lanes, 2)
         else:
             out[...] = coarse
             to_previous[...] = coarse[:w]
@@ -769,22 +744,23 @@
     args = [*statics, rhs, *static_planes, *static_rows, *rhs_planes, *rhs_rows]
     if to_coarsest:
         args.append(tail)
-        outs = [f32(members, ni // 2, nj // 2, LANES)]
+        outs = [f32(ni // 2, nj // 2, LANES)]
     else:
         outs = [f32(ni // 2, nj // 2, LANES)] + [f32(w, nj // 2, LANES)] * 2
     scratch = level_scratch(pairs, count_j, nk) + restrict_scratch(ni, count_j, nk)
-    return call(kernel, f"level_{level}", outs, args, None, scratch)
-
-
-def coarsest_level(blocks, lanes):
-    members, mi, mj, _ = blocks.shape
-    gx, gy = lax.axis_size("gx"), lax.axis_size("gy")
-    pairs = gx * mi // 2
-    nj = gy * mj
-    count_j = nj + 8
+    return call(kernel, f"level_{level}", outs, args, None, scratch, LEVEL_LIMIT)
+
+
+def coarsest_level(columns, reach, mi, lanes):
+    mj = columns[0].shape[1]
+    planes = columns[0].shape[0]
+    pairs = planes // 2
+    count_j = -(-len(columns) * mj // 8) * 8
     level = LEVELS - 1
 
-    def kernel(blocks_ref, out, d0, d1, m_ref, s_ref, r_ref, w_ref, x0, x1, t_ref):
+    def kernel(*refs):
+        blocks = refs[: len(columns)]
+        out, d0, d1, m_ref, s_ref, r_ref, w_ref, x0, x1, t_ref = refs[len(columns) :]
         d_refs, x_refs = (d0, d1), (x0, x1)
         shape = (count_j, LANES)
         st = Stencil(level, shape)
@@ -792,36 +768,42 @@
         for g in (0, pairs + 1):
             for ref in (*d_refs, *x_refs):
                 ref[g] = zero
-        for i in range(gx * mi):
-            for g in range(gy):
-                t_ref[i, pl.ds(g * mj, mj), :] = blocks_ref[i // mi * gy + g, i % mi]
-            t_ref[i, pl.ds(nj, 8), :] = jnp.zeros((8, LANES), jnp.float32)
+        t_ref[:, pl.ds(count_j - 8, 8), :] = jnp.zeros((planes, 8, LANES), jnp.float32)
+        for g, block in enumerate(blocks):
+            t_ref[:, pl.ds(g * mj, mj), :] = block[...]
         inside = st.lane < lanes
+        first_i = (lax.axis_index("gx") - reach) * mi
+        row = lax.broadcasted_iota(jnp.int32, shape, 0)
+        j = row + (lax.axis_index("gy") - reach) * mj
+        known = (j >= 0) & (j < lax.axis_size("gy") * mj) & (row < len(columns) * mj) & inside
+        known = known.astype(jnp.float32)
 
         def split(q):
+            i = first_i + 2 * q
+            here = ((i >= 0) & (i < lax.axis_size("gx") * mi)).astype(jnp.float32)
             both = st.whole(t_ref[2 * q], t_ref[2 * q + 1])
-            for a in range(4):
-                for c in range(2):
-                    v = both[c] if a == 0 else pltpu.roll(both[c], LANES - a * lanes, 1)
-                    v = jnp.where(inside, v, 0.0)
-                    if a == 0:
-                        d_refs[c][q + 1] = v
-                    else:
-                        (m_ref, s_ref, r_ref.at[0])[a - 1][c, q] = v
-
-        loop(0, pairs, split, 8)
-        level_sweeps(
-            st, level, pairs, d_refs, m_ref, s_ref, r_ref, w_ref, x_refs, lambda half: (0, pairs), 8
-        )
-        at_x, at_y = lax.axis_index("gx"), lax.axis_index("gy")
+            for c in range(2):
+                d_refs[c][q + 1] = both[c] * (known * here)
+                for a in range(1, 4):
+                    v = pltpu.roll(both[c], LANES - a * lanes, 1)
+                    (m_ref, s_ref, r_ref.at[0])[a - 1][c, q] = jnp.where(inside, v, 0.0)
+
+        loop(0, pairs, split, pairs)
+
+        def bounds(half):
+            more = 2 * SWEEPS - 1 - half
+            return (reach * mi - more) // 2, (reach * mi + mi - 1 + more) // 2 + 1
+
+        level_sweeps(st, level, pairs, d_refs, m_ref, s_ref, r_ref, w_ref, x_refs, bounds, pairs)
         for n in range(mi // 2):
-            p = at_x * (mi // 2) + n + 1
+            p = reach * mi // 2 + n + 1
             for k, v in enumerate(st.whole(x0[p], x1[p])):
-                out[2 * n + k] = pltpu.roll(v, count_j - at_y * mj, 0)[:mj, :lanes]
+                out[2 * n + k] = v[reach * mj : reach * mj + mj, :lanes]
 
     scratch = level_scratch(pairs, count_j, LANES)
-    scratch += [pltpu.VMEM((gx * mi, count_j, LANES), jnp.float32)]
-    (out,) = call(kernel, f"level_{level}", [f32(mi, mj, lanes)], (blocks,), None, scratch)
+    scratch += [pltpu.VMEM((planes, count_j, LANES), jnp.float32)]
+    outs = [f32(mi, mj, lanes)]
+    (out,) = call(kernel, f"level_{level}", outs, columns, None, scratch, LEVEL_LIMIT)
     return out
 
 
@@ -832,8 +814,13 @@
     return lax.ppermute(to_next, axis, up), lax.ppermute(to_previous, axis, down)
 
 
-def tied(first, *others):
-    return lax.optimization_barrier((first, *others))[0]
+def window(block, axis, reach):
+    size = lax.axis_size(axis)
+    got = {0: block}
+    for off in range(-reach, reach + 1):
+        if off % size not in got:
+            got[off % size] = lax.ppermute(block, axis, [(i, (i - off) % size) for i in range(size)])
+    return [got[off % size] for off in range(-reach, reach + 1)]
 
 
 def per_device(sample_field, mean_shift, class_map, noise_seed, diffusion_table, mass_table):
@@ -871,8 +858,12 @@
         )
         if not last:
             rhs, to_next, to_previous = got
-    blocks = lax.all_to_all(got[0], ("gx", "gy"), 0, 0, tiled=True)
-    return fine, coarsest_level(blocks, nk >> (LEVELS - 1))
+    (block,) = got
+    mi, mj, _ = block.shape
+    reach = -(-2 * SWEEPS // min(mi, mj))
+    column = jnp.concatenate(window(block, "gx", reach))
+    columns = window(column, "gy", reach)
+    return fine, coarsest_level(columns, reach, mi, nk >> (LEVELS - 1))
 
 
 def solution(mesh):

time: 176 us -> 135 us (0.77)
  local copies, waits for them, and re-layouts: 28.9 us -> 4.95 us
  Pallas kernels: 67.5 us -> 43.7 us
  blocking collectives: 16.6 us -> 0 us
  starting transfers between devices: 38.7 us -> 52.4 us
  waiting for transfers between devices: 22.6 us -> 32.8 us
    unnamed x100 -> x24, local copies, waits for them, and re-layouts: 28.9 us -> 4.94 us
    all_to_all x1 -> x0, blocking collectives: 16.6 us -> none  [per_device(): blocks = lax.all_to_all(got[0], ('gx', 'gy'), 0, 0, tiled=True)]
    pallas_call x9 -> x13, Pallas kernels: 57.1 us -> 43.7 us  [call(): pl.pallas_call(kernel, out_shape=tuple(outs), in_specs=specs or [VMEM] *...]
    ppermute x0 -> x7, starting transfers between devices: none -> 11 us  [window(): lax.ppermute(block, axis, [(i, (i - off) % size) for i in range(size)])]
    pallas_call x4 -> x0, Pallas kernels: 7.96 us -> none  [the longest x3 4.99 us: pack_rows(): pl.pallas_call(kernel, grid=(1,), out_shape=(f32(total, w, nk),) * 2, in_...]
    ppermute x0 -> x7, waiting for transfers between devices: none -> 3.79 us  [window(): lax.ppermute(block, axis, [(i, (i - off) % size) for i in range(size)])]
    ppermute x10, waiting for transfers between devices: 14.8 us -> 18.4 us  [both_ways(): lax.ppermute(to_next, axis, up)]
    ppermute x10, waiting for transfers between devices: 7.78 us -> 10.6 us  [both_ways(): lax.ppermute(to_previous, axis, down)]
  transfers between devices with their start and end apart: 20 -> 27, of which waited for: 10 -> 16; matrix products, arithmetic and copies ran while one was open for 0% -> 0% of each run, Pallas kernels for 28% -> 24%
where the time goes in v3:
time: 135 us
  starting transfers between devices  52.4 us (39%)
  Pallas kernels  43.7 us (32%)
  waiting for transfers between devices  32.8 us (24%)
  local copies, waits for them, and re-layouts  4.95 us (4%)
    pallas_call x13, Pallas kernels, call(): pl.pallas_call(kernel, out_shape=tuple(outs), in_specs=specs or [VMEM] *...  43.7 us
    ppermute x10, starting transfers between devices, both_ways(): lax.ppermute(to_previous, axis, down)  25.4 us
    ppermute x10, waiting for transfers between devices, both_ways(): lax.ppermute(to_next, axis, up)  18.4 us
    ppermute x10, starting transfers between devices, both_ways(): lax.ppermute(to_next, axis, up)  16 us
    ppermute x7, starting transfers between devices, window(): lax.ppermute(block, axis, [(i, (i - off) % size) for i in range(size)])  11 us
    ppermute x10, waiting for transfers between devices, both_ways(): lax.ppermute(to_previous, axis, down)  10.6 us
    unnamed x24, local copies, waits for them, and re-layouts  4.94 us
    ppermute x7, waiting for transfers between devices, window(): lax.ppermute(block, axis, [(i, (i - off) % size) for i in range(size)])  3.79 us
  transfers between devices with their start and end apart: 27, of which 16 were waited for; matrix products, arithmetic and copies ran while one was open for 0% of the time, Pallas kernels for 24%

profile of v3, /device:TPU:0, one launch (start us, length us, event | category | flops | bytes accessed | tf_op | source)
XLA Modules:
  0.0 134.7 jit_solution(2705347514591628581)
XLA Ops:
  5.6 5.0 %collective-permute-start = (f32[14,32,256]{2,1,0:T(8,128)S(1)}, f32[14,32,256]{2,1,0:T(8,128)S(1)}, u32[]{:S(2)}, u32[]{:S(2)}) collective-permute-start(f32[14,32,256]{2,1,0:T(8,128)S(1)} %get-tuple-element.43), channel_id=1, source_target_pairs={{0,8},{8,16},{16,24},{1,9},{9,17},{17,25},{2,10},{10,18},{18,26},{... | collective-permute-start | bytes 1376264 | tf_op jit(solution)/shard_map/ppermute | solution.py:814
  11.9 4.0 %coarse_statics.1 = (f32[16,16,128]{2,1,0:T(8,128)S(1)}, f32[16,16,128]{2,1,0:T(8,128)S(1)}, f32[16,16,128]{2,1,0:T(8,128)S(1)}, f32[8,8,128]{2,1,0:T(8,128)S(1)...) custom-call(f32[8]{0:T(128)S(1)} %copy-done.8, ...), custom_call_target="tpu_custom_call" | custom-call | tf_op jit(solution)/shard_map/coarse_statics/pallas_call | solution.py:127
  15.9 2.7 %collective-permute-start.8 = (f32[36,16,128]{2,1,0:T(8,128)S(1)}, f32[36,16,128]{2,1,0:T(8,128)S(1)}, u32[]{:S(2)}, u32[]{:S(2)}) collective-permute-start(f32[36,16,128]{2,1,0:T(8,128)S(1)} %get-tuple-element.45), channel_id=1, source_target_pairs={{0,8},{8,16},{16,24},{24,0},{1,9},{9,17},{17,25},{25,1},{2,10},{10... | collective-permute-start | bytes 884744 | tf_op jit(solution)/shard_map/ppermute | solution.py:814
  20.7 4.5 %own_noise.1.g_own = f32[3,2,16,32,256]{4,3,2,1,0:T(8,128)S(1)} custom-call(s32[32,32,256]{2,1,0:T(8,128)S(1)} %copy-done.2), custom_call_target="tpu_custom_call" | custom-call | tf_op jit(solution)/shard_map/own_noise/pallas_call | solution.py:127
  27.0 2.6 %collective-permute-start.3 = (f32[140,4,256]{2,1,0:T(4,128)S(1)}, f32[140,4,256]{2,1,0:T(4,128)S(1)}, u32[]{:S(2)}, u32[]{:S(2)}) collective-permute-start(f32[140,4,256]{2,1,0:T(4,128)S(1)} %get-tuple-element.51), channel_id=1, source_target_pairs={{1,0},{2,1},{3,2},{4,3},{5,4},{6,5},{7,6},{0,7},{9,8},{10,9},{11,1... | collective-permute-start | bytes 1720328 | tf_op jit(solution)/shard_map/ppermute | solution.py:814
  29.6 4.7 %collective-permute-done.8.low.refs_4_ = f32[36,16,128]{2,1,0:T(8,128)S(1)} collective-permute-done((f32[36,16,128]{2,1,0:T(8,128)S(1)}, f32[36,16,128]{2,1,0:T(8,128)S(1)}, u32[]{:S(2)}, u32[]{:S(2)}) %collective-permute-start.8) | collective-permute-done | bytes 294944 | tf_op jit(solution)/shard_map/ppermute | solution.py:814
  34.3 2.9 %collective-permute-done.9.high.refs_5_ = f32[36,16,128]{2,1,0:T(8,128)S(1)} collective-permute-done((f32[36,16,128]{2,1,0:T(8,128)S(1)}, f32[36,16,128]{2,1,0:T(8,128)S(1)}, u32[]{:S(2)}, u32[]{:S(2)}) %collective-permute-start.9) | collective-permute-done | bytes 294944 | tf_op jit(solution)/shard_map/ppermute | solution.py:814
  37.3 2.6 %collective-permute-start.11 = (f32[168,8,128]{2,1,0:T(8,128)S(1)}, f32[168,8,128]{2,1,0:T(8,128)S(1)}, u32[]{:S(2)}, u32[]{:S(2)}) collective-permute-start(f32[168,8,128]{2,1,0:T(8,128)S(1)} %get-tuple-element.73), channel_id=1, source_target_pairs={{1,0},{2,1},{3,2},{4,3},{5,4},{6,5},{7,6},{0,7},{9,8},{10,9},{11,1... | collective-permute-start | bytes 2064392 | tf_op jit(solution)/shard_map/ppermute | solution.py:814
  43.0 15.4 %fine_start.1 = (f32[6,2,20,40,256]{4,3,2,1,0:T(8,128)S(1)}, f32[2,20,40,256]{3,2,1,0:T(8,128)S(1)}, f32[2,20,40,256]{3,2,1,0:T(8,128)S(1)}, f32[2,20,40,256]{3,...) custom-call(f32[8]{0:T(128)S(1)} %copy-done.8, ...), custom_call_target="tpu_custom_call" | custom-call | tf_op jit(solution)/shard_map/fine_start/pallas_call | solution.py:127
  58.4 7.9 %collective-permute-start.4 = (f32[2,32,256]{2,1,0:T(8,128)S(1)}, f32[2,32,256]{2,1,0:T(8,128)S(1)}, u32[]{:S(2)}, u32[]{:S(2)}) collective-permute-start(f32[2,32,256]{2,1,0:T(8,128)S(1)} %get-tuple-element.59), channel_id=1, source_target_pairs={{0,8},{8,16},{16,24},{1,9},{9,17},{17,25},{2,10},{10,18},{18,26},{... | collective-permute-start | bytes 196616 | tf_op jit(solution)/shard_map/ppermute | solution.py:814
  68.6 4.5 %collective-permute-done.5.refs_2_.x_hi = f32[2,32,256]{2,1,0:T(8,128)S(1)} collective-permute-done((f32[2,32,256]{2,1,0:T(8,128)S(1)}, f32[2,32,256]{2,1,0:T(8,128)S(1)}, u32[]{:S(2)}, u32[]{:S(2)}) %collective-permute-start.5) | collective-permute-done | bytes 65568 | tf_op jit(solution)/shard_map/ppermute | solution.py:814
  73.2 2.6 %collective-permute-start.7 = (f32[20,4,256]{2,1,0:T(4,128)S(1)}, f32[20,4,256]{2,1,0:T(4,128)S(1)}, u32[]{:S(2)}, u32[]{:S(2)}) collective-permute-start(f32[20,4,256]{2,1,0:T(4,128)S(1)} %get-tuple-element.62), channel_id=1, source_target_pairs={{1,0},{2,1},{3,2},{4,3},{5,4},{6,5},{7,6},{0,7},{9,8},{10,9},{11,1... | collective-permute-start | bytes 245768 | tf_op jit(solution)/shard_map/ppermute | solution.py:814
  75.8 2.4 %collective-permute-done.6.y_lo = f32[20,4,256]{2,1,0:T(4,128)S(1)} collective-permute-done((f32[20,4,256]{2,1,0:T(4,128)S(1)}, f32[20,4,256]{2,1,0:T(4,128)S(1)}, u32[]{:S(2)}, u32[]{:S(2)}) %collective-permute-start.6) | collective-permute-done | bytes 81952 | tf_op jit(solution)/shard_map/ppermute | solution.py:814
  78.2 6.7 %fine_finish.1 = (f32[32,32,256]{2,1,0:T(8,128)}, f32[16,16,128]{2,1,0:T(8,128)S(1)}, f32[8,16,128]{2,1,0:T(8,128)S(1)}, f32[8,16,128]{2,1,0:T(8,128)S(1)}) custom-call(f32[6,2,20,40,256]{4,3,2,1,0:T(8,128)S(1)} %get-tuple-element.54.w_ref, f32[2,20,40,256]{3,2,1,0:T(8,128)S(1)} %get-tuple-element.55.r3_ref, ...), custom_call_target="tpu_custom_call" | custom-call | tf_op jit(solution)/shard_map/fine_finish/pallas_call | solution.py:127
  85.0 3.8 %collective-permute-start.13 = (f32[8,16,128]{2,1,0:T(8,128)S(1)}, f32[8,16,128]{2,1,0:T(8,128)S(1)}, u32[]{:S(2)}, u32[]{:S(2)}) collective-permute-start(f32[8,16,128]{2,1,0:T(8,128)S(1)} %get-tuple-element.75), channel_id=1, source_target_pairs={{8,0},{16,8},{24,16},{0,24},{9,1},{17,9},{25,17},{1,25},{10,2},{18... | collective-permute-start | bytes 196616 | tf_op jit(solution)/shard_map/ppermute | solution.py:814
  91.1 2.6 %collective-permute-start.15 = (f32[32,8,128]{2,1,0:T(8,128)S(1)}, f32[32,8,128]{2,1,0:T(8,128)S(1)}, u32[]{:S(2)}, u32[]{:S(2)}) collective-permute-start(f32[32,8,128]{2,1,0:T(8,128)S(1)} %get-tuple-element.77), channel_id=1, source_target_pairs={{1,0},{2,1},{3,2},{4,3},{5,4},{6,5},{7,6},{0,7},{9,8},{10,9},{11,1... | collective-permute-start | bytes 393224 | tf_op jit(solution)/shard_map/ppermute | solution.py:814
  93.7 3.7 %collective-permute-done.14.refs_10_ = f32[32,8,128]{2,1,0:T(8,128)S(1)} collective-permute-done((f32[32,8,128]{2,1,0:T(8,128)S(1)}, f32[32,8,128]{2,1,0:T(8,128)S(1)}, u32[]{:S(2)}, u32[]{:S(2)}) %collective-permute-start.14) | collective-permute-done | bytes 131104 | tf_op jit(solution)/shard_map/ppermute | solution.py:814
  97.4 5.7 %level_1.1 = (f32[8,8,128]{2,1,0:T(8,128)S(1)}, f32[8,8,128]{2,1,0:T(8,128)S(1)}, f32[8,8,128]{2,1,0:T(8,128)S(1)}) custom-call(f32[16,16,128]{2,1,0:T(8,128)S(1)} %get-tuple-element.67.refs_0_, f32[16,16,128]{2,1,0:T(8,128)S(1)} %get-tuple-element.68.refs_1_, f32[16,16,128]{2,1,0:T(8,128)S(1)} %get-tuple-element.69.refs_2_, ...), custom_call_target="tpu_custom_call" | custom-call | tf_op jit(solution)/shard_map/level_1/pallas_call | solution.py:127
  103.1 3.8 %collective-permute-start.17 = (f32[8,8,128]{2,1,0:T(8,128)S(1)}, f32[8,8,128]{2,1,0:T(8,128)S(1)}, u32[]{:S(2)}, u32[]{:S(2)}) collective-permute-start(f32[8,8,128]{2,1,0:T(8,128)S(1)} %get-tuple-element.80), channel_id=1, source_target_pairs={{8,0},{16,8},{24,16},{0,24},{9,1},{17,9},{25,17},{1,25},{10,2},{18... | collective-permute-start | bytes 98312 | tf_op jit(solution)/shard_map/ppermute | solution.py:814
  108.9 2.6 %collective-permute-start.19 = (f32[24,8,128]{2,1,0:T(8,128)S(1)}, f32[24,8,128]{2,1,0:T(8,128)S(1)}, u32[]{:S(2)}, u32[]{:S(2)}) collective-permute-start(f32[24,8,128]{2,1,0:T(8,128)S(1)} %get-tuple-element.82), channel_id=1, source_target_pairs={{1,0},{2,1},{3,2},{4,3},{5,4},{6,5},{7,6},{0,7},{9,8},{10,9},{11,1... | collective-permute-start | bytes 294920 | tf_op jit(solution)/shard_map/ppermute | solution.py:814
  111.6 2.3 %collective-permute-done.18.refs_10_ = f32[24,8,128]{2,1,0:T(8,128)S(1)} collective-permute-done((f32[24,8,128]{2,1,0:T(8,128)S(1)}, f32[24,8,128]{2,1,0:T(8,128)S(1)}, u32[]{:S(2)}, u32[]{:S(2)}) %collective-permute-start.18) | collective-permute-done | bytes 98336 | tf_op jit(solution)/shard_map/ppermute | solution.py:814
  113.9 3.3 %level_2.1 = f32[4,4,128]{2,1,0:T(4,128)S(1)} custom-call(f32[8,8,128]{2,1,0:T(8,128)S(1)} %get-tuple-element.64.refs_3_.refs_0_, f32[8,8,128]{2,1,0:T(8,128)S(1)} %get-tuple-element.65.refs_4_.refs_1_, f32[8,8,128]{2,1,0:T(8,128)S(1)} %get-tuple-element.66.refs_5_.refs_2_, f32[8,8,128]{2,1,0:T(8,128)S(1)} %get-tuple-element.78.refs_1_.refs_3_, ...), custom_call_target="tpu_custom_call" | custom-call | tf_op jit(solution)/shard_map/level_2/pallas_call | solution.py:127
  117.2 2.5 %collective-permute-start.20 = (f32[4,4,128]{2,1,0:T(4,128)S(1)}, f32[4,4,128]{2,1,0:T(4,128)S(1)}, u32[]{:S(2)}, u32[]{:S(2)}) collective-permute-start(f32[4,4,128]{2,1,0:T(4,128)S(1)} %level_2.1), channel_id=1, source_target_pairs={{0,16},{8,24},{16,0},{24,8},{1,17},{9,25},{17,1},{25,9},{2,18},{10... | collective-permute-start | bytes 24584 | tf_op jit(solution)/shard_map/ppermute | solution.py:822
  132.0 2.7 %level_3.1 = f32[4,4,32]{2,1,0:T(4,128)} custom-call(f32[20,4,128]{2,1,0:T(4,128)S(1)} %collective-permute-done.23.refs_0_, f32[20,4,128]{2,1,0:T(4,128)S(1)} %collective-permute-done.24.refs_1_, f32[20,4,128]{2,1,0:T(4,128)S(1)} %constant_dynamic-update-slice_fusion.refs_2_, f32[20,4,128]{2,1,0:T(4,128)S(1)} %collective-permute-done.25.refs_3_, ...), custom_call_target="tpu_custom_call" | custom-call | tf_op jit(solution)/shard_map/level_3/pallas_call | solution.py:127
  (69 shorter events, 32.5 us)
Async XLA Ops:
  5.6 19.5 %collective-permute-start = (f32[14,32,256]{2,1,0:T(8,128)S(1)}, f32[14,32,256]{2,1,0:T(8,128)S(1)}, u32[]{:S(2)}, u32[]{:S(2)}) collective-permute-start(f32[14,32,256]{2,1,0:T(8,128)S(1)} %get-tuple-element.43), channel_id=1, source_target_pairs={{0,8},{8,16},{16,24},{1,9},{9,17},{17,25},{2,10},{10,18},{18,26},{... | collective-permute-start | bytes 1376264 | tf_op jit(solution)/shard_map/ppermute | solution.py:814
  10.6 16.1 %collective-permute-start.1 = (f32[14,32,256]{2,1,0:T(8,128)S(1)}, f32[14,32,256]{2,1,0:T(8,128)S(1)}, u32[]{:S(2)}, u32[]{:S(2)}) collective-permute-start(f32[14,32,256]{2,1,0:T(8,128)S(1)} %get-tuple-element.44), channel_id=1, source_target_pairs={{8,0},{16,8},{24,16},{9,1},{17,9},{25,17},{10,2},{18,10},{26,18},{... | collective-permute-start | bytes 1376264 | tf_op jit(solution)/shard_map/ppermute | solution.py:814
  15.9 18.3 %collective-permute-start.8 = (f32[36,16,128]{2,1,0:T(8,128)S(1)}, f32[36,16,128]{2,1,0:T(8,128)S(1)}, u32[]{:S(2)}, u32[]{:S(2)}) collective-permute-start(f32[36,16,128]{2,1,0:T(8,128)S(1)} %get-tuple-element.45), channel_id=1, source_target_pairs={{0,8},{8,16},{16,24},{24,0},{1,9},{9,17},{17,25},{25,1},{2,10},{10... | collective-permute-start | bytes 884744 | tf_op jit(solution)/shard_map/ppermute | solution.py:814
  18.6 18.5 %collective-permute-start.9 = (f32[36,16,128]{2,1,0:T(8,128)S(1)}, f32[36,16,128]{2,1,0:T(8,128)S(1)}, u32[]{:S(2)}, u32[]{:S(2)}) collective-permute-start(f32[36,16,128]{2,1,0:T(8,128)S(1)} %get-tuple-element.71), channel_id=1, source_target_pairs={{8,0},{16,8},{24,16},{0,24},{9,1},{17,9},{25,17},{1,25},{10,2},{18... | collective-permute-start | bytes 884744 | tf_op jit(solution)/shard_map/ppermute | solution.py:814
  26.9 14.4 %collective-permute-start.2 = (f32[140,4,256]{2,1,0:T(4,128)S(1)}, f32[140,4,256]{2,1,0:T(4,128)S(1)}, u32[]{:S(2)}, u32[]{:S(2)}) collective-permute-start(f32[140,4,256]{2,1,0:T(4,128)S(1)} %get-tuple-element.50), channel_id=1, source_target_pairs={{0,1},{1,2},{2,3},{3,4},{4,5},{5,6},{6,7},{7,0},{8,9},{9,10},{10,1... | collective-permute-start | bytes 1720328 | tf_op jit(solution)/shard_map/ppermute | solution.py:814
  27.0 16.0 %collective-permute-start.3 = (f32[140,4,256]{2,1,0:T(4,128)S(1)}, f32[140,4,256]{2,1,0:T(4,128)S(1)}, u32[]{:S(2)}, u32[]{:S(2)}) collective-permute-start(f32[140,4,256]{2,1,0:T(4,128)S(1)} %get-tuple-element.51), channel_id=1, source_target_pairs={{1,0},{2,1},{3,2},{4,3},{5,4},{6,5},{7,6},{0,7},{9,8},{10,9},{11,1... | collective-permute-start | bytes 1720328 | tf_op jit(solution)/shard_map/ppermute | solution.py:814
  37.2 56.5 %collective-permute-start.10 = (f32[168,8,128]{2,1,0:T(8,128)S(1)}, f32[168,8,128]{2,1,0:T(8,128)S(1)}, u32[]{:S(2)}, u32[]{:S(2)}) collective-permute-start(f32[168,8,128]{2,1,0:T(8,128)S(1)} %get-tuple-element.72), channel_id=1, source_target_pairs={{0,1},{1,2},{2,3},{3,4},{4,5},{5,6},{6,7},{7,0},{8,9},{9,10},{10,1... | collective-permute-start | bytes 2064392 | tf_op jit(solution)/shard_map/ppermute | solution.py:814
  37.3 56.4 %collective-permute-start.11 = (f32[168,8,128]{2,1,0:T(8,128)S(1)}, f32[168,8,128]{2,1,0:T(8,128)S(1)}, u32[]{:S(2)}, u32[]{:S(2)}) collective-permute-start(f32[168,8,128]{2,1,0:T(8,128)S(1)} %get-tuple-element.73), channel_id=1, source_target_pairs={{1,0},{2,1},{3,2},{4,3},{5,4},{6,5},{7,6},{0,7},{9,8},{10,9},{11,1... | collective-permute-start | bytes 2064392 | tf_op jit(solution)/shard_map/ppermute | solution.py:814
  58.4 10.2 %collective-permute-start.4 = (f32[2,32,256]{2,1,0:T(8,128)S(1)}, f32[2,32,256]{2,1,0:T(8,128)S(1)}, u32[]{:S(2)}, u32[]{:S(2)}) collective-permute-start(f32[2,32,256]{2,1,0:T(8,128)S(1)} %get-tuple-element.59), channel_id=1, source_target_pairs={{0,8},{8,16},{16,24},{1,9},{9,17},{17,25},{2,10},{10,18},{18,26},{... | collective-permute-start | bytes 196616 | tf_op jit(solution)/shard_map/ppermute | solution.py:814
  66.3 6.8 %collective-permute-start.5 = (f32[2,32,256]{2,1,0:T(8,128)S(1)}, f32[2,32,256]{2,1,0:T(8,128)S(1)}, u32[]{:S(2)}, u32[]{:S(2)}) collective-permute-start(f32[2,32,256]{2,1,0:T(8,128)S(1)} %get-tuple-element.60), channel_id=1, source_target_pairs={{8,0},{16,8},{24,16},{9,1},{17,9},{25,17},{10,2},{18,10},{26,18},{... | collective-permute-start | bytes 196616 | tf_op jit(solution)/shard_map/ppermute | solution.py:814
  73.1 5.1 %collective-permute-start.6 = (f32[20,4,256]{2,1,0:T(4,128)S(1)}, f32[20,4,256]{2,1,0:T(4,128)S(1)}, u32[]{:S(2)}, u32[]{:S(2)}) collective-permute-start(f32[20,4,256]{2,1,0:T(4,128)S(1)} %get-tuple-element.61), channel_id=1, source_target_pairs={{0,1},{1,2},{2,3},{3,4},{4,5},{5,6},{6,7},{7,0},{8,9},{9,10},{10,1... | collective-permute-start | bytes 245768 | tf_op jit(solution)/shard_map/ppermute | solution.py:814
  73.2 5.0 %collective-permute-start.7 = (f32[20,4,256]{2,1,0:T(4,128)S(1)}, f32[20,4,256]{2,1,0:T(4,128)S(1)}, u32[]{:S(2)}, u32[]{:S(2)}) collective-permute-start(f32[20,4,256]{2,1,0:T(4,128)S(1)} %get-tuple-element.62), channel_id=1, source_target_pairs={{1,0},{2,1},{3,2},{4,3},{5,4},{6,5},{7,6},{0,7},{9,8},{10,9},{11,1... | collective-permute-start | bytes 245768 | tf_op jit(solution)/shard_map/ppermute | solution.py:814
  84.9 6.1 %collective-permute-start.12 = (f32[8,16,128]{2,1,0:T(8,128)S(1)}, f32[8,16,128]{2,1,0:T(8,128)S(1)}, u32[]{:S(2)}, u32[]{:S(2)}) collective-permute-start(f32[8,16,128]{2,1,0:T(8,128)S(1)} %get-tuple-element.74), channel_id=1, source_target_pairs={{0,8},{8,16},{16,24},{24,0},{1,9},{9,17},{17,25},{25,1},{2,10},{10... | collective-permute-start | bytes 196616 | tf_op jit(solution)/shard_map/ppermute | solution.py:814
  85.0 6.0 %collective-permute-start.13 = (f32[8,16,128]{2,1,0:T(8,128)S(1)}, f32[8,16,128]{2,1,0:T(8,128)S(1)}, u32[]{:S(2)}, u32[]{:S(2)}) collective-permute-start(f32[8,16,128]{2,1,0:T(8,128)S(1)} %get-tuple-element.75), channel_id=1, source_target_pairs={{8,0},{16,8},{24,16},{0,24},{9,1},{17,9},{25,17},{1,25},{10,2},{18... | collective-permute-start | bytes 196616 | tf_op jit(solution)/shard_map/ppermute | solution.py:814
  91.0 6.4 %collective-permute-start.14 = (f32[32,8,128]{2,1,0:T(8,128)S(1)}, f32[32,8,128]{2,1,0:T(8,128)S(1)}, u32[]{:S(2)}, u32[]{:S(2)}) collective-permute-start(f32[32,8,128]{2,1,0:T(8,128)S(1)} %get-tuple-element.76), channel_id=1, source_target_pairs={{0,1},{1,2},{2,3},{3,4},{4,5},{5,6},{6,7},{7,0},{8,9},{9,10},{10,1... | collective-permute-start | bytes 393224 | tf_op jit(solution)/shard_map/ppermute | solution.py:814
  91.1 6.3 %collective-permute-start.15 = (f32[32,8,128]{2,1,0:T(8,128)S(1)}, f32[32,8,128]{2,1,0:T(8,128)S(1)}, u32[]{:S(2)}, u32[]{:S(2)}) collective-permute-start(f32[32,8,128]{2,1,0:T(8,128)S(1)} %get-tuple-element.77), channel_id=1, source_target_pairs={{1,0},{2,1},{3,2},{4,3},{5,4},{6,5},{7,6},{0,7},{9,8},{10,9},{11,1... | collective-permute-start | bytes 393224 | tf_op jit(solution)/shard_map/ppermute | solution.py:814
  103.1 5.8 %collective-permute-start.16 = (f32[8,8,128]{2,1,0:T(8,128)S(1)}, f32[8,8,128]{2,1,0:T(8,128)S(1)}, u32[]{:S(2)}, u32[]{:S(2)}) collective-permute-start(f32[8,8,128]{2,1,0:T(8,128)S(1)} %get-tuple-element.79), channel_id=1, source_target_pairs={{0,8},{8,16},{16,24},{24,0},{1,9},{9,17},{17,25},{25,1},{2,10},{10... | collective-permute-start | bytes 98312 | tf_op jit(solution)/shard_map/ppermute | solution.py:814
  103.1 5.7 %collective-permute-start.17 = (f32[8,8,128]{2,1,0:T(8,128)S(1)}, f32[8,8,128]{2,1,0:T(8,128)S(1)}, u32[]{:S(2)}, u32[]{:S(2)}) collective-permute-start(f32[8,8,128]{2,1,0:T(8,128)S(1)} %get-tuple-element.80), channel_id=1, source_target_pairs={{8,0},{16,8},{24,16},{0,24},{9,1},{17,9},{25,17},{1,25},{10,2},{18... | collective-permute-start | bytes 98312 | tf_op jit(solution)/shard_map/ppermute | solution.py:814
  108.9 5.0 %collective-permute-start.18 = (f32[24,8,128]{2,1,0:T(8,128)S(1)}, f32[24,8,128]{2,1,0:T(8,128)S(1)}, u32[]{:S(2)}, u32[]{:S(2)}) collective-permute-start(f32[24,8,128]{2,1,0:T(8,128)S(1)} %get-tuple-element.81), channel_id=1, source_target_pairs={{0,1},{1,2},{2,3},{3,4},{4,5},{5,6},{6,7},{7,0},{8,9},{9,10},{10,1... | collective-permute-start | bytes 294920 | tf_op jit(solution)/shard_map/ppermute | solution.py:814
  108.9 4.9 %collective-permute-start.19 = (f32[24,8,128]{2,1,0:T(8,128)S(1)}, f32[24,8,128]{2,1,0:T(8,128)S(1)}, u32[]{:S(2)}, u32[]{:S(2)}) collective-permute-start(f32[24,8,128]{2,1,0:T(8,128)S(1)} %get-tuple-element.82), channel_id=1, source_target_pairs={{1,0},{2,1},{3,2},{4,3},{5,4},{6,5},{7,6},{0,7},{9,8},{10,9},{11,1... | collective-permute-start | bytes 294920 | tf_op jit(solution)/shard_map/ppermute | solution.py:814
  117.2 6.3 %collective-permute-start.20 = (f32[4,4,128]{2,1,0:T(4,128)S(1)}, f32[4,4,128]{2,1,0:T(4,128)S(1)}, u32[]{:S(2)}, u32[]{:S(2)}) collective-permute-start(f32[4,4,128]{2,1,0:T(4,128)S(1)} %level_2.1), channel_id=1, source_target_pairs={{0,16},{8,24},{16,0},{24,8},{1,17},{9,25},{17,1},{25,9},{2,18},{10... | collective-permute-start | bytes 24584 | tf_op jit(solution)/shard_map/ppermute | solution.py:822
  119.6 5.4 %collective-permute-start.21 = (f32[4,4,128]{2,1,0:T(4,128)S(1)}, f32[4,4,128]{2,1,0:T(4,128)S(1)}, u32[]{:S(2)}, u32[]{:S(2)}) collective-permute-start(f32[4,4,128]{2,1,0:T(4,128)S(1)} %level_2.1), channel_id=1, source_target_pairs={{0,8},{8,16},{16,24},{24,0},{1,9},{9,17},{17,25},{25,1},{2,10},{10... | collective-permute-start | bytes 24584 | tf_op jit(solution)/shard_map/ppermute | solution.py:822
  125.2 4.9 %collective-permute-start.23 = (f32[20,4,128]{2,1,0:T(4,128)S(1)}, f32[20,4,128]{2,1,0:T(4,128)S(1)}, u32[]{:S(2)}, u32[]{:S(2)}) collective-permute-start(f32[20,4,128]{2,1,0:T(4,128)S(1)} %constant_dynamic-update-slice_fusion.refs_2_), channel_id=1, source_target_pairs={{0,2},{1,3},{2,4},{3,5},{4,6},{5,7},{6,0},{7,1},{8,10},{9,11},{10,... | collective-permute-start | bytes 122888 | tf_op jit(solution)/shard_map/ppermute | solution.py:822
  125.2 4.9 %collective-permute-start.24 = (f32[20,4,128]{2,1,0:T(4,128)S(1)}, f32[20,4,128]{2,1,0:T(4,128)S(1)}, u32[]{:S(2)}, u32[]{:S(2)}) collective-permute-start(f32[20,4,128]{2,1,0:T(4,128)S(1)} %constant_dynamic-update-slice_fusion.refs_2_), channel_id=1, source_target_pairs={{0,1},{1,2},{2,3},{3,4},{4,5},{5,6},{6,7},{7,0},{8,9},{9,10},{10,1... | collective-permute-start | bytes 122888 | tf_op jit(solution)/shard_map/ppermute | solution.py:822
  (13 other events, 78.0 us)

commit v4 on v3

--- a/solution.py
+++ b/solution.py
@@ -12,9 +12,11 @@
 LEVELS = 4
 LANES = 128
 FINE_HALO = 4
+PACK_LIMIT = 58
 START_LIMIT = 14
 FINISH_LIMIT = 8
 LEVEL_LIMIT = 12
+UNROLL = 4
 HALO = 8
 PRIMES = (65521, 65519)
 FACTORS = (40503, 30011)
@@ -141,27 +143,33 @@
     arrays = (class_map, noise_seed, mean_shift, sample_field)
 
     def kernel(*refs):
+        sources, outs, (whole_ref, real_ref, sems) = refs[:4], refs[4:6], refs[6:]
+        copies = []
+        for side, start in enumerate((ni - w, 0)):
+            for a, source in enumerate(sources):
+                target = (whole_ref, real_ref)[a // 2].at[side, a % 2]
+                copy = pltpu.make_async_copy(source.at[pl.ds(start, w)], target, sems.at[side, a])
+                copy.start()
+                copies.append(copy)
+        for copy in copies:
+            copy.wait()
         even = checker((nj, nk))
-        for out, ins in ((refs[9], refs[0:8:2]), (refs[8], refs[1:8:2])):
+        for side, out in enumerate(outs):
             for e in range(w):
-                out[e] = (ins[0][e] + 1).astype(jnp.float32)
-                out[w + e] = ins[1][e].astype(jnp.float32)
-                out[2 * w + e] = ins[2][e]
+                out[e] = (whole_ref[side, 0, e] + 1).astype(jnp.float32)
+                out[w + e] = whole_ref[side, 1, e].astype(jnp.float32)
+                out[2 * w + e] = real_ref[side, 0, e]
             for q in range(w // 2):
-                out[3 * w + q] = jnp.where(even, ins[3][2 * q + 1], ins[3][2 * q])
-
-    first = pl.BlockSpec((w, nj, nk), lambda n: (0, 0, 0))
-    last = pl.BlockSpec((w, nj, nk), lambda n: (ni // w - 1, 0, 0))
-    whole = pl.BlockSpec((3 * w + w // 2, nj, nk), lambda n: (0, 0, 0))
-    return pl.pallas_call(
-        kernel,
-        grid=(1,),
-        out_shape=(f32(3 * w + w // 2, nj, nk),) * 2,
-        in_specs=[first, last] * 4,
-        out_specs=(whole, whole),
-        compiler_params=pltpu.CompilerParams(vmem_limit_bytes=8 * 1024 * 1024),
-        name="pack_planes",
-    )(*[a for a in arrays for _ in range(2)])
+                out[3 * w + q] = jnp.where(even, real_ref[side, 1, 2 * q + 1], real_ref[side, 1, 2 * q])
+
+    scratch = [
+        pltpu.VMEM((2, 2, w, nj, nk), jnp.int32),
+        pltpu.VMEM((2, 2, w, nj, nk), jnp.float32),
+        pltpu.SemaphoreType.DMA((2, 4)),
+    ]
+    outs = [f32(3 * w + w // 2, nj, nk)] * 2
+    specs = [pl.BlockSpec(memory_space=pltpu.HBM)] * 4
+    return call(kernel, "pack_planes", outs, arrays, specs, scratch, PACK_LIMIT)
 
 
 def pack_rows_fine(from_low, from_high, class_map, noise_seed, mean_shift, sample_field):
@@ -510,7 +518,7 @@
                 r_ref[0, c, q] = b + r_ref[1, c, q] * root
                 r_ref[1, c, q] = b + r_ref[2, c, q] * root
 
-        loop(0, pairs, prepare)
+        loop(0, pairs, prepare, 2)
 
         for half in range(2 * SWEEPS - 2):
             t, c = half // 2, half % 2
@@ -518,7 +526,7 @@
             def update(q, t=t, c=c):
                 x_refs[c][q + 1] = r_ref[t, c, q] + st.gathered(x_refs, w_ref, c, q)
 
-            loop((half + 1) // 2, pairs - (half + 1) // 2, update)
+            loop((half + 1) // 2, pairs - (half + 1) // 2, update, UNROLL)
 
         def write(q):
             xb_ref[q] = x1[q + h + 1, :nj]
@@ -558,17 +566,19 @@
         shape = (count_j, nk)
         st = Stencil(0, shape)
         has_low, has_high = has_neighbours("gy")
+        has_x = has_neighbours("gx")
         zero = jnp.zeros(shape, jnp.float32)
         for g in (0, pairs + 1):
             for ref in x_refs:
                 ref[g] = zero
 
-        def join(q, mid):
-            x1[q + 1] = jnp.concatenate([mid, y_hi[q] * has_high, y_lo[q] * has_low], axis=0)
+        def join(q, mid, here=1.0):
+            hi, lo = y_hi[q] * (has_high * here), y_lo[q] * (has_low * here)
+            x1[q + 1] = jnp.concatenate([mid * here, hi, lo], axis=0)
 
         for q in range(h):
-            join(q, x_lo[q])
-            join(h + ni // 2 + q, x_hi[q])
+            join(q, x_lo[q], has_x[0])
+            join(h + ni // 2 + q, x_hi[q], has_x[1])
         loop(0, ni // 2, lambda q: join(h + q, xb_ref[q]), 4)
 
         for c, (start, stop) in enumerate(((0, pairs - 1), (1, pairs - 1))):
@@ -576,14 +586,14 @@
             def update(q, c=c):
                 x_refs[c][q + 1] = r3_ref[c, q] + st.gathered(x_refs, w_ref, c, q)
 
-            loop(start, stop, update)
+            loop(start, stop, update, UNROLL)
 
         def residual(q):
             red = r3_ref[0, q] - n3_ref[0, q] + st.gathered(x_refs, w_ref, 0, q) - x0[q + 1]
             res_ref[0, q] = m_ref[0, q] * red
             res_ref[1, q] = -m_ref[1, q] * n3_ref[1, q]
 
-        loop(h - 1, h + ni // 2, residual)
+        loop(h - 1, h + ni // 2, residual, UNROLL)
 
         def write(q):
             both = st.whole(x0[q + h + 1], x1[q + h + 1])
@@ -833,19 +843,28 @@
     statics1, statics2, static_next, static_previous, tail = coarse_statics(
         tables, class_map, noise_seed
     )
-    planes = lax.optimization_barrier((*planes, noise, static_next))[:2]
+    *planes, noise, static_next, static_previous = lax.optimization_barrier(
+        (*planes, noise, static_next, static_previous)
+    )
+    static_planes = both_ways(static_next, static_previous, "gx", False)
 
     rows = both_ways(*pack_rows_fine(*planes, *arrays), "gy")
     plane_noise = halo_noise(*planes)
-    rows = lax.optimization_barrier((*rows, *plane_noise))[:2]
+    *rows, low_noise, high_noise, static_low, static_high = lax.optimization_barrier(
+        (*rows, *plane_noise, *static_planes)
+    )
+    static_planes = (static_low, static_high)
+    static_next, static_previous = pack_static_rows(static_planes, statics1, statics2)
+    *rows, static_next, static_previous = lax.optimization_barrier(
+        (*rows, static_next, static_previous)
+    )
+    static_rows = both_ways(static_next, static_previous, "gy")
 
     *state, black, to_next, to_previous = fine_start(
-        tables, (class_map, mean_shift, sample_field), noise, planes, plane_noise, rows
+        tables, (class_map, mean_shift, sample_field), noise, planes, (low_noise, high_noise), rows
     )
-    planes = both_ways(to_next, to_previous, "gx", False)
-    static_planes = both_ways(static_next, static_previous, "gx")
+    planes = both_ways(to_next, to_previous, "gx")
     rows = both_ways(*pack_rows([(planes[0], black, planes[1])], FINE_HALO, "pack_rows_black"), "gy")
-    static_rows = both_ways(*pack_static_rows(static_planes, statics1, statics2), "gy")
 
     fine, rhs, to_next, to_previous = fine_finish(state, black, planes, rows)
     for level in range(1, LEVELS - 1):

time: 135 us -> 119 us (0.88)
  starting transfers between devices: 52.4 us -> 43.4 us
  local copies, waits for them, and re-layouts: 4.95 us -> 0.07 us
  Pallas kernels: 43.7 us -> 39.1 us
  waiting for transfers between devices: 32.8 us -> 35.4 us
    unnamed x24 -> x16, local copies, waits for them, and re-layouts: 4.94 us -> 0.06 us
    ppermute x7, waiting for transfers between devices: 3.79 us -> 8.47 us  [window(): lax.ppermute(block, axis, [(i, (i - off) % size) for i in range(size)])]
    pallas_call x13 -> x14, Pallas kernels: 43.7 us -> 39.1 us  [call(): pl.pallas_call(kernel, out_shape=tuple(outs), in_specs=specs or [VMEM] *...]
    ppermute x10, starting transfers between devices: 16 us -> 12.1 us  [both_ways(): lax.ppermute(to_next, axis, up)]
    ppermute x7, starting transfers between devices: 11 us -> 7.19 us  [window(): lax.ppermute(block, axis, [(i, (i - off) % size) for i in range(size)])]
    ppermute x10, waiting for transfers between devices: 10.6 us -> 8.72 us  [both_ways(): lax.ppermute(to_previous, axis, down)]
  transfers between devices with their start and end apart: 27 -> 27, of which waited for: 16 -> 16; matrix products, arithmetic and copies ran while one was open for 0% -> 0% of each run, Pallas kernels for 24% -> 21%
where the time goes in v4:
time: 119 us
  starting transfers between devices  43.4 us (36%)
  Pallas kernels  39.1 us (33%)
  waiting for transfers between devices  35.4 us (30%)
    pallas_call x14, Pallas kernels, call(): pl.pallas_call(kernel, out_shape=tuple(outs), in_specs=specs or [VMEM] *...  39.1 us
    ppermute x10, starting transfers between devices, both_ways(): lax.ppermute(to_previous, axis, down)  24.1 us
    ppermute x10, waiting for transfers between devices, both_ways(): lax.ppermute(to_next, axis, up)  18.2 us
    ppermute x10, starting transfers between devices, both_ways(): lax.ppermute(to_next, axis, up)  12.1 us
    ppermute x10, waiting for transfers between devices, both_ways(): lax.ppermute(to_previous, axis, down)  8.72 us
    ppermute x7, waiting for transfers between devices, window(): lax.ppermute(block, axis, [(i, (i - off) % size) for i in range(size)])  8.47 us
    ppermute x7, starting transfers between devices, window(): lax.ppermute(block, axis, [(i, (i - off) % size) for i in range(size)])  7.19 us
  transfers between devices with their start and end apart: 27, of which 16 were waited for; matrix products, arithmetic and copies ran while one was open for 0% of the time, Pallas kernels for 21%

profile of v4, /device:TPU:0, one launch (start us, length us, event | category | flops | bytes accessed | tf_op | source)
XLA Modules:
  0.0 118.9 jit_solution(8997227737579009364)
XLA Ops:
  0.6 2.4 %pack_planes.1 = (f32[14,32,256]{2,1,0:T(8,128)}, f32[14,32,256]{2,1,0:T(8,128)}) custom-call(s32[32,32,256]{2,1,0:T(8,128)} %cls_ref.3, s32[32,32,256]{2,1,0:T(8,128)} %refs_3_.3, f32[32,32,256]{2,1,0:T(8,128)} %b_ref.1, f32[32,32,256]{2,1,0:T(8,128)} %sample.1), custom_call_target="tpu_custom_call" | custom-call | tf_op jit(solution)/shard_map/pack_planes/pallas_call | solution.py:129
  3.0 5.0 %collective-permute-start = (f32[14,32,256]{2,1,0:T(8,128)}, f32[14,32,256]{2,1,0:T(8,128)S(1)}, u32[]{:S(2)}, u32[]{:S(2)}) collective-permute-start(f32[14,32,256]{2,1,0:T(8,128)} %get-tuple-element.54), channel_id=1, source_target_pairs={{0,8},{8,16},{16,24},{1,9},{9,17},{17,25},{2,10},{10,18},{18,26},{... | collective-permute-start | bytes 1376264 | tf_op jit(solution)/shard_map/ppermute | solution.py:824
  9.5 4.5 %own_noise.1.g_own = f32[3,2,16,32,256]{4,3,2,1,0:T(8,128)S(1)} custom-call(s32[32,32,256]{2,1,0:T(8,128)S(1)} %copy-done.1), custom_call_target="tpu_custom_call" | custom-call | tf_op jit(solution)/shard_map/own_noise/pallas_call | solution.py:129
  14.0 4.0 %coarse_statics.1 = (f32[16,16,128]{2,1,0:T(8,128)S(1)}, f32[16,16,128]{2,1,0:T(8,128)S(1)}, f32[16,16,128]{2,1,0:T(8,128)S(1)}, f32[8,8,128]{2,1,0:T(8,128)S(1)...) custom-call(f32[8]{0:T(128)S(1)} %copy-done.4, ...), custom_call_target="tpu_custom_call" | custom-call | tf_op jit(solution)/shard_map/coarse_statics/pallas_call | solution.py:129
  18.1 4.2 %collective-permute-done.1.refs_1_.high.x_hi = f32[14,32,256]{2,1,0:T(8,128)S(1)} collective-permute-done((f32[14,32,256]{2,1,0:T(8,128)}, f32[14,32,256]{2,1,0:T(8,128)S(1)}, u32[]{:S(2)}, u32[]{:S(2)}) %collective-permute-start.1) | collective-permute-done | bytes 458784 | tf_op jit(solution)/shard_map/ppermute | solution.py:824
  22.5 2.6 %collective-permute-start.3 = (f32[140,4,256]{2,1,0:T(4,128)S(1)}, f32[140,4,256]{2,1,0:T(4,128)S(1)}, u32[]{:S(2)}, u32[]{:S(2)}) collective-permute-start(f32[140,4,256]{2,1,0:T(4,128)S(1)} %get-tuple-element.62), channel_id=1, source_target_pairs={{1,0},{2,1},{3,2},{4,3},{5,4},{6,5},{7,6},{0,7},{9,8},{10,9},{11,1... | collective-permute-start | bytes 1720328 | tf_op jit(solution)/shard_map/ppermute | solution.py:824
  25.2 3.5 %collective-permute-start.4 = (f32[36,16,128]{2,1,0:T(8,128)S(1)}, f32[36,16,128]{2,1,0:T(8,128)S(1)}, u32[]{:S(2)}, u32[]{:S(2)}) collective-permute-start(f32[36,16,128]{2,1,0:T(8,128)S(1)} %get-tuple-element.65), channel_id=1, source_target_pairs={{0,8},{8,16},{16,24},{1,9},{9,17},{17,25},{2,10},{10,18},{18,26},{... | collective-permute-start | bytes 884744 | tf_op jit(solution)/shard_map/ppermute | solution.py:824
  31.1 2.9 %collective-permute-done.4.low.refs_4_ = f32[36,16,128]{2,1,0:T(8,128)S(1)} collective-permute-done((f32[36,16,128]{2,1,0:T(8,128)S(1)}, f32[36,16,128]{2,1,0:T(8,128)S(1)}, u32[]{:S(2)}, u32[]{:S(2)}) %collective-permute-start.4) | collective-permute-done | bytes 294944 | tf_op jit(solution)/shard_map/ppermute | solution.py:824
  34.0 4.1 %collective-permute-done.5.high.refs_5_ = f32[36,16,128]{2,1,0:T(8,128)S(1)} collective-permute-done((f32[36,16,128]{2,1,0:T(8,128)S(1)}, f32[36,16,128]{2,1,0:T(8,128)S(1)}, u32[]{:S(2)}, u32[]{:S(2)}) %collective-permute-start.5) | collective-permute-done | bytes 294944 | tf_op jit(solution)/shard_map/ppermute | solution.py:824
  40.9 11.1 %fine_start.1 = (f32[6,2,20,40,256]{4,3,2,1,0:T(8,128)S(1)}, f32[2,20,40,256]{3,2,1,0:T(8,128)S(1)}, f32[2,20,40,256]{3,2,1,0:T(8,128)S(1)}, f32[2,20,40,256]{3,...) custom-call(f32[8]{0:T(128)S(1)} %copy-done.4, ...), custom_call_target="tpu_custom_call" | custom-call | tf_op jit(solution)/shard_map/fine_start/pallas_call | solution.py:129
  58.7 2.6 %collective-permute-start.9 = (f32[20,4,256]{2,1,0:T(4,128)S(1)}, f32[20,4,256]{2,1,0:T(4,128)S(1)}, u32[]{:S(2)}, u32[]{:S(2)}) collective-permute-start(f32[20,4,256]{2,1,0:T(4,128)S(1)} %get-tuple-element.91), channel_id=1, source_target_pairs={{1,0},{2,1},{3,2},{4,3},{5,4},{6,5},{7,6},{0,7},{9,8},{10,9},{11,1... | collective-permute-start | bytes 245768 | tf_op jit(solution)/shard_map/ppermute | solution.py:824
  61.3 2.9 %collective-permute-done.8.y_lo = f32[20,4,256]{2,1,0:T(4,128)S(1)} collective-permute-done((f32[20,4,256]{2,1,0:T(4,128)S(1)}, f32[20,4,256]{2,1,0:T(4,128)S(1)}, u32[]{:S(2)}, u32[]{:S(2)}) %collective-permute-start.8) | collective-permute-done | bytes 81952 | tf_op jit(solution)/shard_map/ppermute | solution.py:824
  64.2 4.1 %fine_finish.1 = (f32[32,32,256]{2,1,0:T(8,128)}, f32[16,16,128]{2,1,0:T(8,128)S(1)}, f32[8,16,128]{2,1,0:T(8,128)S(1)}, f32[8,16,128]{2,1,0:T(8,128)S(1)}) custom-call(f32[6,2,20,40,256]{4,3,2,1,0:T(8,128)S(1)} %get-tuple-element.83.w_ref, f32[2,20,40,256]{3,2,1,0:T(8,128)S(1)} %get-tuple-element.84.r3_ref, ...), custom_call_target="tpu_custom_call" | custom-call | tf_op jit(solution)/shard_map/fine_finish/pallas_call | solution.py:129
  68.5 3.7 %collective-permute-start.13 = (f32[8,16,128]{2,1,0:T(8,128)S(1)}, f32[8,16,128]{2,1,0:T(8,128)S(1)}, u32[]{:S(2)}, u32[]{:S(2)}) collective-permute-start(f32[8,16,128]{2,1,0:T(8,128)S(1)} %get-tuple-element.97), channel_id=1, source_target_pairs={{8,0},{16,8},{24,16},{0,24},{9,1},{17,9},{25,17},{1,25},{10,2},{18... | collective-permute-start | bytes 196616 | tf_op jit(solution)/shard_map/ppermute | solution.py:824
  72.2 2.6 %collective-permute-done.12.refs_0_.refs_8_ = f32[8,16,128]{2,1,0:T(8,128)S(1)} collective-permute-done((f32[8,16,128]{2,1,0:T(8,128)S(1)}, f32[8,16,128]{2,1,0:T(8,128)S(1)}, u32[]{:S(2)}, u32[]{:S(2)}) %collective-permute-start.12) | collective-permute-done | bytes 65568 | tf_op jit(solution)/shard_map/ppermute | solution.py:824
  74.8 2.6 %collective-permute-start.15 = (f32[32,8,128]{2,1,0:T(8,128)S(1)}, f32[32,8,128]{2,1,0:T(8,128)S(1)}, u32[]{:S(2)}, u32[]{:S(2)}) collective-permute-start(f32[32,8,128]{2,1,0:T(8,128)S(1)} %get-tuple-element.99), channel_id=1, source_target_pairs={{1,0},{2,1},{3,2},{4,3},{5,4},{6,5},{7,6},{0,7},{9,8},{10,9},{11,1... | collective-permute-start | bytes 393224 | tf_op jit(solution)/shard_map/ppermute | solution.py:824
  77.5 3.0 %collective-permute-done.14.refs_10_ = f32[32,8,128]{2,1,0:T(8,128)S(1)} collective-permute-done((f32[32,8,128]{2,1,0:T(8,128)S(1)}, f32[32,8,128]{2,1,0:T(8,128)S(1)}, u32[]{:S(2)}, u32[]{:S(2)}) %collective-permute-start.14) | collective-permute-done | bytes 131104 | tf_op jit(solution)/shard_map/ppermute | solution.py:824
  80.5 5.7 %level_1.1 = (f32[8,8,128]{2,1,0:T(8,128)S(1)}, f32[8,8,128]{2,1,0:T(8,128)S(1)}, f32[8,8,128]{2,1,0:T(8,128)S(1)}) custom-call(f32[16,16,128]{2,1,0:T(8,128)S(1)} %get-tuple-element.73.refs_0_, f32[16,16,128]{2,1,0:T(8,128)S(1)} %get-tuple-element.74.refs_1_, f32[16,16,128]{2,1,0:T(8,128)S(1)} %get-tuple-element.75.refs_2_, ...), custom_call_target="tpu_custom_call" | custom-call | tf_op jit(solution)/shard_map/level_1/pallas_call | solution.py:129
  87.3 2.7 %collective-permute-start.17 = (f32[8,8,128]{2,1,0:T(8,128)S(1)}, f32[8,8,128]{2,1,0:T(8,128)S(1)}, u32[]{:S(2)}, u32[]{:S(2)}) collective-permute-start(f32[8,8,128]{2,1,0:T(8,128)S(1)} %get-tuple-element.102), channel_id=1, source_target_pairs={{8,0},{16,8},{24,16},{0,24},{9,1},{17,9},{25,17},{1,25},{10,2},{18... | collective-permute-start | bytes 98312 | tf_op jit(solution)/shard_map/ppermute | solution.py:824
  92.0 2.6 %collective-permute-start.19 = (f32[24,8,128]{2,1,0:T(8,128)S(1)}, f32[24,8,128]{2,1,0:T(8,128)S(1)}, u32[]{:S(2)}, u32[]{:S(2)}) collective-permute-start(f32[24,8,128]{2,1,0:T(8,128)S(1)} %get-tuple-element.104), channel_id=1, source_target_pairs={{1,0},{2,1},{3,2},{4,3},{5,4},{6,5},{7,6},{0,7},{9,8},{10,9},{11,1... | collective-permute-start | bytes 294920 | tf_op jit(solution)/shard_map/ppermute | solution.py:824
  94.7 2.5 %collective-permute-done.18.refs_10_ = f32[24,8,128]{2,1,0:T(8,128)S(1)} collective-permute-done((f32[24,8,128]{2,1,0:T(8,128)S(1)}, f32[24,8,128]{2,1,0:T(8,128)S(1)}, u32[]{:S(2)}, u32[]{:S(2)}) %collective-permute-start.18) | collective-permute-done | bytes 98336 | tf_op jit(solution)/shard_map/ppermute | solution.py:824
  97.2 3.3 %level_2.1 = f32[4,4,128]{2,1,0:T(4,128)S(1)} custom-call(f32[8,8,128]{2,1,0:T(8,128)S(1)} %get-tuple-element.76.refs_3_.refs_0_, f32[8,8,128]{2,1,0:T(8,128)S(1)} %get-tuple-element.77.refs_4_.refs_1_, f32[8,8,128]{2,1,0:T(8,128)S(1)} %get-tuple-element.78.refs_5_.refs_2_, f32[8,8,128]{2,1,0:T(8,128)S(1)} %get-tuple-element.100.refs_1_.refs_3_, ...), custom_call_target="tpu_custom_call" | custom-call | tf_op jit(solution)/shard_map/level_2/pallas_call | solution.py:129
  105.0 4.6 %collective-permute-done.21 = f32[4,4,128]{2,1,0:T(4,128)S(1)} collective-permute-done((f32[4,4,128]{2,1,0:T(4,128)S(1)}, f32[4,4,128]{2,1,0:T(4,128)S(1)}, u32[]{:S(2)}, u32[]{:S(2)}) %collective-permute-start.21) | collective-permute-done | bytes 8224 | tf_op jit(solution)/shard_map/ppermute | solution.py:832
  116.2 2.7 %level_3.1 = f32[4,4,32]{2,1,0:T(4,128)} custom-call(f32[20,4,128]{2,1,0:T(4,128)S(1)} %collective-permute-done.23.refs_0_, f32[20,4,128]{2,1,0:T(4,128)S(1)} %collective-permute-done.24.refs_1_, f32[20,4,128]{2,1,0:T(4,128)S(1)} %constant_dynamic-update-slice_fusion.refs_2_, f32[20,4,128]{2,1,0:T(4,128)S(1)} %collective-permute-done.25.refs_3_, ...), custom_call_target="tpu_custom_call" | custom-call | tf_op jit(solution)/shard_map/level_3/pallas_call | solution.py:129
  (61 shorter events, 28.1 us)
Async XLA Ops:
  3.0 15.0 %collective-permute-start = (f32[14,32,256]{2,1,0:T(8,128)}, f32[14,32,256]{2,1,0:T(8,128)S(1)}, u32[]{:S(2)}, u32[]{:S(2)}) collective-permute-start(f32[14,32,256]{2,1,0:T(8,128)} %get-tuple-element.54), channel_id=1, source_target_pairs={{0,8},{8,16},{16,24},{1,9},{9,17},{17,25},{2,10},{10,18},{18,26},{... | collective-permute-start | bytes 1376264 | tf_op jit(solution)/shard_map/ppermute | solution.py:824
  8.1 14.2 %collective-permute-start.1 = (f32[14,32,256]{2,1,0:T(8,128)}, f32[14,32,256]{2,1,0:T(8,128)S(1)}, u32[]{:S(2)}, u32[]{:S(2)}) collective-permute-start(f32[14,32,256]{2,1,0:T(8,128)} %get-tuple-element.55), channel_id=1, source_target_pairs={{8,0},{16,8},{24,16},{9,1},{17,9},{25,17},{10,2},{18,10},{26,18},{... | collective-permute-start | bytes 1376264 | tf_op jit(solution)/shard_map/ppermute | solution.py:824
  22.5 15.7 %collective-permute-start.2 = (f32[140,4,256]{2,1,0:T(4,128)S(1)}, f32[140,4,256]{2,1,0:T(4,128)S(1)}, u32[]{:S(2)}, u32[]{:S(2)}) collective-permute-start(f32[140,4,256]{2,1,0:T(4,128)S(1)} %get-tuple-element.61), channel_id=1, source_target_pairs={{0,1},{1,2},{2,3},{3,4},{4,5},{5,6},{6,7},{7,0},{8,9},{9,10},{10,1... | collective-permute-start | bytes 1720328 | tf_op jit(solution)/shard_map/ppermute | solution.py:824
  22.5 15.6 %collective-permute-start.3 = (f32[140,4,256]{2,1,0:T(4,128)S(1)}, f32[140,4,256]{2,1,0:T(4,128)S(1)}, u32[]{:S(2)}, u32[]{:S(2)}) collective-permute-start(f32[140,4,256]{2,1,0:T(4,128)S(1)} %get-tuple-element.62), channel_id=1, source_target_pairs={{1,0},{2,1},{3,2},{4,3},{5,4},{6,5},{7,6},{0,7},{9,8},{10,9},{11,1... | collective-permute-start | bytes 1720328 | tf_op jit(solution)/shard_map/ppermute | solution.py:824
  25.2 8.8 %collective-permute-start.4 = (f32[36,16,128]{2,1,0:T(8,128)S(1)}, f32[36,16,128]{2,1,0:T(8,128)S(1)}, u32[]{:S(2)}, u32[]{:S(2)}) collective-permute-start(f32[36,16,128]{2,1,0:T(8,128)S(1)} %get-tuple-element.65), channel_id=1, source_target_pairs={{0,8},{8,16},{16,24},{1,9},{9,17},{17,25},{2,10},{10,18},{18,26},{... | collective-permute-start | bytes 884744 | tf_op jit(solution)/shard_map/ppermute | solution.py:824
  28.6 9.5 %collective-permute-start.5 = (f32[36,16,128]{2,1,0:T(8,128)S(1)}, f32[36,16,128]{2,1,0:T(8,128)S(1)}, u32[]{:S(2)}, u32[]{:S(2)}) collective-permute-start(f32[36,16,128]{2,1,0:T(8,128)S(1)} %get-tuple-element.66), channel_id=1, source_target_pairs={{8,0},{16,8},{24,16},{9,1},{17,9},{25,17},{10,2},{18,10},{26,18},{... | collective-permute-start | bytes 884744 | tf_op jit(solution)/shard_map/ppermute | solution.py:824
  38.2 42.3 %collective-permute-start.10 = (f32[168,8,128]{2,1,0:T(8,128)S(1)}, f32[168,8,128]{2,1,0:T(8,128)S(1)}, u32[]{:S(2)}, u32[]{:S(2)}) collective-permute-start(f32[168,8,128]{2,1,0:T(8,128)S(1)} %get-tuple-element.94), channel_id=1, source_target_pairs={{0,1},{1,2},{2,3},{3,4},{4,5},{5,6},{6,7},{7,0},{8,9},{9,10},{10,1... | collective-permute-start | bytes 2064392 | tf_op jit(solution)/shard_map/ppermute | solution.py:824
  38.7 41.8 %collective-permute-start.11 = (f32[168,8,128]{2,1,0:T(8,128)S(1)}, f32[168,8,128]{2,1,0:T(8,128)S(1)}, u32[]{:S(2)}, u32[]{:S(2)}) collective-permute-start(f32[168,8,128]{2,1,0:T(8,128)S(1)} %get-tuple-element.95), channel_id=1, source_target_pairs={{1,0},{2,1},{3,2},{4,3},{5,4},{6,5},{7,6},{0,7},{9,8},{10,9},{11,1... | collective-permute-start | bytes 2064392 | tf_op jit(solution)/shard_map/ppermute | solution.py:824
  52.0 6.2 %collective-permute-start.6 = (f32[2,32,256]{2,1,0:T(8,128)S(1)}, f32[2,32,256]{2,1,0:T(8,128)S(1)}, u32[]{:S(2)}, u32[]{:S(2)}) collective-permute-start(f32[2,32,256]{2,1,0:T(8,128)S(1)} %get-tuple-element.88), channel_id=1, source_target_pairs={{0,8},{8,16},{16,24},{24,0},{1,9},{9,17},{17,25},{25,1},{2,10},{10... | collective-permute-start | bytes 196616 | tf_op jit(solution)/shard_map/ppermute | solution.py:824
  53.6 5.0 %collective-permute-start.7 = (f32[2,32,256]{2,1,0:T(8,128)S(1)}, f32[2,32,256]{2,1,0:T(8,128)S(1)}, u32[]{:S(2)}, u32[]{:S(2)}) collective-permute-start(f32[2,32,256]{2,1,0:T(8,128)S(1)} %get-tuple-element.89), channel_id=1, source_target_pairs={{8,0},{16,8},{24,16},{0,24},{9,1},{17,9},{25,17},{1,25},{10,2},{18... | collective-permute-start | bytes 196616 | tf_op jit(solution)/shard_map/ppermute | solution.py:824
  58.6 5.6 %collective-permute-start.8 = (f32[20,4,256]{2,1,0:T(4,128)S(1)}, f32[20,4,256]{2,1,0:T(4,128)S(1)}, u32[]{:S(2)}, u32[]{:S(2)}) collective-permute-start(f32[20,4,256]{2,1,0:T(4,128)S(1)} %get-tuple-element.90), channel_id=1, source_target_pairs={{0,1},{1,2},{2,3},{3,4},{4,5},{5,6},{6,7},{7,0},{8,9},{9,10},{10,1... | collective-permute-start | bytes 245768 | tf_op jit(solution)/shard_map/ppermute | solution.py:824
  58.7 5.6 %collective-permute-start.9 = (f32[20,4,256]{2,1,0:T(4,128)S(1)}, f32[20,4,256]{2,1,0:T(4,128)S(1)}, u32[]{:S(2)}, u32[]{:S(2)}) collective-permute-start(f32[20,4,256]{2,1,0:T(4,128)S(1)} %get-tuple-element.91), channel_id=1, source_target_pairs={{1,0},{2,1},{3,2},{4,3},{5,4},{6,5},{7,6},{0,7},{9,8},{10,9},{11,1... | collective-permute-start | bytes 245768 | tf_op jit(solution)/shard_map/ppermute | solution.py:824
  68.4 6.4 %collective-permute-start.12 = (f32[8,16,128]{2,1,0:T(8,128)S(1)}, f32[8,16,128]{2,1,0:T(8,128)S(1)}, u32[]{:S(2)}, u32[]{:S(2)}) collective-permute-start(f32[8,16,128]{2,1,0:T(8,128)S(1)} %get-tuple-element.96), channel_id=1, source_target_pairs={{0,8},{8,16},{16,24},{24,0},{1,9},{9,17},{17,25},{25,1},{2,10},{10... | collective-permute-start | bytes 196616 | tf_op jit(solution)/shard_map/ppermute | solution.py:824
  68.5 6.3 %collective-permute-start.13 = (f32[8,16,128]{2,1,0:T(8,128)S(1)}, f32[8,16,128]{2,1,0:T(8,128)S(1)}, u32[]{:S(2)}, u32[]{:S(2)}) collective-permute-start(f32[8,16,128]{2,1,0:T(8,128)S(1)} %get-tuple-element.97), channel_id=1, source_target_pairs={{8,0},{16,8},{24,16},{0,24},{9,1},{17,9},{25,17},{1,25},{10,2},{18... | collective-permute-start | bytes 196616 | tf_op jit(solution)/shard_map/ppermute | solution.py:824
  74.8 5.7 %collective-permute-start.14 = (f32[32,8,128]{2,1,0:T(8,128)S(1)}, f32[32,8,128]{2,1,0:T(8,128)S(1)}, u32[]{:S(2)}, u32[]{:S(2)}) collective-permute-start(f32[32,8,128]{2,1,0:T(8,128)S(1)} %get-tuple-element.98), channel_id=1, source_target_pairs={{0,1},{1,2},{2,3},{3,4},{4,5},{5,6},{6,7},{7,0},{8,9},{9,10},{10,1... | collective-permute-start | bytes 393224 | tf_op jit(solution)/shard_map/ppermute | solution.py:824
  74.8 5.7 %collective-permute-start.15 = (f32[32,8,128]{2,1,0:T(8,128)S(1)}, f32[32,8,128]{2,1,0:T(8,128)S(1)}, u32[]{:S(2)}, u32[]{:S(2)}) collective-permute-start(f32[32,8,128]{2,1,0:T(8,128)S(1)} %get-tuple-element.99), channel_id=1, source_target_pairs={{1,0},{2,1},{3,2},{4,3},{5,4},{6,5},{7,6},{0,7},{9,8},{10,9},{11,1... | collective-permute-start | bytes 393224 | tf_op jit(solution)/shard_map/ppermute | solution.py:824
  86.2 5.8 %collective-permute-start.16 = (f32[8,8,128]{2,1,0:T(8,128)S(1)}, f32[8,8,128]{2,1,0:T(8,128)S(1)}, u32[]{:S(2)}, u32[]{:S(2)}) collective-permute-start(f32[8,8,128]{2,1,0:T(8,128)S(1)} %get-tuple-element.101), channel_id=1, source_target_pairs={{0,8},{8,16},{16,24},{24,0},{1,9},{9,17},{17,25},{25,1},{2,10},{10... | collective-permute-start | bytes 98312 | tf_op jit(solution)/shard_map/ppermute | solution.py:824
  87.3 4.6 %collective-permute-start.17 = (f32[8,8,128]{2,1,0:T(8,128)S(1)}, f32[8,8,128]{2,1,0:T(8,128)S(1)}, u32[]{:S(2)}, u32[]{:S(2)}) collective-permute-start(f32[8,8,128]{2,1,0:T(8,128)S(1)} %get-tuple-element.102), channel_id=1, source_target_pairs={{8,0},{16,8},{24,16},{0,24},{9,1},{17,9},{25,17},{1,25},{10,2},{18... | collective-permute-start | bytes 98312 | tf_op jit(solution)/shard_map/ppermute | solution.py:824
  92.0 5.2 %collective-permute-start.18 = (f32[24,8,128]{2,1,0:T(8,128)S(1)}, f32[24,8,128]{2,1,0:T(8,128)S(1)}, u32[]{:S(2)}, u32[]{:S(2)}) collective-permute-start(f32[24,8,128]{2,1,0:T(8,128)S(1)} %get-tuple-element.103), channel_id=1, source_target_pairs={{0,1},{1,2},{2,3},{3,4},{4,5},{5,6},{6,7},{7,0},{8,9},{9,10},{10,1... | collective-permute-start | bytes 294920 | tf_op jit(solution)/shard_map/ppermute | solution.py:824
  92.0 5.1 %collective-permute-start.19 = (f32[24,8,128]{2,1,0:T(8,128)S(1)}, f32[24,8,128]{2,1,0:T(8,128)S(1)}, u32[]{:S(2)}, u32[]{:S(2)}) collective-permute-start(f32[24,8,128]{2,1,0:T(8,128)S(1)} %get-tuple-element.104), channel_id=1, source_target_pairs={{1,0},{2,1},{3,2},{4,3},{5,4},{6,5},{7,6},{0,7},{9,8},{10,9},{11,1... | collective-permute-start | bytes 294920 | tf_op jit(solution)/shard_map/ppermute | solution.py:824
  100.5 4.6 %collective-permute-start.20 = (f32[4,4,128]{2,1,0:T(4,128)S(1)}, f32[4,4,128]{2,1,0:T(4,128)S(1)}, u32[]{:S(2)}, u32[]{:S(2)}) collective-permute-start(f32[4,4,128]{2,1,0:T(4,128)S(1)} %level_2.1), channel_id=1, source_target_pairs={{0,16},{8,24},{16,0},{24,8},{1,17},{9,25},{17,1},{25,9},{2,18},{10... | collective-permute-start | bytes 24584 | tf_op jit(solution)/shard_map/ppermute | solution.py:832
  102.5 7.1 %collective-permute-start.22 = (f32[4,4,128]{2,1,0:T(4,128)S(1)}, f32[4,4,128]{2,1,0:T(4,128)S(1)}, u32[]{:S(2)}, u32[]{:S(2)}) collective-permute-start(f32[4,4,128]{2,1,0:T(4,128)S(1)} %level_2.1), channel_id=1, source_target_pairs={{0,24},{8,0},{16,8},{24,16},{1,25},{9,1},{17,9},{25,17},{2,26},{10... | collective-permute-start | bytes 24584 | tf_op jit(solution)/shard_map/ppermute | solution.py:832
  104.1 5.4 %collective-permute-start.21 = (f32[4,4,128]{2,1,0:T(4,128)S(1)}, f32[4,4,128]{2,1,0:T(4,128)S(1)}, u32[]{:S(2)}, u32[]{:S(2)}) collective-permute-start(f32[4,4,128]{2,1,0:T(4,128)S(1)} %level_2.1), channel_id=1, source_target_pairs={{0,8},{8,16},{16,24},{24,0},{1,9},{9,17},{17,25},{25,1},{2,10},{10... | collective-permute-start | bytes 24584 | tf_op jit(solution)/shard_map/ppermute | solution.py:832
  111.0 5.2 %collective-permute-start.23 = (f32[20,4,128]{2,1,0:T(4,128)S(1)}, f32[20,4,128]{2,1,0:T(4,128)S(1)}, u32[]{:S(2)}, u32[]{:S(2)}) collective-permute-start(f32[20,4,128]{2,1,0:T(4,128)S(1)} %constant_dynamic-update-slice_fusion.refs_2_), channel_id=1, source_target_pairs={{0,2},{1,3},{2,4},{3,5},{4,6},{5,7},{6,0},{7,1},{8,10},{9,11},{10,... | collective-permute-start | bytes 122888 | tf_op jit(solution)/shard_map/ppermute | solution.py:832
  (9 other events, 55.8 us)

commit v5 on v4

--- a/solution.py
+++ b/solution.py
@@ -172,39 +172,25 @@
     return call(kernel, "pack_planes", outs, arrays, specs, scratch, PACK_LIMIT)
 
 
-def pack_rows_fine(from_low, from_high, class_map, noise_seed, mean_shift, sample_field):
+def pack_rows_fine(class_map, noise_seed, mean_shift, sample_field):
     ni, nj, nk = class_map.shape
     w = FINE_HALO
-    count = ni + 2 * w
-    arrays = (from_low, from_high, class_map, noise_seed, mean_shift, sample_field)
 
     def kernel(*refs):
-        low, high, *own = refs[:6]
-        to_next, to_previous = refs[6:]
+        own, (to_next, to_previous) = refs[:4], refs[4:]
         even = checker((nj, nk))
         for out, start in ((to_previous, 0), (to_next, nj - w)):
             rows = pl.ds(start, w)
             mask = even[start : start + w]
-            for a in range(3):
-                for e in range(w):
-                    out[a * count + e] = low[a * w + e, rows]
-                    out[a * count + ni + w + e] = high[a * w + e, rows]
-                for e in range(ni):
-                    if a == 0:
-                        v = (own[0][e, rows] + 1).astype(jnp.float32)
-                    else:
-                        v = own[a][e, rows].astype(jnp.float32)
-                    out[a * count + w + e] = v
-            base = 3 * count
-            for q in range(w // 2):
-                out[base + q] = low[3 * w + q, rows]
-                out[base + (ni + w) // 2 + q] = high[3 * w + q, rows]
+            for e in range(ni):
+                out[e] = (own[0][e, rows] + 1).astype(jnp.float32)
+                out[ni + e] = own[1][e, rows].astype(jnp.float32)
+                out[2 * ni + e] = own[2][e, rows]
             for q in range(ni // 2):
-                v = jnp.where(mask, own[3][2 * q + 1, rows], own[3][2 * q, rows])
-                out[base + w // 2 + q] = v
-
-    total = 3 * count + count // 2
-    return call(kernel, "pack_rows_fine", [f32(total, w, nk)] * 2, arrays)
+                out[3 * ni + q] = jnp.where(mask, own[3][2 * q + 1, rows], own[3][2 * q, rows])
+
+    args = (class_map, noise_seed, mean_shift, sample_field)
+    return call(kernel, "pack_rows_fine", [f32(3 * ni + ni // 2, w, nk)] * 2, args)
 
 
 def pack_rows(triples, w, name):
@@ -442,7 +428,7 @@
     return call(kernel, "halo_noise", [f32(SWEEPS, 2, w // 2, nj, nk)] * 2, (from_low, from_high))
 
 
-def fine_start(tables, own, noise, planes, plane_noise, rows):
+def fine_start(tables, own, noise, planes, plane_noise, rows, corners):
     class_map, mean_shift, sample_field = own
     ni, nj, nk = class_map.shape
     w = FINE_HALO
@@ -451,7 +437,9 @@
     pairs = count // 2
     count_j = nj + 2 * w
 
-    def kernel(d_tab, m_tab, cls_ref, b_ref, sample, g_own, x_lo, x_hi, g_lo, g_hi, y_lo, y_hi, *refs):
+    def kernel(d_tab, m_tab, cls_ref, b_ref, sample, g_own, x_lo, x_hi, g_lo, g_hi, *refs):
+        y_lo, y_hi, c_lo, c_hi = refs[:4]
+        refs = refs[4:]
         w_ref, r3_ref, n3_ref, m_ref, xb_ref, to_next, to_previous = refs[:7]
         d0, d1, r_ref, x0, x1 = refs[7:]
         d_refs, x_refs = (d0, d1), (x0, x1)
@@ -465,8 +453,15 @@
             for ref in (*d_refs, *x_refs):
                 ref[g] = zero
 
-        def edge(at, mask=False):
-            hi, lo = y_hi[at], y_lo[at]
+        def edge(a, n, where, mask=False):
+            part = 2 if a == 3 else 1
+            if where == 1:
+                at, refs = a * ni + n - w // part, (y_hi, y_lo)
+            elif where == 0:
+                at, refs = a * w + n, (c_hi, c_lo)
+            else:
+                at, refs = 3 * w + h + a * w + n - (w + ni) // part, (c_hi, c_lo)
+            hi, lo = refs[0][at], refs[1][at]
             if mask:
                 hi, lo = hi * has_high, lo * has_low
             return jnp.concatenate([hi, lo], axis=0)
@@ -485,10 +480,10 @@
                 bs = [src[2 * w + n + off] for n in e]
                 g_at = q + off // 2
                 x = src[3 * w + g_at]
-            cls = [jnp.concatenate([mids[c], edge(e[c], True)], axis=0) for c in range(2)]
-            b = [jnp.concatenate([bs[c], edge(2 * count + e[c])], axis=0) for c in range(2)]
-            x1[q + 1] = jnp.concatenate([x, edge(3 * count + q, True)], axis=0)
-            seeds = [edge(count + e[c]) for c in range(2)]
+            cls = [jnp.concatenate([mids[c], edge(0, e[c], where, True)], axis=0) for c in range(2)]
+            b = [jnp.concatenate([bs[c], edge(2, e[c], where)], axis=0) for c in range(2)]
+            x1[q + 1] = jnp.concatenate([x, edge(3, q, where, True)], axis=0)
+            seeds = [edge(1, e[c], where) for c in range(2)]
             for c in range(2):
                 number = jnp.where(even, cls[c], cls[1 - c]).astype(jnp.int32)
                 d, m = lookups(number, [d_tab, m_tab])
@@ -546,7 +541,7 @@
         pltpu.VMEM((pairs + 2, count_j, nk), jnp.float32),
         pltpu.VMEM((pairs + 2, count_j, nk), jnp.float32),
     ]
-    args = (*tables, class_map, mean_shift, sample_field, noise, *planes, *plane_noise, *rows)
+    args = (*tables, class_map, mean_shift, sample_field, noise, *planes, *plane_noise, *rows, *corners)
     specs = [SMEM, SMEM] + [VMEM] * (len(args) - 2)
     return call(kernel, "fine_start", outs, args, specs, scratch, START_LIMIT)
 
@@ -839,29 +834,32 @@
     arrays = (class_map, noise_seed, mean_shift, sample_field)
 
     planes = both_ways(*pack_planes(*arrays), "gx", False)
-    noise = own_noise(noise_seed)
-    statics1, statics2, static_next, static_previous, tail = coarse_statics(
-        tables, class_map, noise_seed
+    *rows, classes, seed = lax.optimization_barrier(
+        (*pack_rows_fine(*arrays), class_map, noise_seed)
     )
-    *planes, noise, static_next, static_previous = lax.optimization_barrier(
-        (*planes, noise, static_next, static_previous)
+    rows = both_ways(*rows, "gy")
+    statics1, statics2, static_next, static_previous, tail = coarse_statics(tables, classes, seed)
+    seed, static_next, static_previous = lax.optimization_barrier(
+        (noise_seed, static_next, static_previous)
     )
     static_planes = both_ways(static_next, static_previous, "gx", False)
-
-    rows = both_ways(*pack_rows_fine(*planes, *arrays), "gy")
+    noise = own_noise(seed)
+    *planes, noise = lax.optimization_barrier((*planes, noise))
+
+    corners = both_ways(*pack_rows([planes], FINE_HALO, "pack_corners"), "gy")
     plane_noise = halo_noise(*planes)
-    *rows, low_noise, high_noise, static_low, static_high = lax.optimization_barrier(
-        (*rows, *plane_noise, *static_planes)
+    *early, low_noise, high_noise, static_low, static_high = lax.optimization_barrier(
+        (*rows, *corners, *plane_noise, *static_planes)
     )
     static_planes = (static_low, static_high)
-    static_next, static_previous = pack_static_rows(static_planes, statics1, statics2)
-    *rows, static_next, static_previous = lax.optimization_barrier(
-        (*rows, static_next, static_previous)
+    *early, static_next, static_previous = lax.optimization_barrier(
+        (*early, *pack_static_rows(static_planes, statics1, statics2))
     )
+    rows, corners = early[:2], early[2:]
     static_rows = both_ways(static_next, static_previous, "gy")
 
     *state, black, to_next, to_previous = fine_start(
-        tables, (class_map, mean_shift, sample_field), noise, planes, (low_noise, high_noise), rows
+        tables, (class_map, mean_shift, sample_field), noise, planes, (low_noise, high_noise), rows, corners
     )
     planes = both_ways(to_next, to_previous, "gx")
     rows = both_ways(*pack_rows([(planes[0], black, planes[1])], FINE_HALO, "pack_rows_black"), "gy")

time: 119 us -> 115 us (0.966)
  waiting for transfers between devices: 35.4 us -> 27.1 us
  starting transfers between devices: 43.4 us -> 47.7 us
    ppermute x10 -> x11, waiting for transfers between devices: 8.72 us -> 0.59 us  [both_ways(): lax.ppermute(to_previous, axis, down)]
    ppermute x10 -> x11, starting transfers between devices: 12.1 us -> 15 us  [both_ways(): lax.ppermute(to_next, axis, up)]
    ppermute x10 -> x11, starting transfers between devices: 24.1 us -> 25.8 us  [both_ways(): lax.ppermute(to_previous, axis, down)]
    ppermute x10 -> x11, waiting for transfers between devices: 18.2 us -> 17.1 us  [both_ways(): lax.ppermute(to_next, axis, up)]
    pallas_call x14 -> x15, Pallas kernels: 39.1 us -> 39.1 us  [call(): pl.pallas_call(kernel, out_shape=tuple(outs), in_specs=specs or [VMEM] *...]
  transfers between devices with their start and end apart: 27 -> 29, of which waited for: 16 -> 13; matrix products, arithmetic and copies ran while one was open for 0% -> 0% of each run, Pallas kernels for 21% -> 22%
where the time goes in v5:
time: 115 us
  starting transfers between devices  47.7 us (41%)
  Pallas kernels  39.1 us (34%)
  waiting for transfers between devices  27.1 us (24%)
    pallas_call x15, Pallas kernels, call(): pl.pallas_call(kernel, out_shape=tuple(outs), in_specs=specs or [VMEM] *...  39.1 us
    ppermute x11, starting transfers between devices, both_ways(): lax.ppermute(to_previous, axis, down)  25.8 us
    ppermute x11, waiting for transfers between devices, both_ways(): lax.ppermute(to_next, axis, up)  17.1 us
    ppermute x11, starting transfers between devices, both_ways(): lax.ppermute(to_next, axis, up)  15 us
    ppermute x7, waiting for transfers between devices, window(): lax.ppermute(block, axis, [(i, (i - off) % size) for i in range(size)])  9.39 us
    ppermute x7, starting transfers between devices, window(): lax.ppermute(block, axis, [(i, (i - off) % size) for i in range(size)])  6.9 us
  transfers between devices with their start and end apart: 29, of which 13 were waited for; matrix products, arithmetic and copies ran while one was open for 0% of the time, Pallas kernels for 22%

profile of v5, /device:TPU:0, one launch (start us, length us, event | category | flops | bytes accessed | tf_op | source)
XLA Modules:
  0.0 114.8 jit_solution(11384705145745742340)
XLA Ops:
  0.7 2.4 %pack_planes.1 = (f32[14,32,256]{2,1,0:T(8,128)}, f32[14,32,256]{2,1,0:T(8,128)}) custom-call(s32[32,32,256]{2,1,0:T(8,128)} %cls_ref.2, s32[32,32,256]{2,1,0:T(8,128)} %seed_ref.1, f32[32,32,256]{2,1,0:T(8,128)} %b_ref.1, f32[32,32,256]{2,1,0:T(8,128)} %sample.1), custom_call_target="tpu_custom_call" | custom-call | tf_op jit(solution)/shard_map/pack_planes/pallas_call | solution.py:129
  3.1 5.0 %collective-permute-start = (f32[14,32,256]{2,1,0:T(8,128)}, f32[14,32,256]{2,1,0:T(8,128)S(1)}, u32[]{:S(2)}, u32[]{:S(2)}) collective-permute-start(f32[14,32,256]{2,1,0:T(8,128)} %get-tuple-element.65), channel_id=1, source_target_pairs={{0,8},{8,16},{16,24},{1,9},{9,17},{17,25},{2,10},{10,18},{18,26},{... | collective-permute-start | bytes 1376264 | tf_op jit(solution)/shard_map/ppermute | solution.py:819
  9.7 2.6 %collective-permute-start.3 = (f32[112,4,256]{2,1,0:T(4,128)S(1)}, f32[112,4,256]{2,1,0:T(4,128)S(1)}, u32[]{:S(2)}, u32[]{:S(2)}) collective-permute-start(f32[112,4,256]{2,1,0:T(4,128)S(1)} %get-tuple-element.78), channel_id=1, source_target_pairs={{1,0},{2,1},{3,2},{4,3},{5,4},{6,5},{7,6},{0,7},{9,8},{10,9},{11,1... | collective-permute-start | bytes 1376264 | tf_op jit(solution)/shard_map/ppermute | solution.py:819
  12.3 4.0 %coarse_statics.1 = (f32[16,16,128]{2,1,0:T(8,128)S(1)}, f32[16,16,128]{2,1,0:T(8,128)S(1)}, f32[16,16,128]{2,1,0:T(8,128)S(1)}, f32[8,8,128]{2,1,0:T(8,128)S(1)...) custom-call(f32[8]{0:T(128)S(1)} %copy-done.4, ...), custom_call_target="tpu_custom_call" | custom-call | tf_op jit(solution)/shard_map/coarse_statics/pallas_call | solution.py:129
  16.3 4.6 %collective-permute-start.6 = (f32[36,16,128]{2,1,0:T(8,128)S(1)}, f32[36,16,128]{2,1,0:T(8,128)S(1)}, u32[]{:S(2)}, u32[]{:S(2)}) collective-permute-start(f32[36,16,128]{2,1,0:T(8,128)S(1)} %get-tuple-element.83), channel_id=1, source_target_pairs={{0,8},{8,16},{16,24},{1,9},{9,17},{17,25},{2,10},{10,18},{18,26},{... | collective-permute-start | bytes 884744 | tf_op jit(solution)/shard_map/ppermute | solution.py:819
  22.2 4.5 %own_noise.1.g_own = f32[3,2,16,32,256]{4,3,2,1,0:T(8,128)S(1)} custom-call(s32[32,32,256]{2,1,0:T(8,128)S(1)} %copy-done.1), custom_call_target="tpu_custom_call" | custom-call | tf_op jit(solution)/shard_map/own_noise/pallas_call | solution.py:129
  26.8 2.6 %collective-permute-start.5 = (f32[28,4,256]{2,1,0:T(4,128)S(1)}, f32[28,4,256]{2,1,0:T(4,128)S(1)}, u32[]{:S(2)}, u32[]{:S(2)}) collective-permute-start(f32[28,4,256]{2,1,0:T(4,128)S(1)} %get-tuple-element.80), channel_id=1, source_target_pairs={{1,0},{2,1},{3,2},{4,3},{5,4},{6,5},{7,6},{0,7},{9,8},{10,9},{11,1... | collective-permute-start | bytes 344072 | tf_op jit(solution)/shard_map/ppermute | solution.py:819
  34.9 11.1 %fine_start.1 = (f32[6,2,20,40,256]{4,3,2,1,0:T(8,128)S(1)}, f32[2,20,40,256]{3,2,1,0:T(8,128)S(1)}, f32[2,20,40,256]{3,2,1,0:T(8,128)S(1)}, f32[2,20,40,256]{3,...) custom-call(f32[8]{0:T(128)S(1)} %copy-done.4, ...), custom_call_target="tpu_custom_call" | custom-call | tf_op jit(solution)/shard_map/fine_start/pallas_call | solution.py:129
  46.0 2.7 %collective-permute-start.8 = (f32[2,32,256]{2,1,0:T(8,128)S(1)}, f32[2,32,256]{2,1,0:T(8,128)S(1)}, u32[]{:S(2)}, u32[]{:S(2)}) collective-permute-start(f32[2,32,256]{2,1,0:T(8,128)S(1)} %get-tuple-element.110), channel_id=1, source_target_pairs={{0,8},{8,16},{16,24},{24,0},{1,9},{9,17},{17,25},{25,1},{2,10},{10... | collective-permute-start | bytes 196616 | tf_op jit(solution)/shard_map/ppermute | solution.py:819
  50.8 2.3 %collective-permute-done.8.refs_0_.x_lo = f32[2,32,256]{2,1,0:T(8,128)S(1)} collective-permute-done((f32[2,32,256]{2,1,0:T(8,128)S(1)}, f32[2,32,256]{2,1,0:T(8,128)S(1)}, u32[]{:S(2)}, u32[]{:S(2)}) %collective-permute-start.8) | collective-permute-done | bytes 65568 | tf_op jit(solution)/shard_map/ppermute | solution.py:819
  53.8 2.6 %collective-permute-start.11 = (f32[20,4,256]{2,1,0:T(4,128)S(1)}, f32[20,4,256]{2,1,0:T(4,128)S(1)}, u32[]{:S(2)}, u32[]{:S(2)}) collective-permute-start(f32[20,4,256]{2,1,0:T(4,128)S(1)} %get-tuple-element.113), channel_id=1, source_target_pairs={{1,0},{2,1},{3,2},{4,3},{5,4},{6,5},{7,6},{0,7},{9,8},{10,9},{11,1... | collective-permute-start | bytes 245768 | tf_op jit(solution)/shard_map/ppermute | solution.py:819
  56.4 2.8 %collective-permute-done.10.y_lo = f32[20,4,256]{2,1,0:T(4,128)S(1)} collective-permute-done((f32[20,4,256]{2,1,0:T(4,128)S(1)}, f32[20,4,256]{2,1,0:T(4,128)S(1)}, u32[]{:S(2)}, u32[]{:S(2)}) %collective-permute-start.10) | collective-permute-done | bytes 81952 | tf_op jit(solution)/shard_map/ppermute | solution.py:819
  59.2 4.1 %fine_finish.1 = (f32[32,32,256]{2,1,0:T(8,128)}, f32[16,16,128]{2,1,0:T(8,128)S(1)}, f32[8,16,128]{2,1,0:T(8,128)S(1)}, f32[8,16,128]{2,1,0:T(8,128)S(1)}) custom-call(f32[6,2,20,40,256]{4,3,2,1,0:T(8,128)S(1)} %get-tuple-element.105.w_ref, f32[2,20,40,256]{3,2,1,0:T(8,128)S(1)} %get-tuple-element.106.r3_ref, ...), custom_call_target="tpu_custom_call" | custom-call | tf_op jit(solution)/shard_map/fine_finish/pallas_call | solution.py:129
  63.9 3.3 %collective-permute-start.15 = (f32[8,16,128]{2,1,0:T(8,128)S(1)}, f32[8,16,128]{2,1,0:T(8,128)S(1)}, u32[]{:S(2)}, u32[]{:S(2)}) collective-permute-start(f32[8,16,128]{2,1,0:T(8,128)S(1)} %get-tuple-element.119), channel_id=1, source_target_pairs={{8,0},{16,8},{24,16},{0,24},{9,1},{17,9},{25,17},{1,25},{10,2},{18... | collective-permute-start | bytes 196616 | tf_op jit(solution)/shard_map/ppermute | solution.py:819
  67.1 2.9 %collective-permute-done.14.refs_0_.refs_8_ = f32[8,16,128]{2,1,0:T(8,128)S(1)} collective-permute-done((f32[8,16,128]{2,1,0:T(8,128)S(1)}, f32[8,16,128]{2,1,0:T(8,128)S(1)}, u32[]{:S(2)}, u32[]{:S(2)}) %collective-permute-start.14) | collective-permute-done | bytes 65568 | tf_op jit(solution)/shard_map/ppermute | solution.py:819
  70.2 2.6 %collective-permute-start.17 = (f32[32,8,128]{2,1,0:T(8,128)S(1)}, f32[32,8,128]{2,1,0:T(8,128)S(1)}, u32[]{:S(2)}, u32[]{:S(2)}) collective-permute-start(f32[32,8,128]{2,1,0:T(8,128)S(1)} %get-tuple-element.121), channel_id=1, source_target_pairs={{1,0},{2,1},{3,2},{4,3},{5,4},{6,5},{7,6},{0,7},{9,8},{10,9},{11,1... | collective-permute-start | bytes 393224 | tf_op jit(solution)/shard_map/ppermute | solution.py:819
  72.8 2.6 %collective-permute-done.16.refs_10_ = f32[32,8,128]{2,1,0:T(8,128)S(1)} collective-permute-done((f32[32,8,128]{2,1,0:T(8,128)S(1)}, f32[32,8,128]{2,1,0:T(8,128)S(1)}, u32[]{:S(2)}, u32[]{:S(2)}) %collective-permute-start.16) | collective-permute-done | bytes 131104 | tf_op jit(solution)/shard_map/ppermute | solution.py:819
  75.5 5.7 %level_1.1 = (f32[8,8,128]{2,1,0:T(8,128)S(1)}, f32[8,8,128]{2,1,0:T(8,128)S(1)}, f32[8,8,128]{2,1,0:T(8,128)S(1)}) custom-call(f32[16,16,128]{2,1,0:T(8,128)S(1)} %get-tuple-element.93.refs_0_, f32[16,16,128]{2,1,0:T(8,128)S(1)} %get-tuple-element.94.refs_1_, f32[16,16,128]{2,1,0:T(8,128)S(1)} %get-tuple-element.95.refs_2_, ...), custom_call_target="tpu_custom_call" | custom-call | tf_op jit(solution)/shard_map/level_1/pallas_call | solution.py:129
  82.3 2.7 %collective-permute-start.19 = (f32[8,8,128]{2,1,0:T(8,128)S(1)}, f32[8,8,128]{2,1,0:T(8,128)S(1)}, u32[]{:S(2)}, u32[]{:S(2)}) collective-permute-start(f32[8,8,128]{2,1,0:T(8,128)S(1)} %get-tuple-element.124), channel_id=1, source_target_pairs={{8,0},{16,8},{24,16},{0,24},{9,1},{17,9},{25,17},{1,25},{10,2},{18... | collective-permute-start | bytes 98312 | tf_op jit(solution)/shard_map/ppermute | solution.py:819
  87.0 2.6 %collective-permute-start.21 = (f32[24,8,128]{2,1,0:T(8,128)S(1)}, f32[24,8,128]{2,1,0:T(8,128)S(1)}, u32[]{:S(2)}, u32[]{:S(2)}) collective-permute-start(f32[24,8,128]{2,1,0:T(8,128)S(1)} %get-tuple-element.126), channel_id=1, source_target_pairs={{1,0},{2,1},{3,2},{4,3},{5,4},{6,5},{7,6},{0,7},{9,8},{10,9},{11,1... | collective-permute-start | bytes 294920 | tf_op jit(solution)/shard_map/ppermute | solution.py:819
  89.6 2.9 %collective-permute-done.20.refs_10_ = f32[24,8,128]{2,1,0:T(8,128)S(1)} collective-permute-done((f32[24,8,128]{2,1,0:T(8,128)S(1)}, f32[24,8,128]{2,1,0:T(8,128)S(1)}, u32[]{:S(2)}, u32[]{:S(2)}) %collective-permute-start.20) | collective-permute-done | bytes 98336 | tf_op jit(solution)/shard_map/ppermute | solution.py:819
  92.5 3.3 %level_2.1 = f32[4,4,128]{2,1,0:T(4,128)S(1)} custom-call(f32[8,8,128]{2,1,0:T(8,128)S(1)} %get-tuple-element.96.refs_3_.refs_0_, f32[8,8,128]{2,1,0:T(8,128)S(1)} %get-tuple-element.97.refs_4_.refs_1_, f32[8,8,128]{2,1,0:T(8,128)S(1)} %get-tuple-element.98.refs_5_.refs_2_, f32[8,8,128]{2,1,0:T(8,128)S(1)} %get-tuple-element.122.refs_1_.refs_3_, ...), custom_call_target="tpu_custom_call" | custom-call | tf_op jit(solution)/shard_map/level_2/pallas_call | solution.py:129
  100.4 4.4 %collective-permute-done.23 = f32[4,4,128]{2,1,0:T(4,128)S(1)} collective-permute-done((f32[4,4,128]{2,1,0:T(4,128)S(1)}, f32[4,4,128]{2,1,0:T(4,128)S(1)}, u32[]{:S(2)}, u32[]{:S(2)}) %collective-permute-start.23) | collective-permute-done | bytes 8224 | tf_op jit(solution)/shard_map/ppermute | solution.py:827
  112.1 2.7 %level_3.1 = f32[4,4,32]{2,1,0:T(4,128)} custom-call(f32[20,4,128]{2,1,0:T(4,128)S(1)} %collective-permute-done.25.refs_0_, f32[20,4,128]{2,1,0:T(4,128)S(1)} %collective-permute-done.26.refs_1_, f32[20,4,128]{2,1,0:T(4,128)S(1)} %constant_dynamic-update-slice_fusion.refs_2_, f32[20,4,128]{2,1,0:T(4,128)S(1)} %collective-permute-done.27.refs_3_, ...), custom_call_target="tpu_custom_call" | custom-call | tf_op jit(solution)/shard_map/level_3/pallas_call | solution.py:129
  (66 shorter events, 26.8 us)
Async XLA Ops:
  3.1 17.8 %collective-permute-start = (f32[14,32,256]{2,1,0:T(8,128)}, f32[14,32,256]{2,1,0:T(8,128)S(1)}, u32[]{:S(2)}, u32[]{:S(2)}) collective-permute-start(f32[14,32,256]{2,1,0:T(8,128)} %get-tuple-element.65), channel_id=1, source_target_pairs={{0,8},{8,16},{16,24},{1,9},{9,17},{17,25},{2,10},{10,18},{18,26},{... | collective-permute-start | bytes 1376264 | tf_op jit(solution)/shard_map/ppermute | solution.py:819
  8.1 18.5 %collective-permute-start.1 = (f32[14,32,256]{2,1,0:T(8,128)}, f32[14,32,256]{2,1,0:T(8,128)S(1)}, u32[]{:S(2)}, u32[]{:S(2)}) collective-permute-start(f32[14,32,256]{2,1,0:T(8,128)} %get-tuple-element.66), channel_id=1, source_target_pairs={{8,0},{16,8},{24,16},{9,1},{17,9},{25,17},{10,2},{18,10},{26,18},{... | collective-permute-start | bytes 1376264 | tf_op jit(solution)/shard_map/ppermute | solution.py:819
  9.6 20.9 %collective-permute-start.2 = (f32[112,4,256]{2,1,0:T(4,128)S(1)}, f32[112,4,256]{2,1,0:T(4,128)S(1)}, u32[]{:S(2)}, u32[]{:S(2)}) collective-permute-start(f32[112,4,256]{2,1,0:T(4,128)S(1)} %get-tuple-element.77), channel_id=1, source_target_pairs={{0,1},{1,2},{2,3},{3,4},{4,5},{5,6},{6,7},{7,0},{8,9},{9,10},{10,1... | collective-permute-start | bytes 1376264 | tf_op jit(solution)/shard_map/ppermute | solution.py:819
  9.7 20.9 %collective-permute-start.3 = (f32[112,4,256]{2,1,0:T(4,128)S(1)}, f32[112,4,256]{2,1,0:T(4,128)S(1)}, u32[]{:S(2)}, u32[]{:S(2)}) collective-permute-start(f32[112,4,256]{2,1,0:T(4,128)S(1)} %get-tuple-element.78), channel_id=1, source_target_pairs={{1,0},{2,1},{3,2},{4,3},{5,4},{6,5},{7,6},{0,7},{9,8},{10,9},{11,1... | collective-permute-start | bytes 1376264 | tf_op jit(solution)/shard_map/ppermute | solution.py:819
  16.3 10.5 %collective-permute-start.6 = (f32[36,16,128]{2,1,0:T(8,128)S(1)}, f32[36,16,128]{2,1,0:T(8,128)S(1)}, u32[]{:S(2)}, u32[]{:S(2)}) collective-permute-start(f32[36,16,128]{2,1,0:T(8,128)S(1)} %get-tuple-element.83), channel_id=1, source_target_pairs={{0,8},{8,16},{16,24},{1,9},{9,17},{17,25},{2,10},{10,18},{18,26},{... | collective-permute-start | bytes 884744 | tf_op jit(solution)/shard_map/ppermute | solution.py:819
  20.9 9.6 %collective-permute-start.7 = (f32[36,16,128]{2,1,0:T(8,128)S(1)}, f32[36,16,128]{2,1,0:T(8,128)S(1)}, u32[]{:S(2)}, u32[]{:S(2)}) collective-permute-start(f32[36,16,128]{2,1,0:T(8,128)S(1)} %get-tuple-element.84), channel_id=1, source_target_pairs={{8,0},{16,8},{24,16},{9,1},{17,9},{25,17},{10,2},{18,10},{26,18},{... | collective-permute-start | bytes 884744 | tf_op jit(solution)/shard_map/ppermute | solution.py:819
  26.7 5.4 %collective-permute-start.4 = (f32[28,4,256]{2,1,0:T(4,128)S(1)}, f32[28,4,256]{2,1,0:T(4,128)S(1)}, u32[]{:S(2)}, u32[]{:S(2)}) collective-permute-start(f32[28,4,256]{2,1,0:T(4,128)S(1)} %get-tuple-element.79), channel_id=1, source_target_pairs={{0,1},{1,2},{2,3},{3,4},{4,5},{5,6},{6,7},{7,0},{8,9},{9,10},{10,1... | collective-permute-start | bytes 344072 | tf_op jit(solution)/shard_map/ppermute | solution.py:819
  26.8 5.4 %collective-permute-start.5 = (f32[28,4,256]{2,1,0:T(4,128)S(1)}, f32[28,4,256]{2,1,0:T(4,128)S(1)}, u32[]{:S(2)}, u32[]{:S(2)}) collective-permute-start(f32[28,4,256]{2,1,0:T(4,128)S(1)} %get-tuple-element.80), channel_id=1, source_target_pairs={{1,0},{2,1},{3,2},{4,3},{5,4},{6,5},{7,6},{0,7},{9,8},{10,9},{11,1... | collective-permute-start | bytes 344072 | tf_op jit(solution)/shard_map/ppermute | solution.py:819
  32.2 43.2 %collective-permute-start.12 = (f32[168,8,128]{2,1,0:T(8,128)S(1)}, f32[168,8,128]{2,1,0:T(8,128)S(1)}, u32[]{:S(2)}, u32[]{:S(2)}) collective-permute-start(f32[168,8,128]{2,1,0:T(8,128)S(1)} %get-tuple-element.116), channel_id=1, source_target_pairs={{0,1},{1,2},{2,3},{3,4},{4,5},{5,6},{6,7},{7,0},{8,9},{9,10},{10,1... | collective-permute-start | bytes 2064392 | tf_op jit(solution)/shard_map/ppermute | solution.py:819
  33.0 42.5 %collective-permute-start.13 = (f32[168,8,128]{2,1,0:T(8,128)S(1)}, f32[168,8,128]{2,1,0:T(8,128)S(1)}, u32[]{:S(2)}, u32[]{:S(2)}) collective-permute-start(f32[168,8,128]{2,1,0:T(8,128)S(1)} %get-tuple-element.117), channel_id=1, source_target_pairs={{1,0},{2,1},{3,2},{4,3},{5,4},{6,5},{7,6},{0,7},{9,8},{10,9},{11,1... | collective-permute-start | bytes 2064392 | tf_op jit(solution)/shard_map/ppermute | solution.py:819
  46.0 7.1 %collective-permute-start.8 = (f32[2,32,256]{2,1,0:T(8,128)S(1)}, f32[2,32,256]{2,1,0:T(8,128)S(1)}, u32[]{:S(2)}, u32[]{:S(2)}) collective-permute-start(f32[2,32,256]{2,1,0:T(8,128)S(1)} %get-tuple-element.110), channel_id=1, source_target_pairs={{0,8},{8,16},{16,24},{24,0},{1,9},{9,17},{17,25},{25,1},{2,10},{10... | collective-permute-start | bytes 196616 | tf_op jit(solution)/shard_map/ppermute | solution.py:819
  48.7 5.0 %collective-permute-start.9 = (f32[2,32,256]{2,1,0:T(8,128)S(1)}, f32[2,32,256]{2,1,0:T(8,128)S(1)}, u32[]{:S(2)}, u32[]{:S(2)}) collective-permute-start(f32[2,32,256]{2,1,0:T(8,128)S(1)} %get-tuple-element.111), channel_id=1, source_target_pairs={{8,0},{16,8},{24,16},{0,24},{9,1},{17,9},{25,17},{1,25},{10,2},{18... | collective-permute-start | bytes 196616 | tf_op jit(solution)/shard_map/ppermute | solution.py:819
  53.7 5.5 %collective-permute-start.10 = (f32[20,4,256]{2,1,0:T(4,128)S(1)}, f32[20,4,256]{2,1,0:T(4,128)S(1)}, u32[]{:S(2)}, u32[]{:S(2)}) collective-permute-start(f32[20,4,256]{2,1,0:T(4,128)S(1)} %get-tuple-element.112), channel_id=1, source_target_pairs={{0,1},{1,2},{2,3},{3,4},{4,5},{5,6},{6,7},{7,0},{8,9},{9,10},{10,1... | collective-permute-start | bytes 245768 | tf_op jit(solution)/shard_map/ppermute | solution.py:819
  53.8 5.5 %collective-permute-start.11 = (f32[20,4,256]{2,1,0:T(4,128)S(1)}, f32[20,4,256]{2,1,0:T(4,128)S(1)}, u32[]{:S(2)}, u32[]{:S(2)}) collective-permute-start(f32[20,4,256]{2,1,0:T(4,128)S(1)} %get-tuple-element.113), channel_id=1, source_target_pairs={{1,0},{2,1},{3,2},{4,3},{5,4},{6,5},{7,6},{0,7},{9,8},{10,9},{11,1... | collective-permute-start | bytes 245768 | tf_op jit(solution)/shard_map/ppermute | solution.py:819
  63.3 6.8 %collective-permute-start.14 = (f32[8,16,128]{2,1,0:T(8,128)S(1)}, f32[8,16,128]{2,1,0:T(8,128)S(1)}, u32[]{:S(2)}, u32[]{:S(2)}) collective-permute-start(f32[8,16,128]{2,1,0:T(8,128)S(1)} %get-tuple-element.118), channel_id=1, source_target_pairs={{0,8},{8,16},{16,24},{24,0},{1,9},{9,17},{17,25},{25,1},{2,10},{10... | collective-permute-start | bytes 196616 | tf_op jit(solution)/shard_map/ppermute | solution.py:819
  63.9 6.2 %collective-permute-start.15 = (f32[8,16,128]{2,1,0:T(8,128)S(1)}, f32[8,16,128]{2,1,0:T(8,128)S(1)}, u32[]{:S(2)}, u32[]{:S(2)}) collective-permute-start(f32[8,16,128]{2,1,0:T(8,128)S(1)} %get-tuple-element.119), channel_id=1, source_target_pairs={{8,0},{16,8},{24,16},{0,24},{9,1},{17,9},{25,17},{1,25},{10,2},{18... | collective-permute-start | bytes 196616 | tf_op jit(solution)/shard_map/ppermute | solution.py:819
  70.1 5.3 %collective-permute-start.16 = (f32[32,8,128]{2,1,0:T(8,128)S(1)}, f32[32,8,128]{2,1,0:T(8,128)S(1)}, u32[]{:S(2)}, u32[]{:S(2)}) collective-permute-start(f32[32,8,128]{2,1,0:T(8,128)S(1)} %get-tuple-element.120), channel_id=1, source_target_pairs={{0,1},{1,2},{2,3},{3,4},{4,5},{5,6},{6,7},{7,0},{8,9},{9,10},{10,1... | collective-permute-start | bytes 393224 | tf_op jit(solution)/shard_map/ppermute | solution.py:819
  70.2 5.3 %collective-permute-start.17 = (f32[32,8,128]{2,1,0:T(8,128)S(1)}, f32[32,8,128]{2,1,0:T(8,128)S(1)}, u32[]{:S(2)}, u32[]{:S(2)}) collective-permute-start(f32[32,8,128]{2,1,0:T(8,128)S(1)} %get-tuple-element.121), channel_id=1, source_target_pairs={{1,0},{2,1},{3,2},{4,3},{5,4},{6,5},{7,6},{0,7},{9,8},{10,9},{11,1... | collective-permute-start | bytes 393224 | tf_op jit(solution)/shard_map/ppermute | solution.py:819
  81.1 5.8 %collective-permute-start.18 = (f32[8,8,128]{2,1,0:T(8,128)S(1)}, f32[8,8,128]{2,1,0:T(8,128)S(1)}, u32[]{:S(2)}, u32[]{:S(2)}) collective-permute-start(f32[8,8,128]{2,1,0:T(8,128)S(1)} %get-tuple-element.123), channel_id=1, source_target_pairs={{0,8},{8,16},{16,24},{24,0},{1,9},{9,17},{17,25},{25,1},{2,10},{10... | collective-permute-start | bytes 98312 | tf_op jit(solution)/shard_map/ppermute | solution.py:819
  86.9 5.6 %collective-permute-start.20 = (f32[24,8,128]{2,1,0:T(8,128)S(1)}, f32[24,8,128]{2,1,0:T(8,128)S(1)}, u32[]{:S(2)}, u32[]{:S(2)}) collective-permute-start(f32[24,8,128]{2,1,0:T(8,128)S(1)} %get-tuple-element.125), channel_id=1, source_target_pairs={{0,1},{1,2},{2,3},{3,4},{4,5},{5,6},{6,7},{7,0},{8,9},{9,10},{10,1... | collective-permute-start | bytes 294920 | tf_op jit(solution)/shard_map/ppermute | solution.py:819
  87.0 5.5 %collective-permute-start.21 = (f32[24,8,128]{2,1,0:T(8,128)S(1)}, f32[24,8,128]{2,1,0:T(8,128)S(1)}, u32[]{:S(2)}, u32[]{:S(2)}) collective-permute-start(f32[24,8,128]{2,1,0:T(8,128)S(1)} %get-tuple-element.126), channel_id=1, source_target_pairs={{1,0},{2,1},{3,2},{4,3},{5,4},{6,5},{7,6},{0,7},{9,8},{10,9},{11,1... | collective-permute-start | bytes 294920 | tf_op jit(solution)/shard_map/ppermute | solution.py:819
  98.0 6.9 %collective-permute-start.24 = (f32[4,4,128]{2,1,0:T(4,128)S(1)}, f32[4,4,128]{2,1,0:T(4,128)S(1)}, u32[]{:S(2)}, u32[]{:S(2)}) collective-permute-start(f32[4,4,128]{2,1,0:T(4,128)S(1)} %level_2.1), channel_id=1, source_target_pairs={{0,24},{8,0},{16,8},{24,16},{1,25},{9,1},{17,9},{25,17},{2,26},{10... | collective-permute-start | bytes 24584 | tf_op jit(solution)/shard_map/ppermute | solution.py:827
  99.4 5.4 %collective-permute-start.23 = (f32[4,4,128]{2,1,0:T(4,128)S(1)}, f32[4,4,128]{2,1,0:T(4,128)S(1)}, u32[]{:S(2)}, u32[]{:S(2)}) collective-permute-start(f32[4,4,128]{2,1,0:T(4,128)S(1)} %level_2.1), channel_id=1, source_target_pairs={{0,8},{8,16},{16,24},{24,0},{1,9},{9,17},{17,25},{25,1},{2,10},{10... | collective-permute-start | bytes 24584 | tf_op jit(solution)/shard_map/ppermute | solution.py:827
  106.0 6.2 %collective-permute-start.25 = (f32[20,4,128]{2,1,0:T(4,128)S(1)}, f32[20,4,128]{2,1,0:T(4,128)S(1)}, u32[]{:S(2)}, u32[]{:S(2)}) collective-permute-start(f32[20,4,128]{2,1,0:T(4,128)S(1)} %constant_dynamic-update-slice_fusion.refs_2_), channel_id=1, source_target_pairs={{0,2},{1,3},{2,4},{3,5},{4,6},{5,7},{6,0},{7,1},{8,10},{9,11},{10,... | collective-permute-start | bytes 122888 | tf_op jit(solution)/shard_map/ppermute | solution.py:827
  (11 other events, 65.6 us)

commit v6 on v5

--- a/solution.py
+++ b/solution.py
@@ -33,38 +33,34 @@
 SINE = sine_terms(6)
 
 
-def hash_base(seed, which):
+def folded(seed, which):
     gap = 65536 - PRIMES[which]
     v = seed * FACTORS[which]
     v = (v >> 16) * gap + (v & 65535)
-    v = (v >> 16) * gap + (v & 65535)
-    v = jnp.where(v >= PRIMES[which], v - PRIMES[which], v)
-    return v.astype(jnp.float32)
-
-
-def hash_step(base, which, tag):
-    prime = float(PRIMES[which])
-    h = base + float(((tag + 1) * STEPS[which]) % PRIMES[which])
-    return jnp.where(h >= prime, h - prime, h)
-
-
-def raw_noise(base1, base2, tag):
-    h1 = hash_step(base1, 0, tag)
-    h2 = hash_step(base2, 1, tag)
-    u1 = h1 * (1.0 / PRIMES[0]) + 0.5 / PRIMES[0]
-    v = -2.0 * jnp.log(u1)
-    radius = v * lax.rsqrt(v)
-    z = jnp.abs(h2 - float(PRIMES[1] // 2)) * (1.0 / PRIMES[1]) - 0.25
-    zz = z * z
-    poly = jnp.full_like(zz, SINE[-1])
-    for term in SINE[-2::-1]:
-        poly = poly * zz + term
-    return radius * (poly * z)
+    return (v >> 16) * gap + (v & 65535)
 
 
 def raw_noises(seed, level):
-    base1, base2 = hash_base(seed, 0), hash_base(seed, 1)
-    return [raw_noise(base1, base2, level * SWEEPS + t) for t in range(SWEEPS)]
+    prime1, prime2 = PRIMES
+    base1 = folded(seed, 0)
+    base1 = jnp.where(base1 >= prime1, base1 - prime1, base1).astype(jnp.float32)
+    base2 = folded(seed, 1).astype(jnp.float32) * (1.0 / prime2) + 0.5 / prime2
+    noises = []
+    for t in range(SWEEPS):
+        tag = level * SWEEPS + t
+        h1 = base1 + float(((tag + 1) * STEPS[0]) % prime1 - prime1)
+        h1 = jnp.where(h1 < 0.0, h1 + float(prime1), h1)
+        u1 = h1 * (1.0 / prime1) + 0.5 / prime1
+        v = -2.0 * jnp.log(u1)
+        radius = v * lax.rsqrt(v)
+        u2 = jnp.abs(base2 + (((tag + 1) * STEPS[1]) % prime2 / prime2 - 1.0))
+        z = jnp.abs(u2 - 0.5) - 0.25
+        zz = z * z
+        poly = jnp.full_like(zz, SINE[-1])
+        for term in SINE[-2::-1]:
+            poly = poly * zz + term
+        noises.append(radius * (poly * z))
+    return noises
 
 
 def dot32(a, b):
@@ -611,132 +607,143 @@
     return call(kernel, "fine_finish", outs, args, None, scratch, FINISH_LIMIT)
 
 
-def level_sweeps(st, level, pairs, d_refs, m_ref, s_ref, r_ref, w_ref, x_refs, bounds, unroll):
+def prepared(st, level, pairs, d_refs, m_ref, s_ref, v_ref, n_ref, w_ref, unroll):
     def prepare(q):
         for c in range(2):
             diagonal, inverse, weights = st.weights(d_refs, m_ref[c, q], c, q)
             m_ref[c, q] = diagonal
+            v_ref[c, q] = inverse
             for n in range(6):
                 w_ref[n, c, q] = weights[n]
             root = jnp.where(inverse > 0.0, lax.rsqrt(diagonal), 0.0)
-            b = r_ref[0, c, q] * inverse
             for t, g in enumerate(raw_noises(s_ref[c, q].astype(jnp.int32), level)):
-                noise = g * root
-                r_ref[t, c, q] = b + noise
-            s_ref[c, q] = noise
-
-    loop(0, pairs, prepare, min(unroll, 2))
+                n_ref[t, c, q] = g * root
+
+    loop(0, pairs, prepare, unroll)
+
+
+def swept(st, pairs, b_ref, v_ref, n_ref, w_ref, x_refs, bounds, unroll):
+    def update(q, t, c, half):
+        if t == 0:
+            b_ref[c, q] = b_ref[c, q] * v_ref[c, q]
+        total = b_ref[c, q] + n_ref[t, c, q]
+        if half:
+            total = total + st.gathered(x_refs, w_ref, c, q)
+        x_refs[c][q + 1] = total
+
     for half in range(2 * SWEEPS):
         t, c = half // 2, half % 2
-
-        def update(q, t=t, c=c, half=half):
-            if half == 0:
-                x_refs[c][q + 1] = r_ref[t, c, q]
-            else:
-                x_refs[c][q + 1] = r_ref[t, c, q] + st.gathered(x_refs, w_ref, c, q)
-
-        loop(*bounds(half), update, unroll)
-
-
-def level_scratch(pairs, rows, lanes):
-    guarded = pltpu.VMEM((pairs + 2, rows, lanes), jnp.float32)
-    return [
-        guarded,
-        guarded,
-        pltpu.VMEM((2, pairs, rows, lanes), jnp.float32),
-        pltpu.VMEM((2, pairs, rows, lanes), jnp.float32),
-        pltpu.VMEM((SWEEPS, 2, pairs, rows, lanes), jnp.float32),
-        pltpu.VMEM((6, 2, pairs, rows, lanes), jnp.float32),
-        guarded,
-        guarded,
-    ]
-
-
-def middle_level(level, statics, static_planes, static_rows, rhs, rhs_planes, rhs_rows, tail=None):
-    ni, nj, nk = rhs.shape
+        loop(*bounds(half), functools.partial(update, t=t, c=c, half=half), unroll)
+
+
+def middle_static(level, statics, static_planes, static_rows):
+    ni, nj, nk = statics[0].shape
     w = HALO
     h = w // 2
     count, count_j = ni + 2 * w, nj + 2 * w
     pairs = count // 2
-    to_coarsest = level == LEVELS - 2
     plane_base = 0 if level == 1 else 3 * w
     row_base = 0 if level == 1 else 3 * (2 * ni + 2 * w)
 
     def kernel(*refs):
-        refs = list(refs)
-        own = refs[:4]
-        sx_lo, sx_hi, sy_lo, sy_hi, bx_lo, bx_hi, by_lo, by_hi = refs[4:12]
-        at = 12
-        if to_coarsest:
-            tail_ref, out = refs[12:14]
-            at = 14
-        else:
-            out, to_next, to_previous = refs[12:15]
-            at = 15
-        d0, d1, m_ref, s_ref, r_ref, w_ref, x0, x1, t_ref, u_ref = refs[at:]
-        d_refs, x_refs = (d0, d1), (x0, x1)
+        own, (x_lo, x_hi, y_lo, y_hi), refs = refs[:3], refs[3:7], refs[7:]
+        m_ref, v_ref, n_ref, w_ref, d0, d1, s_ref = refs
+        d_refs = (d0, d1)
         shape = (count_j, nk)
         st = Stencil(level, shape)
-        x_has = has_neighbours("gx")
-        y_has = has_neighbours("gy")
+        x_has, y_has = has_neighbours("gx"), has_neighbours("gy")
         zero = jnp.zeros(shape, jnp.float32)
         for g in (0, pairs + 1):
-            for ref in (*d_refs, *x_refs):
+            for ref in d_refs:
                 ref[g] = zero
 
-        def static_plane(src, a, q, k):
+        def plane(src, a, q, k):
             if level == 1:
                 return src[a * w + 2 * q + k]
             return src[plane_base + a * h + q, pl.ds(k * nj, nj)]
 
-        def fields(a, q, k, where):
+        def field(a, q, k, where):
             e = 2 * q + k
             if where == 1:
                 mid = own[a][e - w]
             else:
-                p = q if where == 0 else q - h - ni // 2
-                if a < 3:
-                    mid = static_plane((sx_lo, sx_hi)[where // 2], a, p, k)
-                else:
-                    mid = (bx_lo, bx_hi)[where // 2][2 * p + k]
-                if a == 0:
-                    mid = mid * x_has[where // 2]
-            if a < 3:
-                r = row_base + a * count + e
-                hi, lo = sy_hi[r], sy_lo[r]
-            else:
-                hi, lo = by_hi[e], by_lo[e]
+                mid = plane((x_lo, x_hi)[where // 2], a, q if where == 0 else q - h - ni // 2, k)
+            r = row_base + a * count + e
+            hi, lo = y_hi[r], y_lo[r]
             if a == 0:
                 hi, lo = hi * y_has[1], lo * y_has[0]
                 if where != 1:
-                    hi, lo = hi * x_has[where // 2], lo * x_has[where // 2]
+                    mid, hi, lo = [v * x_has[where // 2] for v in (mid, hi, lo)]
             return jnp.concatenate([mid, hi, lo], axis=0)
 
         def split(q, where):
-            for a in range(4):
-                v = st.whole(fields(a, q, 0, where), fields(a, q, 1, where))
+            for a in range(3):
+                v = st.whole(field(a, q, 0, where), field(a, q, 1, where))
                 for c in range(2):
                     if a == 0:
                         d_refs[c][q + 1] = v[c]
                     else:
-                        (m_ref, s_ref, r_ref.at[0])[a - 1][c, q] = v[c]
+                        (m_ref, s_ref)[a - 1][c, q] = v[c]
 
         loop(0, h, lambda q: split(q, 0), 4)
         loop(h, h + ni // 2, lambda q: split(q, 1), 4)
         loop(h + ni // 2, pairs, lambda q: split(q, 2), 4)
+        prepared(st, level, pairs, d_refs, m_ref, s_ref, v_ref, n_ref, w_ref, 2)
+
+    field_shape = (2, pairs, count_j, nk)
+    outs = [f32(*field_shape), f32(*field_shape), f32(SWEEPS, *field_shape), f32(6, *field_shape)]
+    scratch = [pltpu.VMEM((pairs + 2, count_j, nk), jnp.float32)] * 2
+    scratch += [pltpu.VMEM(field_shape, jnp.float32)]
+    args = [*statics, *static_planes, *static_rows]
+    return call(kernel, f"static_{level}", outs, args, None, scratch)
+
+
+def middle_level(level, state, rhs, planes, rows, tail=None):
+    ni, nj, nk = rhs.shape
+    w = HALO
+    h = w // 2
+    count_j = nj + 2 * w
+    pairs = (ni + 2 * w) // 2
+    to_coarsest = level == LEVELS - 2
+
+    def kernel(m_ref, v_ref, n_ref, w_ref, own, x_lo, x_hi, y_lo, y_hi, *refs):
+        if to_coarsest:
+            tail_ref, out, *refs = refs
+        else:
+            out, to_next, to_previous, *refs = refs
+        b_ref, x0, x1, t_ref, u_ref = refs
+        x_refs = (x0, x1)
+        shape = (count_j, nk)
+        st = Stencil(level, shape)
+        zero = jnp.zeros(shape, jnp.float32)
+        for g in (0, pairs + 1):
+            for ref in x_refs:
+                ref[g] = zero
+
+        def split(q, where):
+            both = []
+            for e in (2 * q, 2 * q + 1):
+                mid = own[e - w] if where == 1 else (x_lo[e] if where == 0 else x_hi[e - w - ni])
+                both.append(jnp.concatenate([mid, y_hi[e], y_lo[e]], axis=0))
+            b_ref[0, q], b_ref[1, q] = st.whole(*both)
+
+        loop(0, h, lambda q: split(q, 0), 4)
+        loop(h, h + ni // 2, lambda q: split(q, 1), 4)
+        loop(h + ni // 2, pairs, lambda q: split(q, 2), 4)
 
         def bounds(half):
             return half // 2, (ni + w + 2 * SWEEPS - half) // 2 + 1
 
-        level_sweeps(st, level, pairs, d_refs, m_ref, s_ref, r_ref, w_ref, x_refs, bounds, 4)
+        swept(st, pairs, b_ref, v_ref, n_ref, w_ref, x_refs, bounds, 4)
+        last = SWEEPS - 1
 
         def residual(q):
-            red = r_ref[SWEEPS - 1, 0, q] - s_ref[0, q] + st.gathered(x_refs, w_ref, 0, q) - x0[q + 1]
-            r_ref[0, 0, q] = m_ref[0, q] * red
-            r_ref[0, 1, q] = -m_ref[1, q] * s_ref[1, q]
+            red = b_ref[0, q] + st.gathered(x_refs, w_ref, 0, q) - x0[q + 1]
+            b_ref[0, q] = m_ref[0, q] * red
+            b_ref[1, q] = -m_ref[1, q] * n_ref[last, 1, q]
 
         loop(h - 1, h + ni // 2, residual, 4)
-        coarse = restricted(st, r_ref.at[0], h, ni, nj, t_ref, u_ref, 4)
+        coarse = restricted(st, b_ref, h, ni, nj, t_ref, u_ref, 4)
         if to_coarsest:
             lanes = nk // 4
             coarse = jnp.where(lax.broadcasted_iota(jnp.int32, coarse.shape, 2) < lanes, coarse, 0.0)
@@ -746,14 +753,16 @@
             to_previous[...] = coarse[:w]
             to_next[...] = coarse[ni // 2 - w :]
 
-    args = [*statics, rhs, *static_planes, *static_rows, *rhs_planes, *rhs_rows]
+    args = [*state, rhs, *planes, *rows]
+    outs = [f32(ni // 2, nj // 2, LANES)]
     if to_coarsest:
         args.append(tail)
-        outs = [f32(ni // 2, nj // 2, LANES)]
     else:
-        outs = [f32(ni // 2, nj // 2, LANES)] + [f32(w, nj // 2, LANES)] * 2
-    scratch = level_scratch(pairs, count_j, nk) + restrict_scratch(ni, count_j, nk)
-    return call(kernel, f"level_{level}", outs, args, None, scratch, LEVEL_LIMIT)
+        outs += [f32(w, nj // 2, LANES)] * 2
+    guarded = pltpu.VMEM((pairs + 2, count_j, nk), jnp.float32)
+    scratch = [pltpu.VMEM((2, pairs, count_j, nk), jnp.float32), guarded, guarded]
+    scratch += restrict_scratch(ni, count_j, nk)
+    return call(kernel, f"level_{level}", outs, args, None, scratch)
 
 
 def coarsest_level(columns, reach, mi, lanes):
@@ -765,7 +774,7 @@
 
     def kernel(*refs):
         blocks = refs[: len(columns)]
-        out, d0, d1, m_ref, s_ref, r_ref, w_ref, x0, x1, t_ref = refs[len(columns) :]
+        out, d0, d1, m_ref, s_ref, b_ref, v_ref, n_ref, w_ref, x0, x1, t_ref = refs[len(columns) :]
         d_refs, x_refs = (d0, d1), (x0, x1)
         shape = (count_j, LANES)
         st = Stencil(level, shape)
@@ -791,7 +800,7 @@
                 d_refs[c][q + 1] = both[c] * (known * here)
                 for a in range(1, 4):
                     v = pltpu.roll(both[c], LANES - a * lanes, 1)
-                    (m_ref, s_ref, r_ref.at[0])[a - 1][c, q] = jnp.where(inside, v, 0.0)
+                    (m_ref, s_ref, b_ref)[a - 1][c, q] = jnp.where(inside, v, 0.0)
 
         loop(0, pairs, split, pairs)
 
@@ -799,14 +808,18 @@
             more = 2 * SWEEPS - 1 - half
             return (reach * mi - more) // 2, (reach * mi + mi - 1 + more) // 2 + 1
 
-        level_sweeps(st, level, pairs, d_refs, m_ref, s_ref, r_ref, w_ref, x_refs, bounds, pairs)
+        prepared(st, level, pairs, d_refs, m_ref, s_ref, v_ref, n_ref, w_ref, 2)
+        swept(st, pairs, b_ref, v_ref, n_ref, w_ref, x_refs, bounds, pairs)
         for n in range(mi // 2):
             p = reach * mi // 2 + n + 1
             for k, v in enumerate(st.whole(x0[p], x1[p])):
                 out[2 * n + k] = v[reach * mj : reach * mj + mj, :lanes]
 
-    scratch = level_scratch(pairs, count_j, LANES)
-    scratch += [pltpu.VMEM((planes, count_j, LANES), jnp.float32)]
+    guarded = pltpu.VMEM((pairs + 2, count_j, LANES), jnp.float32)
+    fields = [(2,), (2,), (2,), (2,), (SWEEPS, 2), (6, 2)]
+    scratch = [guarded, guarded]
+    scratch += [pltpu.VMEM((*lead, pairs, count_j, LANES), jnp.float32) for lead in fields]
+    scratch += [guarded, guarded, pltpu.VMEM((planes, count_j, LANES), jnp.float32)]
     outs = [f32(mi, mj, lanes)]
     (out,) = call(kernel, f"level_{level}", outs, columns, None, scratch, LEVEL_LIMIT)
     return out
@@ -862,17 +875,27 @@
         tables, (class_map, mean_shift, sample_field), noise, planes, (low_noise, high_noise), rows, corners
     )
     planes = both_ways(to_next, to_previous, "gx")
-    rows = both_ways(*pack_rows([(planes[0], black, planes[1])], FINE_HALO, "pack_rows_black"), "gy")
+    messages = pack_rows([(planes[0], black, planes[1])], FINE_HALO, "pack_rows_black")
+    *messages, early, late = lax.optimization_barrier((*messages, *static_rows))
+    static_rows = (early, late)
+    rows = both_ways(*messages, "gy")
+    state1 = middle_static(1, statics1, static_planes, static_rows)
+    *rows, s0, s1, s2, s3 = lax.optimization_barrier((*rows, *state1))
+    states = [(s0, s1, s2, s3)]
 
     fine, rhs, to_next, to_previous = fine_finish(state, black, planes, rows)
+    to_next, to_previous, early, late = lax.optimization_barrier(
+        (to_next, to_previous, *static_rows)
+    )
     for level in range(1, LEVELS - 1):
         planes = both_ways(to_next, to_previous, "gx")
+        if level == 1:
+            state2 = middle_static(2, statics2, static_planes, (early, late))
+            *planes, s0, s1, s2, s3 = lax.optimization_barrier((*planes, *state2))
+            states.append((s0, s1, s2, s3))
         rows = both_ways(*pack_rows([(planes[0], rhs, planes[1])], HALO, f"pack_rows_{level}"), "gy")
-        statics = (statics1, statics2)[level - 1]
         last = level == LEVELS - 2
-        got = middle_level(
-            level, statics, static_planes, static_rows, rhs, planes, rows, tail if last else None
-        )
+        got = middle_level(level, states[level - 1], rhs, planes, rows, tail if last else None)
         if not last:
             rhs, to_next, to_previous = got
     (block,) = got

time: 115 us -> 110 us (0.957)
  waiting for transfers between devices: 27.1 us -> 22.6 us
    ppermute x11, waiting for transfers between devices: 17.1 us -> 12.4 us  [both_ways(): lax.ppermute(to_next, axis, up)]
    pallas_call x15 -> x17, Pallas kernels: 39.1 us -> 38.1 us  [call(): pl.pallas_call(kernel, out_shape=tuple(outs), in_specs=specs or [VMEM] *...]
  transfers between devices with their start and end apart: 29 -> 29, of which waited for: 13 -> 13; matrix products, arithmetic and copies ran while one was open for 0% -> 0% of each run, Pallas kernels for 22% -> 23%
where the time goes in v6:
time: 110 us; the launch traced here: 109 us
  starting transfers between devices  47.7 us (43%)
  Pallas kernels  38.1 us (35%)
  waiting for transfers between devices  22.6 us (21%)
    pallas_call x17, Pallas kernels, call(): pl.pallas_call(kernel, out_shape=tuple(outs), in_specs=specs or [VMEM] *...  38.1 us
    ppermute x11, starting transfers between devices, both_ways(): lax.ppermute(to_previous, axis, down)  25.7 us
    ppermute x11, starting transfers between devices, both_ways(): lax.ppermute(to_next, axis, up)  15 us
    ppermute x11, waiting for transfers between devices, both_ways(): lax.ppermute(to_next, axis, up)  12.4 us
    ppermute x7, waiting for transfers between devices, window(): lax.ppermute(block, axis, [(i, (i - off) % size) for i in range(size)])  9.3 us
    ppermute x7, starting transfers between devices, window(): lax.ppermute(block, axis, [(i, (i - off) % size) for i in range(size)])  6.94 us
  transfers between devices with their start and end apart: 29, of which 13 were waited for; matrix products, arithmetic and copies ran while one was open for 0% of the time, Pallas kernels for 23%

profile of v6, /device:TPU:0, one launch (start us, length us, event | category | flops | bytes accessed | tf_op | source)
XLA Modules:
  0.0 109.4 jit_solution(12078455421637448592)
XLA Ops:
  0.7 2.5 %pack_planes.1 = (f32[14,32,256]{2,1,0:T(8,128)}, f32[14,32,256]{2,1,0:T(8,128)}) custom-call(s32[32,32,256]{2,1,0:T(8,128)} %cls_ref.2, s32[32,32,256]{2,1,0:T(8,128)} %seed_ref.1, f32[32,32,256]{2,1,0:T(8,128)} %b_ref.1, f32[32,32,256]{2,1,0:T(8,128)} %sample.1), custom_call_target="tpu_custom_call" | custom-call | tf_op jit(solution)/shard_map/pack_planes/pallas_call | solution.py:125
  3.1 5.0 %collective-permute-start = (f32[14,32,256]{2,1,0:T(8,128)}, f32[14,32,256]{2,1,0:T(8,128)S(1)}, u32[]{:S(2)}, u32[]{:S(2)}) collective-permute-start(f32[14,32,256]{2,1,0:T(8,128)} %get-tuple-element.93), channel_id=1, source_target_pairs={{0,8},{8,16},{16,24},{1,9},{9,17},{17,25},{2,10},{10,18},{18,26},{... | collective-permute-start | bytes 1376264 | tf_op jit(solution)/shard_map/ppermute | solution.py:832
  9.7 2.6 %collective-permute-start.3 = (f32[112,4,256]{2,1,0:T(4,128)S(1)}, f32[112,4,256]{2,1,0:T(4,128)S(1)}, u32[]{:S(2)}, u32[]{:S(2)}) collective-permute-start(f32[112,4,256]{2,1,0:T(4,128)S(1)} %get-tuple-element.106), channel_id=1, source_target_pairs={{1,0},{2,1},{3,2},{4,3},{5,4},{6,5},{7,6},{0,7},{9,8},{10,9},{11,1... | collective-permute-start | bytes 1376264 | tf_op jit(solution)/shard_map/ppermute | solution.py:832
  12.3 4.0 %coarse_statics.1 = (f32[16,16,128]{2,1,0:T(8,128)S(1)}, f32[16,16,128]{2,1,0:T(8,128)S(1)}, f32[16,16,128]{2,1,0:T(8,128)S(1)}, f32[8,8,128]{2,1,0:T(8,128)S(1)...) custom-call(f32[8]{0:T(128)S(1)} %copy-done.4, ...), custom_call_target="tpu_custom_call" | custom-call | tf_op jit(solution)/shard_map/coarse_statics/pallas_call | solution.py:125
  16.3 4.6 %collective-permute-start.6 = (f32[36,16,128]{2,1,0:T(8,128)S(1)}, f32[36,16,128]{2,1,0:T(8,128)S(1)}, u32[]{:S(2)}, u32[]{:S(2)}) collective-permute-start(f32[36,16,128]{2,1,0:T(8,128)S(1)} %get-tuple-element.111), channel_id=1, source_target_pairs={{0,8},{8,16},{16,24},{1,9},{9,17},{17,25},{2,10},{10,18},{18,26},{... | collective-permute-start | bytes 884744 | tf_op jit(solution)/shard_map/ppermute | solution.py:832
  22.2 4.1 %own_noise.1.g_own = f32[3,2,16,32,256]{4,3,2,1,0:T(8,128)S(1)} custom-call(s32[32,32,256]{2,1,0:T(8,128)S(1)} %copy-done.1), custom_call_target="tpu_custom_call" | custom-call | tf_op jit(solution)/shard_map/own_noise/pallas_call | solution.py:125
  26.4 2.6 %collective-permute-start.5 = (f32[28,4,256]{2,1,0:T(4,128)S(1)}, f32[28,4,256]{2,1,0:T(4,128)S(1)}, u32[]{:S(2)}, u32[]{:S(2)}) collective-permute-start(f32[28,4,256]{2,1,0:T(4,128)S(1)} %get-tuple-element.108), channel_id=1, source_target_pairs={{1,0},{2,1},{3,2},{4,3},{5,4},{6,5},{7,6},{0,7},{9,8},{10,9},{11,1... | collective-permute-start | bytes 344072 | tf_op jit(solution)/shard_map/ppermute | solution.py:832
  34.5 10.9 %fine_start.1 = (f32[6,2,20,40,256]{4,3,2,1,0:T(8,128)S(1)}, f32[2,20,40,256]{3,2,1,0:T(8,128)S(1)}, f32[2,20,40,256]{3,2,1,0:T(8,128)S(1)}, f32[2,20,40,256]{3,...) custom-call(f32[8]{0:T(128)S(1)} %copy-done.4, ...), custom_call_target="tpu_custom_call" | custom-call | tf_op jit(solution)/shard_map/fine_start/pallas_call | solution.py:125
  45.5 2.7 %collective-permute-start.8 = (f32[2,32,256]{2,1,0:T(8,128)S(1)}, f32[2,32,256]{2,1,0:T(8,128)S(1)}, u32[]{:S(2)}, u32[]{:S(2)}) collective-permute-start(f32[2,32,256]{2,1,0:T(8,128)S(1)} %get-tuple-element.138), channel_id=1, source_target_pairs={{0,8},{8,16},{16,24},{24,0},{1,9},{9,17},{17,25},{25,1},{2,10},{10... | collective-permute-start | bytes 196616 | tf_op jit(solution)/shard_map/ppermute | solution.py:832
  48.2 2.1 %collective-permute-start.9 = (f32[2,32,256]{2,1,0:T(8,128)S(1)}, f32[2,32,256]{2,1,0:T(8,128)S(1)}, u32[]{:S(2)}, u32[]{:S(2)}) collective-permute-start(f32[2,32,256]{2,1,0:T(8,128)S(1)} %get-tuple-element.139), channel_id=1, source_target_pairs={{8,0},{16,8},{24,16},{0,24},{9,1},{17,9},{25,17},{1,25},{10,2},{18... | collective-permute-start | bytes 196616 | tf_op jit(solution)/shard_map/ppermute | solution.py:832
  50.3 2.3 %collective-permute-done.8.refs_0_.x_lo = f32[2,32,256]{2,1,0:T(8,128)S(1)} collective-permute-done((f32[2,32,256]{2,1,0:T(8,128)S(1)}, f32[2,32,256]{2,1,0:T(8,128)S(1)}, u32[]{:S(2)}, u32[]{:S(2)}) %collective-permute-start.8) | collective-permute-done | bytes 65568 | tf_op jit(solution)/shard_map/ppermute | solution.py:832
  53.3 2.6 %collective-permute-start.13 = (f32[20,4,256]{2,1,0:T(4,128)S(1)}, f32[20,4,256]{2,1,0:T(4,128)S(1)}, u32[]{:S(2)}, u32[]{:S(2)}) collective-permute-start(f32[20,4,256]{2,1,0:T(4,128)S(1)} %get-tuple-element.145), channel_id=1, source_target_pairs={{1,0},{2,1},{3,2},{4,3},{5,4},{6,5},{7,6},{0,7},{9,8},{10,9},{11,1... | collective-permute-start | bytes 245768 | tf_op jit(solution)/shard_map/ppermute | solution.py:832
  55.9 2.9 %static_1.1 = (f32[2,16,32,128]{3,2,1,0:T(8,128)S(1)}, f32[2,16,32,128]{3,2,1,0:T(8,128)S(1)}, f32[3,2,16,32,128]{4,3,2,1,0:T(8,128)S(1)}, f32[6,2,16,32,128]{4,3,2,1,0:T(8,128)S(1)}) custom-call(f32[16,16,128]{2,1,0:T(8,128)S(1)} %get-tuple-element.121.refs_0_, f32[16,16,128]{2,1,0:T(8,128)S(1)} %get-tuple-element.122.refs_1_, ...), custom_call_target="tpu_custom_call" | custom-call | tf_op jit(solution)/shard_map/static_1/pallas_call | solution.py:125
  58.8 4.1 %fine_finish.1 = (f32[32,32,256]{2,1,0:T(8,128)}, f32[16,16,128]{2,1,0:T(8,128)S(1)}, f32[8,16,128]{2,1,0:T(8,128)S(1)}, f32[8,16,128]{2,1,0:T(8,128)S(1)}) custom-call(f32[6,2,20,40,256]{4,3,2,1,0:T(8,128)S(1)} %get-tuple-element.133.w_ref, f32[2,20,40,256]{3,2,1,0:T(8,128)S(1)} %get-tuple-element.134.r3_ref, ...), custom_call_target="tpu_custom_call" | custom-call | tf_op jit(solution)/shard_map/fine_finish/pallas_call | solution.py:125
  63.8 3.0 %collective-permute-start.15 = (f32[8,16,128]{2,1,0:T(8,128)S(1)}, f32[8,16,128]{2,1,0:T(8,128)S(1)}, u32[]{:S(2)}, u32[]{:S(2)}) collective-permute-start(f32[8,16,128]{2,1,0:T(8,128)S(1)} %get-tuple-element.158), channel_id=1, source_target_pairs={{8,0},{16,8},{24,16},{0,24},{9,1},{17,9},{25,17},{1,25},{10,2},{18... | collective-permute-start | bytes 196616 | tf_op jit(solution)/shard_map/ppermute | solution.py:832
  69.8 2.6 %collective-permute-start.17 = (f32[32,8,128]{2,1,0:T(8,128)S(1)}, f32[32,8,128]{2,1,0:T(8,128)S(1)}, u32[]{:S(2)}, u32[]{:S(2)}) collective-permute-start(f32[32,8,128]{2,1,0:T(8,128)S(1)} %get-tuple-element.177), channel_id=1, source_target_pairs={{1,0},{2,1},{3,2},{4,3},{5,4},{6,5},{7,6},{0,7},{9,8},{10,9},{11,1... | collective-permute-start | bytes 393224 | tf_op jit(solution)/shard_map/ppermute | solution.py:832
  72.4 2.8 %collective-permute-done.16.y_lo = f32[32,8,128]{2,1,0:T(8,128)S(1)} collective-permute-done((f32[32,8,128]{2,1,0:T(8,128)S(1)}, f32[32,8,128]{2,1,0:T(8,128)S(1)}, u32[]{:S(2)}, u32[]{:S(2)}) %collective-permute-start.16) | collective-permute-done | bytes 131104 | tf_op jit(solution)/shard_map/ppermute | solution.py:832
  75.2 2.5 %level_1.1 = (f32[8,8,128]{2,1,0:T(8,128)S(1)}, f32[8,8,128]{2,1,0:T(8,128)S(1)}, f32[8,8,128]{2,1,0:T(8,128)S(1)}) custom-call(f32[2,16,32,128]{3,2,1,0:T(8,128)S(1)} %get-tuple-element.169.m_ref, f32[2,16,32,128]{3,2,1,0:T(8,128)S(1)} %get-tuple-element.170.v_ref, f32[3,2,16,32,128]{4,3,2,1,0:T(8,128)S(1)} %get-tuple-element.171.n_ref, ...), custom_call_target="tpu_custom_call" | custom-call | tf_op jit(solution)/shard_map/level_1/pallas_call | solution.py:125
  78.7 3.0 %collective-permute-start.19 = (f32[8,8,128]{2,1,0:T(8,128)S(1)}, f32[8,8,128]{2,1,0:T(8,128)S(1)}, u32[]{:S(2)}, u32[]{:S(2)}) collective-permute-start(f32[8,8,128]{2,1,0:T(8,128)S(1)} %get-tuple-element.180), channel_id=1, source_target_pairs={{8,0},{16,8},{24,16},{0,24},{9,1},{17,9},{25,17},{1,25},{10,2},{18... | collective-permute-start | bytes 98312 | tf_op jit(solution)/shard_map/ppermute | solution.py:832
  83.6 2.6 %collective-permute-start.21 = (f32[24,8,128]{2,1,0:T(8,128)S(1)}, f32[24,8,128]{2,1,0:T(8,128)S(1)}, u32[]{:S(2)}, u32[]{:S(2)}) collective-permute-start(f32[24,8,128]{2,1,0:T(8,128)S(1)} %get-tuple-element.182), channel_id=1, source_target_pairs={{1,0},{2,1},{3,2},{4,3},{5,4},{6,5},{7,6},{0,7},{9,8},{10,9},{11,1... | collective-permute-start | bytes 294920 | tf_op jit(solution)/shard_map/ppermute | solution.py:832
  86.3 2.8 %collective-permute-done.20.y_lo = f32[24,8,128]{2,1,0:T(8,128)S(1)} collective-permute-done((f32[24,8,128]{2,1,0:T(8,128)S(1)}, f32[24,8,128]{2,1,0:T(8,128)S(1)}, u32[]{:S(2)}, u32[]{:S(2)}) %collective-permute-start.20) | collective-permute-done | bytes 98336 | tf_op jit(solution)/shard_map/ppermute | solution.py:832
  90.5 2.0 %collective-permute-start.22 = (f32[4,4,128]{2,1,0:T(4,128)S(1)}, f32[4,4,128]{2,1,0:T(4,128)S(1)}, u32[]{:S(2)}, u32[]{:S(2)}) collective-permute-start(f32[4,4,128]{2,1,0:T(4,128)S(1)} %level_2.1), channel_id=1, source_target_pairs={{0,16},{8,24},{16,0},{24,8},{1,17},{9,25},{17,1},{25,9},{2,18},{10... | collective-permute-start | bytes 24584 | tf_op jit(solution)/shard_map/ppermute | solution.py:840
  95.1 4.5 %collective-permute-done.23 = f32[4,4,128]{2,1,0:T(4,128)S(1)} collective-permute-done((f32[4,4,128]{2,1,0:T(4,128)S(1)}, f32[4,4,128]{2,1,0:T(4,128)S(1)}, u32[]{:S(2)}, u32[]{:S(2)}) %collective-permute-start.23) | collective-permute-done | bytes 8224 | tf_op jit(solution)/shard_map/ppermute | solution.py:840
  106.8 2.6 %level_3.1 = f32[4,4,32]{2,1,0:T(4,128)} custom-call(f32[20,4,128]{2,1,0:T(4,128)S(1)} %collective-permute-done.25.refs_0_, f32[20,4,128]{2,1,0:T(4,128)S(1)} %collective-permute-done.26.refs_1_, f32[20,4,128]{2,1,0:T(4,128)S(1)} %constant_dynamic-update-slice_fusion.refs_2_, f32[20,4,128]{2,1,0:T(4,128)S(1)} %collective-permute-done.27.refs_3_, ...), custom_call_target="tpu_custom_call" | custom-call | tf_op jit(solution)/shard_map/level_3/pallas_call | solution.py:125
  (68 shorter events, 27.1 us)
Async XLA Ops:
  3.1 17.8 %collective-permute-start = (f32[14,32,256]{2,1,0:T(8,128)}, f32[14,32,256]{2,1,0:T(8,128)S(1)}, u32[]{:S(2)}, u32[]{:S(2)}) collective-permute-start(f32[14,32,256]{2,1,0:T(8,128)} %get-tuple-element.93), channel_id=1, source_target_pairs={{0,8},{8,16},{16,24},{1,9},{9,17},{17,25},{2,10},{10,18},{18,26},{... | collective-permute-start | bytes 1376264 | tf_op jit(solution)/shard_map/ppermute | solution.py:832
  8.1 18.1 %collective-permute-start.1 = (f32[14,32,256]{2,1,0:T(8,128)}, f32[14,32,256]{2,1,0:T(8,128)S(1)}, u32[]{:S(2)}, u32[]{:S(2)}) collective-permute-start(f32[14,32,256]{2,1,0:T(8,128)} %get-tuple-element.94), channel_id=1, source_target_pairs={{8,0},{16,8},{24,16},{9,1},{17,9},{25,17},{10,2},{18,10},{26,18},{... | collective-permute-start | bytes 1376264 | tf_op jit(solution)/shard_map/ppermute | solution.py:832
  9.6 20.8 %collective-permute-start.2 = (f32[112,4,256]{2,1,0:T(4,128)S(1)}, f32[112,4,256]{2,1,0:T(4,128)S(1)}, u32[]{:S(2)}, u32[]{:S(2)}) collective-permute-start(f32[112,4,256]{2,1,0:T(4,128)S(1)} %get-tuple-element.105), channel_id=1, source_target_pairs={{0,1},{1,2},{2,3},{3,4},{4,5},{5,6},{6,7},{7,0},{8,9},{9,10},{10,1... | collective-permute-start | bytes 1376264 | tf_op jit(solution)/shard_map/ppermute | solution.py:832
  9.7 20.7 %collective-permute-start.3 = (f32[112,4,256]{2,1,0:T(4,128)S(1)}, f32[112,4,256]{2,1,0:T(4,128)S(1)}, u32[]{:S(2)}, u32[]{:S(2)}) collective-permute-start(f32[112,4,256]{2,1,0:T(4,128)S(1)} %get-tuple-element.106), channel_id=1, source_target_pairs={{1,0},{2,1},{3,2},{4,3},{5,4},{6,5},{7,6},{0,7},{9,8},{10,9},{11,1... | collective-permute-start | bytes 1376264 | tf_op jit(solution)/shard_map/ppermute | solution.py:832
  16.3 10.0 %collective-permute-start.6 = (f32[36,16,128]{2,1,0:T(8,128)S(1)}, f32[36,16,128]{2,1,0:T(8,128)S(1)}, u32[]{:S(2)}, u32[]{:S(2)}) collective-permute-start(f32[36,16,128]{2,1,0:T(8,128)S(1)} %get-tuple-element.111), channel_id=1, source_target_pairs={{0,8},{8,16},{16,24},{1,9},{9,17},{17,25},{2,10},{10,18},{18,26},{... | collective-permute-start | bytes 884744 | tf_op jit(solution)/shard_map/ppermute | solution.py:832
  20.9 9.5 %collective-permute-start.7 = (f32[36,16,128]{2,1,0:T(8,128)S(1)}, f32[36,16,128]{2,1,0:T(8,128)S(1)}, u32[]{:S(2)}, u32[]{:S(2)}) collective-permute-start(f32[36,16,128]{2,1,0:T(8,128)S(1)} %get-tuple-element.112), channel_id=1, source_target_pairs={{8,0},{16,8},{24,16},{9,1},{17,9},{25,17},{10,2},{18,10},{26,18},{... | collective-permute-start | bytes 884744 | tf_op jit(solution)/shard_map/ppermute | solution.py:832
  26.3 5.4 %collective-permute-start.4 = (f32[28,4,256]{2,1,0:T(4,128)S(1)}, f32[28,4,256]{2,1,0:T(4,128)S(1)}, u32[]{:S(2)}, u32[]{:S(2)}) collective-permute-start(f32[28,4,256]{2,1,0:T(4,128)S(1)} %get-tuple-element.107), channel_id=1, source_target_pairs={{0,1},{1,2},{2,3},{3,4},{4,5},{5,6},{6,7},{7,0},{8,9},{9,10},{10,1... | collective-permute-start | bytes 344072 | tf_op jit(solution)/shard_map/ppermute | solution.py:832
  26.4 5.4 %collective-permute-start.5 = (f32[28,4,256]{2,1,0:T(4,128)S(1)}, f32[28,4,256]{2,1,0:T(4,128)S(1)}, u32[]{:S(2)}, u32[]{:S(2)}) collective-permute-start(f32[28,4,256]{2,1,0:T(4,128)S(1)} %get-tuple-element.108), channel_id=1, source_target_pairs={{1,0},{2,1},{3,2},{4,3},{5,4},{6,5},{7,6},{0,7},{9,8},{10,9},{11,1... | collective-permute-start | bytes 344072 | tf_op jit(solution)/shard_map/ppermute | solution.py:832
  31.9 21.3 %collective-permute-start.10 = (f32[168,8,128]{2,1,0:T(8,128)S(1)}, f32[168,8,128]{2,1,0:T(8,128)S(1)}, u32[]{:S(2)}, u32[]{:S(2)}) collective-permute-start(f32[168,8,128]{2,1,0:T(8,128)S(1)} %get-tuple-element.142), channel_id=1, source_target_pairs={{0,1},{1,2},{2,3},{3,4},{4,5},{5,6},{6,7},{7,0},{8,9},{9,10},{10,1... | collective-permute-start | bytes 2064392 | tf_op jit(solution)/shard_map/ppermute | solution.py:832
  32.6 20.6 %collective-permute-start.11 = (f32[168,8,128]{2,1,0:T(8,128)S(1)}, f32[168,8,128]{2,1,0:T(8,128)S(1)}, u32[]{:S(2)}, u32[]{:S(2)}) collective-permute-start(f32[168,8,128]{2,1,0:T(8,128)S(1)} %get-tuple-element.143), channel_id=1, source_target_pairs={{1,0},{2,1},{3,2},{4,3},{5,4},{6,5},{7,6},{0,7},{9,8},{10,9},{11,1... | collective-permute-start | bytes 2064392 | tf_op jit(solution)/shard_map/ppermute | solution.py:832
  45.5 7.1 %collective-permute-start.8 = (f32[2,32,256]{2,1,0:T(8,128)S(1)}, f32[2,32,256]{2,1,0:T(8,128)S(1)}, u32[]{:S(2)}, u32[]{:S(2)}) collective-permute-start(f32[2,32,256]{2,1,0:T(8,128)S(1)} %get-tuple-element.138), channel_id=1, source_target_pairs={{0,8},{8,16},{16,24},{24,0},{1,9},{9,17},{17,25},{25,1},{2,10},{10... | collective-permute-start | bytes 196616 | tf_op jit(solution)/shard_map/ppermute | solution.py:832
  48.2 5.0 %collective-permute-start.9 = (f32[2,32,256]{2,1,0:T(8,128)S(1)}, f32[2,32,256]{2,1,0:T(8,128)S(1)}, u32[]{:S(2)}, u32[]{:S(2)}) collective-permute-start(f32[2,32,256]{2,1,0:T(8,128)S(1)} %get-tuple-element.139), channel_id=1, source_target_pairs={{8,0},{16,8},{24,16},{0,24},{9,1},{17,9},{25,17},{1,25},{10,2},{18... | collective-permute-start | bytes 196616 | tf_op jit(solution)/shard_map/ppermute | solution.py:832
  53.2 5.6 %collective-permute-start.12 = (f32[20,4,256]{2,1,0:T(4,128)S(1)}, f32[20,4,256]{2,1,0:T(4,128)S(1)}, u32[]{:S(2)}, u32[]{:S(2)}) collective-permute-start(f32[20,4,256]{2,1,0:T(4,128)S(1)} %get-tuple-element.144), channel_id=1, source_target_pairs={{0,1},{1,2},{2,3},{3,4},{4,5},{5,6},{6,7},{7,0},{8,9},{9,10},{10,1... | collective-permute-start | bytes 245768 | tf_op jit(solution)/shard_map/ppermute | solution.py:832
  53.3 5.6 %collective-permute-start.13 = (f32[20,4,256]{2,1,0:T(4,128)S(1)}, f32[20,4,256]{2,1,0:T(4,128)S(1)}, u32[]{:S(2)}, u32[]{:S(2)}) collective-permute-start(f32[20,4,256]{2,1,0:T(4,128)S(1)} %get-tuple-element.145), channel_id=1, source_target_pairs={{1,0},{2,1},{3,2},{4,3},{5,4},{6,5},{7,6},{0,7},{9,8},{10,9},{11,1... | collective-permute-start | bytes 245768 | tf_op jit(solution)/shard_map/ppermute | solution.py:832
  62.9 6.8 %collective-permute-start.14 = (f32[8,16,128]{2,1,0:T(8,128)S(1)}, f32[8,16,128]{2,1,0:T(8,128)S(1)}, u32[]{:S(2)}, u32[]{:S(2)}) collective-permute-start(f32[8,16,128]{2,1,0:T(8,128)S(1)} %get-tuple-element.157), channel_id=1, source_target_pairs={{0,8},{8,16},{16,24},{24,0},{1,9},{9,17},{17,25},{25,1},{2,10},{10... | collective-permute-start | bytes 196616 | tf_op jit(solution)/shard_map/ppermute | solution.py:832
  63.8 5.9 %collective-permute-start.15 = (f32[8,16,128]{2,1,0:T(8,128)S(1)}, f32[8,16,128]{2,1,0:T(8,128)S(1)}, u32[]{:S(2)}, u32[]{:S(2)}) collective-permute-start(f32[8,16,128]{2,1,0:T(8,128)S(1)} %get-tuple-element.158), channel_id=1, source_target_pairs={{8,0},{16,8},{24,16},{0,24},{9,1},{17,9},{25,17},{1,25},{10,2},{18... | collective-permute-start | bytes 196616 | tf_op jit(solution)/shard_map/ppermute | solution.py:832
  69.7 5.5 %collective-permute-start.16 = (f32[32,8,128]{2,1,0:T(8,128)S(1)}, f32[32,8,128]{2,1,0:T(8,128)S(1)}, u32[]{:S(2)}, u32[]{:S(2)}) collective-permute-start(f32[32,8,128]{2,1,0:T(8,128)S(1)} %get-tuple-element.176), channel_id=1, source_target_pairs={{0,1},{1,2},{2,3},{3,4},{4,5},{5,6},{6,7},{7,0},{8,9},{9,10},{10,1... | collective-permute-start | bytes 393224 | tf_op jit(solution)/shard_map/ppermute | solution.py:832
  69.8 5.4 %collective-permute-start.17 = (f32[32,8,128]{2,1,0:T(8,128)S(1)}, f32[32,8,128]{2,1,0:T(8,128)S(1)}, u32[]{:S(2)}, u32[]{:S(2)}) collective-permute-start(f32[32,8,128]{2,1,0:T(8,128)S(1)} %get-tuple-element.177), channel_id=1, source_target_pairs={{1,0},{2,1},{3,2},{4,3},{5,4},{6,5},{7,6},{0,7},{9,8},{10,9},{11,1... | collective-permute-start | bytes 393224 | tf_op jit(solution)/shard_map/ppermute | solution.py:832
  77.8 5.8 %collective-permute-start.18 = (f32[8,8,128]{2,1,0:T(8,128)S(1)}, f32[8,8,128]{2,1,0:T(8,128)S(1)}, u32[]{:S(2)}, u32[]{:S(2)}) collective-permute-start(f32[8,8,128]{2,1,0:T(8,128)S(1)} %get-tuple-element.179), channel_id=1, source_target_pairs={{0,8},{8,16},{16,24},{24,0},{1,9},{9,17},{17,25},{25,1},{2,10},{10... | collective-permute-start | bytes 98312 | tf_op jit(solution)/shard_map/ppermute | solution.py:832
  83.6 5.5 %collective-permute-start.20 = (f32[24,8,128]{2,1,0:T(8,128)S(1)}, f32[24,8,128]{2,1,0:T(8,128)S(1)}, u32[]{:S(2)}, u32[]{:S(2)}) collective-permute-start(f32[24,8,128]{2,1,0:T(8,128)S(1)} %get-tuple-element.181), channel_id=1, source_target_pairs={{0,1},{1,2},{2,3},{3,4},{4,5},{5,6},{6,7},{7,0},{8,9},{9,10},{10,1... | collective-permute-start | bytes 294920 | tf_op jit(solution)/shard_map/ppermute | solution.py:832
  83.6 5.4 %collective-permute-start.21 = (f32[24,8,128]{2,1,0:T(8,128)S(1)}, f32[24,8,128]{2,1,0:T(8,128)S(1)}, u32[]{:S(2)}, u32[]{:S(2)}) collective-permute-start(f32[24,8,128]{2,1,0:T(8,128)S(1)} %get-tuple-element.182), channel_id=1, source_target_pairs={{1,0},{2,1},{3,2},{4,3},{5,4},{6,5},{7,6},{0,7},{9,8},{10,9},{11,1... | collective-permute-start | bytes 294920 | tf_op jit(solution)/shard_map/ppermute | solution.py:832
  92.5 7.1 %collective-permute-start.24 = (f32[4,4,128]{2,1,0:T(4,128)S(1)}, f32[4,4,128]{2,1,0:T(4,128)S(1)}, u32[]{:S(2)}, u32[]{:S(2)}) collective-permute-start(f32[4,4,128]{2,1,0:T(4,128)S(1)} %level_2.1), channel_id=1, source_target_pairs={{0,24},{8,0},{16,8},{24,16},{1,25},{9,1},{17,9},{25,17},{2,26},{10... | collective-permute-start | bytes 24584 | tf_op jit(solution)/shard_map/ppermute | solution.py:840
  94.1 5.4 %collective-permute-start.23 = (f32[4,4,128]{2,1,0:T(4,128)S(1)}, f32[4,4,128]{2,1,0:T(4,128)S(1)}, u32[]{:S(2)}, u32[]{:S(2)}) collective-permute-start(f32[4,4,128]{2,1,0:T(4,128)S(1)} %level_2.1), channel_id=1, source_target_pairs={{0,8},{8,16},{16,24},{24,0},{1,9},{9,17},{17,25},{25,1},{2,10},{10... | collective-permute-start | bytes 24584 | tf_op jit(solution)/shard_map/ppermute | solution.py:840
  100.8 6.0 %collective-permute-start.25 = (f32[20,4,128]{2,1,0:T(4,128)S(1)}, f32[20,4,128]{2,1,0:T(4,128)S(1)}, u32[]{:S(2)}, u32[]{:S(2)}) collective-permute-start(f32[20,4,128]{2,1,0:T(4,128)S(1)} %constant_dynamic-update-slice_fusion.refs_2_), channel_id=1, source_target_pairs={{0,2},{1,3},{2,4},{3,5},{4,6},{5,7},{6,0},{7,1},{8,10},{9,11},{10,... | collective-permute-start | bytes 122888 | tf_op jit(solution)/shard_map/ppermute | solution.py:840
  (11 other events, 65.9 us)

commit v7 on v6

--- a/solution.py
+++ b/solution.py
@@ -78,7 +78,23 @@
     return jnp.where(k == half, 0.25, jnp.where(near, 0.125, 0.0))
 
 
-def lookups(numbers, tables):
+def spread_table(table, rows):
+    lane = lax.broadcasted_iota(jnp.int32, (rows, LANES), 1)
+    result = jnp.zeros((rows, LANES), jnp.float32)
+    for n in range(table.shape[0]):
+        result = jnp.where(lane == n + 1, table[n], result)
+    return result
+
+
+def lookup(numbers, lanes_table):
+    parts = []
+    for at in range(0, numbers.shape[1], LANES):
+        index = numbers[:, at : at + LANES]
+        parts.append(jnp.take_along_axis(lanes_table, index, axis=1, mode="promise_in_bounds"))
+    return jnp.concatenate(parts, axis=1)
+
+
+def selected(numbers, tables):
     results = [jnp.zeros(numbers.shape, jnp.float32) for _ in tables]
     for n in range(tables[0].shape[0]):
         hit = numbers == n + 1
@@ -105,6 +121,11 @@
 
 def checker(shape):
     return ((lax.broadcasted_iota(jnp.int32, shape, 0) + lax.broadcasted_iota(jnp.int32, shape, 1)) & 1) == 0
+
+
+def swap_starts(axis, length, w):
+    even = lax.axis_index(axis) % 2 == 0
+    return jnp.where(even, length - w, 0), jnp.where(even, 0, length - w)
 
 
 def has_neighbours(axis):
@@ -141,7 +162,7 @@
     def kernel(*refs):
         sources, outs, (whole_ref, real_ref, sems) = refs[:4], refs[4:6], refs[6:]
         copies = []
-        for side, start in enumerate((ni - w, 0)):
+        for side, start in enumerate(swap_starts("gx", ni, w)):
             for a, source in enumerate(sources):
                 target = (whole_ref, real_ref)[a // 2].at[side, a % 2]
                 copy = pltpu.make_async_copy(source.at[pl.ds(start, w)], target, sems.at[side, a])
@@ -241,7 +262,8 @@
     w = HALO
 
     def kernel(d_tab, m_tab, cls_ref, seed_ref, *refs):
-        outs, (to_next, to_previous, packed), (t_ref, u_ref) = refs[:6], refs[6:9], refs[9:]
+        outs, (to_even, to_odd, packed), (t_ref, u_ref) = refs[:6], refs[6:9], refs[9:]
+        spread = [spread_table(table, nj) for table in (d_tab, m_tab)]
         for level in range(1, LEVELS):
             mi, mj, mk = shapes[level - 1]
             rows = mi // 2 * mj
@@ -251,10 +273,8 @@
                 def gather(q):
                     if level == 1:
                         if what < 2:
-                            tab = (d_tab, m_tab)[what]
-                            (a,) = lookups(cls_ref[2 * q] + 1, [tab])
-                            (b,) = lookups(cls_ref[2 * q + 1] + 1, [tab])
-                            a = a + b
+                            a = lookup(cls_ref[2 * q] + 1, spread[what])
+                            a = a + lookup(cls_ref[2 * q + 1] + 1, spread[what])
                         else:
                             a = seed_ref[2 * q].astype(jnp.float32)
                     else:
@@ -280,15 +300,16 @@
                     total = even if what == 0 else total + even
         packed[...] = total.reshape(shapes[-1][0], shapes[-1][1], LANES)
         mj = shapes[1][1]
+        starts1 = swap_starts("gx", shapes[1][0], w)
+        starts2 = swap_starts("gx", shapes[2][0], w)
         for what in range(3):
             one, two = outs[what], outs[3 + what]
-            for e in range(w):
-                to_previous[what * w + e] = one[e]
-                to_next[what * w + e] = one[shapes[1][0] - w + e]
-                n = what * w + e
-                at = (3 * w + n // 2, pl.ds(n % 2 * (mj // 2), mj // 2))
-                to_previous[at] = two[e]
-                to_next[at] = two[shapes[2][0] - w + e]
+            for out, start1, start2 in zip((to_even, to_odd), starts1, starts2):
+                for e in range(w):
+                    out[what * w + e] = one[start1 + e]
+                    n = what * w + e
+                    at = (3 * w + n // 2, pl.ds(n % 2 * (mj // 2), mj // 2))
+                    out[at] = two[start2 + e]
 
     outs = []
     for level in range(1, LEVELS - 1):
@@ -482,7 +503,7 @@
             seeds = [edge(1, e[c], where) for c in range(2)]
             for c in range(2):
                 number = jnp.where(even, cls[c], cls[1 - c]).astype(jnp.int32)
-                d, m = lookups(number, [d_tab, m_tab])
+                d, m = selected(number, (d_tab, m_tab))
                 d_refs[c][q + 1] = d
                 m_ref[c, q] = m
                 r_ref[0, c, q] = jnp.where(even, b[c], b[1 - c])
@@ -832,6 +853,33 @@
     return lax.ppermute(to_next, axis, up), lax.ppermute(to_previous, axis, down)
 
 
+def swapped(first, second, axis):
+    size = lax.axis_size(axis)
+
+    def partner(i, start):
+        j = i + 1 if i % 2 == start else i - 1
+        return j if 0 <= j < size else i
+
+    got = [
+        lax.ppermute(block, axis, [(i, partner(i, start)) for i in range(size)])
+        for start, block in enumerate((first, second))
+    ]
+
+    def kernel(a, b, low, high):
+        even = lax.axis_index(axis) % 2 == 0
+        has_low, has_high = has_neighbours(axis)
+        up = jnp.where(even, 1.0, 0.0)
+
+        def body(n):
+            one, two = a[n], b[n]
+            low[n] = jnp.where(up > 0.0, two, one) * has_low
+            high[n] = jnp.where(up > 0.0, one, two) * has_high
+
+        loop(0, first.shape[0], body, 2)
+
+    return got, lambda pair: call(kernel, "put_in_order", [f32(*first.shape)] * 2, pair)
+
+
 def window(block, axis, reach):
     size = lax.axis_size(axis)
     got = {0: block}
@@ -846,7 +894,7 @@
     nk = class_map.shape[2]
     arrays = (class_map, noise_seed, mean_shift, sample_field)
 
-    planes = both_ways(*pack_planes(*arrays), "gx", False)
+    planes, in_order = swapped(*pack_planes(*arrays), "gx")
     *rows, classes, seed = lax.optimization_barrier(
         (*pack_rows_fine(*arrays), class_map, noise_seed)
     )
@@ -855,16 +903,17 @@
     seed, static_next, static_previous = lax.optimization_barrier(
         (noise_seed, static_next, static_previous)
     )
-    static_planes = both_ways(static_next, static_previous, "gx", False)
+    static_planes, static_in_order = swapped(static_next, static_previous, "gx")
     noise = own_noise(seed)
     *planes, noise = lax.optimization_barrier((*planes, noise))
+    planes = in_order(planes)
 
     corners = both_ways(*pack_rows([planes], FINE_HALO, "pack_corners"), "gy")
     plane_noise = halo_noise(*planes)
     *early, low_noise, high_noise, static_low, static_high = lax.optimization_barrier(
         (*rows, *corners, *plane_noise, *static_planes)
     )
-    static_planes = (static_low, static_high)
+    static_planes = static_in_order((static_low, static_high))
     *early, static_next, static_previous = lax.optimization_barrier(
         (*early, *pack_static_rows(static_planes, statics1, statics2))
     )

time: 110 us -> 106 us (0.964)
  starting transfers between devices: 47.7 us -> 43.2 us
  waiting for transfers between devices: 22.6 us -> 23.8 us
    ppermute x11 -> x9, starting transfers between devices: 15 us -> 5.53 us  [both_ways(): lax.ppermute(to_next, axis, up)]
    ppermute x0 -> x4, starting transfers between devices: none -> 9.01 us  [swapped(): lax.ppermute(block, axis, [(i, partner(i, start)) for i in range(size)])]
    ppermute x11 -> x9, starting transfers between devices: 25.7 us -> 21.2 us  [both_ways(): lax.ppermute(to_previous, axis, down)]
    ppermute x0 -> x4, waiting for transfers between devices: none -> 1.17 us  [swapped(): lax.ppermute(block, axis, [(i, partner(i, start)) for i in range(size)])]
    ppermute x7, waiting for transfers between devices: 9.3 us -> 8.14 us  [window(): lax.ppermute(block, axis, [(i, (i - off) % size) for i in range(size)])]
    ppermute x11 -> x9, waiting for transfers between devices: 12.4 us -> 12.6 us  [both_ways(): lax.ppermute(to_next, axis, up)]
    pallas_call x17 -> x19, Pallas kernels: 38.1 us -> 38.2 us  [call(): pl.pallas_call(kernel, out_shape=tuple(outs), in_specs=specs or [VMEM] *...]
where the time goes in v7:
time: 106 us
  starting transfers between devices  43.2 us (41%)
  Pallas kernels  38.2 us (36%)
  waiting for transfers between devices  23.8 us (22%)
    pallas_call x19, Pallas kernels, call(): pl.pallas_call(kernel, out_shape=tuple(outs), in_specs=specs or [VMEM] *...  38.2 us
    ppermute x9, starting transfers between devices, both_ways(): lax.ppermute(to_previous, axis, down)  21.2 us
    ppermute x9, waiting for transfers between devices, both_ways(): lax.ppermute(to_next, axis, up)  12.6 us
    ppermute x4, starting transfers between devices, swapped(): lax.ppermute(block, axis, [(i, partner(i, start)) for i in range(size)])  9.01 us
    ppermute x7, waiting for transfers between devices, window(): lax.ppermute(block, axis, [(i, (i - off) % size) for i in range(size)])  8.14 us
    ppermute x7, starting transfers between devices, window(): lax.ppermute(block, axis, [(i, (i - off) % size) for i in range(size)])  7.42 us
    ppermute x9, starting transfers between devices, both_ways(): lax.ppermute(to_next, axis, up)  5.53 us
  transfers between devices with their start and end apart: 29, of which 13 were waited for; matrix products, arithmetic and copies ran while one was open for 0% of the time, Pallas kernels for 23%

profile of v7, /device:TPU:0, one launch (start us, length us, event | category | flops | bytes accessed | tf_op | source)
XLA Modules:
  0.0 106.1 jit_solution(3496230144738533334)
XLA Ops:
  0.7 2.5 %pack_planes.1 = (f32[14,32,256]{2,1,0:T(8,128)}, f32[14,32,256]{2,1,0:T(8,128)}) custom-call(s32[32,32,256]{2,1,0:T(8,128)} %cls_ref.2, s32[32,32,256]{2,1,0:T(8,128)} %seed_ref.1, f32[32,32,256]{2,1,0:T(8,128)} %b_ref.1, f32[32,32,256]{2,1,0:T(8,128)} %sample.1), custom_call_target="tpu_custom_call" | custom-call | tf_op jit(solution)/shard_map/pack_planes/pallas_call | solution.py:146
  3.2 3.1 %collective-permute-start = (f32[14,32,256]{2,1,0:T(8,128)}, f32[14,32,256]{2,1,0:T(8,128)S(1)}, u32[]{:S(2)}, u32[]{:S(2)}) collective-permute-start(f32[14,32,256]{2,1,0:T(8,128)} %get-tuple-element.97), channel_id=1, source_target_pairs={{0,8},{8,0},{16,24},{24,16},{1,9},{9,1},{17,25},{25,17},{2,10},{10... | collective-permute-start | bytes 1376264 | tf_op jit(solution)/shard_map/ppermute | solution.py:864
  8.3 2.6 %collective-permute-start.3 = (f32[112,4,256]{2,1,0:T(4,128)S(1)}, f32[112,4,256]{2,1,0:T(4,128)S(1)}, u32[]{:S(2)}, u32[]{:S(2)}) collective-permute-start(f32[112,4,256]{2,1,0:T(4,128)S(1)} %get-tuple-element.112), channel_id=1, source_target_pairs={{1,0},{2,1},{3,2},{4,3},{5,4},{6,5},{7,6},{0,7},{9,8},{10,9},{11,1... | collective-permute-start | bytes 1376264 | tf_op jit(solution)/shard_map/ppermute | solution.py:853
  10.9 3.8 %coarse_statics.1 = (f32[16,16,128]{2,1,0:T(8,128)S(1)}, f32[16,16,128]{2,1,0:T(8,128)S(1)}, f32[16,16,128]{2,1,0:T(8,128)S(1)}, f32[8,8,128]{2,1,0:T(8,128)S(1)...) custom-call(f32[8]{0:T(128)S(1)} %copy-done.4, ...), custom_call_target="tpu_custom_call" | custom-call | tf_op jit(solution)/shard_map/coarse_statics/pallas_call | solution.py:146
  14.7 3.4 %collective-permute-start.6 = (f32[36,16,128]{2,1,0:T(8,128)S(1)}, f32[36,16,128]{2,1,0:T(8,128)S(1)}, u32[]{:S(2)}, u32[]{:S(2)}) collective-permute-start(f32[36,16,128]{2,1,0:T(8,128)S(1)} %get-tuple-element.117), channel_id=1, source_target_pairs={{0,8},{8,0},{16,24},{24,16},{1,9},{9,1},{17,25},{25,17},{2,10},{10... | collective-permute-start | bytes 884744 | tf_op jit(solution)/shard_map/ppermute | solution.py:864
  18.8 4.1 %own_noise.1.g_own = f32[3,2,16,32,256]{4,3,2,1,0:T(8,128)S(1)} custom-call(s32[32,32,256]{2,1,0:T(8,128)S(1)} %copy-done.1), custom_call_target="tpu_custom_call" | custom-call | tf_op jit(solution)/shard_map/own_noise/pallas_call | solution.py:146
  31.2 11.0 %fine_start.1 = (f32[6,2,20,40,256]{4,3,2,1,0:T(8,128)S(1)}, f32[2,20,40,256]{3,2,1,0:T(8,128)S(1)}, f32[2,20,40,256]{3,2,1,0:T(8,128)S(1)}, f32[2,20,40,256]{3,...) custom-call(f32[8]{0:T(128)S(1)} %copy-done.4, ...), custom_call_target="tpu_custom_call" | custom-call | tf_op jit(solution)/shard_map/fine_start/pallas_call | solution.py:146
  42.2 4.1 %collective-permute-start.8 = (f32[2,32,256]{2,1,0:T(8,128)S(1)}, f32[2,32,256]{2,1,0:T(8,128)S(1)}, u32[]{:S(2)}, u32[]{:S(2)}) collective-permute-start(f32[2,32,256]{2,1,0:T(8,128)S(1)} %get-tuple-element.146), channel_id=1, source_target_pairs={{0,8},{8,16},{16,24},{24,0},{1,9},{9,17},{17,25},{25,1},{2,10},{10... | collective-permute-start | bytes 196616 | tf_op jit(solution)/shard_map/ppermute | solution.py:853
  46.3 2.5 %collective-permute-done.8.refs_0_.x_lo = f32[2,32,256]{2,1,0:T(8,128)S(1)} collective-permute-done((f32[2,32,256]{2,1,0:T(8,128)S(1)}, f32[2,32,256]{2,1,0:T(8,128)S(1)}, u32[]{:S(2)}, u32[]{:S(2)}) %collective-permute-start.8) | collective-permute-done | bytes 65568 | tf_op jit(solution)/shard_map/ppermute | solution.py:853
  50.6 2.6 %collective-permute-start.13 = (f32[20,4,256]{2,1,0:T(4,128)S(1)}, f32[20,4,256]{2,1,0:T(4,128)S(1)}, u32[]{:S(2)}, u32[]{:S(2)}) collective-permute-start(f32[20,4,256]{2,1,0:T(4,128)S(1)} %get-tuple-element.153), channel_id=1, source_target_pairs={{1,0},{2,1},{3,2},{4,3},{5,4},{6,5},{7,6},{0,7},{9,8},{10,9},{11,1... | collective-permute-start | bytes 245768 | tf_op jit(solution)/shard_map/ppermute | solution.py:853
  53.3 2.9 %static_1.1 = (f32[2,16,32,128]{3,2,1,0:T(8,128)S(1)}, f32[2,16,32,128]{3,2,1,0:T(8,128)S(1)}, f32[3,2,16,32,128]{4,3,2,1,0:T(8,128)S(1)}, f32[6,2,16,32,128]{4,3,2,1,0:T(8,128)S(1)}) custom-call(f32[16,16,128]{2,1,0:T(8,128)S(1)} %get-tuple-element.129.refs_0_, f32[16,16,128]{2,1,0:T(8,128)S(1)} %get-tuple-element.130.refs_1_, ...), custom_call_target="tpu_custom_call" | custom-call | tf_op jit(solution)/shard_map/static_1/pallas_call | solution.py:146
  56.2 4.1 %fine_finish.1 = (f32[32,32,256]{2,1,0:T(8,128)}, f32[16,16,128]{2,1,0:T(8,128)S(1)}, f32[8,16,128]{2,1,0:T(8,128)S(1)}, f32[8,16,128]{2,1,0:T(8,128)S(1)}) custom-call(f32[6,2,20,40,256]{4,3,2,1,0:T(8,128)S(1)} %get-tuple-element.141.w_ref, f32[2,20,40,256]{3,2,1,0:T(8,128)S(1)} %get-tuple-element.142.r3_ref, ...), custom_call_target="tpu_custom_call" | custom-call | tf_op jit(solution)/shard_map/fine_finish/pallas_call | solution.py:146
  60.4 3.8 %collective-permute-start.15 = (f32[8,16,128]{2,1,0:T(8,128)S(1)}, f32[8,16,128]{2,1,0:T(8,128)S(1)}, u32[]{:S(2)}, u32[]{:S(2)}) collective-permute-start(f32[8,16,128]{2,1,0:T(8,128)S(1)} %get-tuple-element.166), channel_id=1, source_target_pairs={{8,0},{16,8},{24,16},{0,24},{9,1},{17,9},{25,17},{1,25},{10,2},{18... | collective-permute-start | bytes 196616 | tf_op jit(solution)/shard_map/ppermute | solution.py:853
  67.0 2.6 %collective-permute-start.17 = (f32[32,8,128]{2,1,0:T(8,128)S(1)}, f32[32,8,128]{2,1,0:T(8,128)S(1)}, u32[]{:S(2)}, u32[]{:S(2)}) collective-permute-start(f32[32,8,128]{2,1,0:T(8,128)S(1)} %get-tuple-element.185), channel_id=1, source_target_pairs={{1,0},{2,1},{3,2},{4,3},{5,4},{6,5},{7,6},{0,7},{9,8},{10,9},{11,1... | collective-permute-start | bytes 393224 | tf_op jit(solution)/shard_map/ppermute | solution.py:853
  69.6 3.3 %collective-permute-done.16.y_lo = f32[32,8,128]{2,1,0:T(8,128)S(1)} collective-permute-done((f32[32,8,128]{2,1,0:T(8,128)S(1)}, f32[32,8,128]{2,1,0:T(8,128)S(1)}, u32[]{:S(2)}, u32[]{:S(2)}) %collective-permute-start.16) | collective-permute-done | bytes 131104 | tf_op jit(solution)/shard_map/ppermute | solution.py:853
  73.0 2.5 %level_1.1 = (f32[8,8,128]{2,1,0:T(8,128)S(1)}, f32[8,8,128]{2,1,0:T(8,128)S(1)}, f32[8,8,128]{2,1,0:T(8,128)S(1)}) custom-call(f32[2,16,32,128]{3,2,1,0:T(8,128)S(1)} %get-tuple-element.177.m_ref, f32[2,16,32,128]{3,2,1,0:T(8,128)S(1)} %get-tuple-element.178.v_ref, f32[3,2,16,32,128]{4,3,2,1,0:T(8,128)S(1)} %get-tuple-element.179.n_ref, ...), custom_call_target="tpu_custom_call" | custom-call | tf_op jit(solution)/shard_map/level_1/pallas_call | solution.py:146
  75.6 3.8 %collective-permute-start.19 = (f32[8,8,128]{2,1,0:T(8,128)S(1)}, f32[8,8,128]{2,1,0:T(8,128)S(1)}, u32[]{:S(2)}, u32[]{:S(2)}) collective-permute-start(f32[8,8,128]{2,1,0:T(8,128)S(1)} %get-tuple-element.188), channel_id=1, source_target_pairs={{8,0},{16,8},{24,16},{0,24},{9,1},{17,9},{25,17},{1,25},{10,2},{18... | collective-permute-start | bytes 98312 | tf_op jit(solution)/shard_map/ppermute | solution.py:853
  79.4 1.9 %collective-permute-done.18.refs_0_.x_lo = f32[8,8,128]{2,1,0:T(8,128)S(1)} collective-permute-done((f32[8,8,128]{2,1,0:T(8,128)S(1)}, f32[8,8,128]{2,1,0:T(8,128)S(1)}, u32[]{:S(2)}, u32[]{:S(2)}) %collective-permute-start.18) | collective-permute-done | bytes 32800 | tf_op jit(solution)/shard_map/ppermute | solution.py:853
  81.3 2.6 %collective-permute-start.21 = (f32[24,8,128]{2,1,0:T(8,128)S(1)}, f32[24,8,128]{2,1,0:T(8,128)S(1)}, u32[]{:S(2)}, u32[]{:S(2)}) collective-permute-start(f32[24,8,128]{2,1,0:T(8,128)S(1)} %get-tuple-element.190), channel_id=1, source_target_pairs={{1,0},{2,1},{3,2},{4,3},{5,4},{6,5},{7,6},{0,7},{9,8},{10,9},{11,1... | collective-permute-start | bytes 294920 | tf_op jit(solution)/shard_map/ppermute | solution.py:853
  84.0 2.4 %collective-permute-done.20.y_lo = f32[24,8,128]{2,1,0:T(8,128)S(1)} collective-permute-done((f32[24,8,128]{2,1,0:T(8,128)S(1)}, f32[24,8,128]{2,1,0:T(8,128)S(1)}, u32[]{:S(2)}, u32[]{:S(2)}) %collective-permute-start.20) | collective-permute-done | bytes 98336 | tf_op jit(solution)/shard_map/ppermute | solution.py:853
  87.9 2.4 %collective-permute-start.22 = (f32[4,4,128]{2,1,0:T(4,128)S(1)}, f32[4,4,128]{2,1,0:T(4,128)S(1)}, u32[]{:S(2)}, u32[]{:S(2)}) collective-permute-start(f32[4,4,128]{2,1,0:T(4,128)S(1)} %level_2.1), channel_id=1, source_target_pairs={{0,16},{8,24},{16,0},{24,8},{1,17},{9,25},{17,1},{25,9},{2,18},{10... | collective-permute-start | bytes 24584 | tf_op jit(solution)/shard_map/ppermute | solution.py:888
  92.4 4.7 %collective-permute-done.23 = f32[4,4,128]{2,1,0:T(4,128)S(1)} collective-permute-done((f32[4,4,128]{2,1,0:T(4,128)S(1)}, f32[4,4,128]{2,1,0:T(4,128)S(1)}, u32[]{:S(2)}, u32[]{:S(2)}) %collective-permute-start.23) | collective-permute-done | bytes 8224 | tf_op jit(solution)/shard_map/ppermute | solution.py:888
  101.2 1.9 %collective-permute-done.26.refs_1_ = f32[20,4,128]{2,1,0:T(4,128)S(1)} collective-permute-done((f32[20,4,128]{2,1,0:T(4,128)S(1)}, f32[20,4,128]{2,1,0:T(4,128)S(1)}, u32[]{:S(2)}, u32[]{:S(2)}) %collective-permute-start.26) | collective-permute-done | bytes 40992 | tf_op jit(solution)/shard_map/ppermute | solution.py:888
  103.5 2.6 %level_3.1 = f32[4,4,32]{2,1,0:T(4,128)} custom-call(f32[20,4,128]{2,1,0:T(4,128)S(1)} %collective-permute-done.25.refs_0_, f32[20,4,128]{2,1,0:T(4,128)S(1)} %collective-permute-done.26.refs_1_, f32[20,4,128]{2,1,0:T(4,128)S(1)} %constant_dynamic-update-slice_fusion.refs_2_, f32[20,4,128]{2,1,0:T(4,128)S(1)} %collective-permute-done.27.refs_3_, ...), custom_call_target="tpu_custom_call" | custom-call | tf_op jit(solution)/shard_map/level_3/pallas_call | solution.py:146
  (70 shorter events, 24.1 us)
Async XLA Ops:
  3.2 15.0 %collective-permute-start = (f32[14,32,256]{2,1,0:T(8,128)}, f32[14,32,256]{2,1,0:T(8,128)S(1)}, u32[]{:S(2)}, u32[]{:S(2)}) collective-permute-start(f32[14,32,256]{2,1,0:T(8,128)} %get-tuple-element.97), channel_id=1, source_target_pairs={{0,8},{8,0},{16,24},{24,16},{1,9},{9,1},{17,25},{25,17},{2,10},{10... | collective-permute-start | bytes 1376264 | tf_op jit(solution)/shard_map/ppermute | solution.py:864
  6.3 16.6 %collective-permute-start.1 = (f32[14,32,256]{2,1,0:T(8,128)}, f32[14,32,256]{2,1,0:T(8,128)S(1)}, u32[]{:S(2)}, u32[]{:S(2)}) collective-permute-start(f32[14,32,256]{2,1,0:T(8,128)} %get-tuple-element.98), channel_id=1, source_target_pairs={{0,0},{8,16},{16,8},{24,24},{1,1},{9,17},{17,9},{25,25},{2,2},{10,... | collective-permute-start | bytes 1376264 | tf_op jit(solution)/shard_map/ppermute | solution.py:864
  8.2 18.5 %collective-permute-start.2 = (f32[112,4,256]{2,1,0:T(4,128)S(1)}, f32[112,4,256]{2,1,0:T(4,128)S(1)}, u32[]{:S(2)}, u32[]{:S(2)}) collective-permute-start(f32[112,4,256]{2,1,0:T(4,128)S(1)} %get-tuple-element.111), channel_id=1, source_target_pairs={{0,1},{1,2},{2,3},{3,4},{4,5},{5,6},{6,7},{7,0},{8,9},{9,10},{10,1... | collective-permute-start | bytes 1376264 | tf_op jit(solution)/shard_map/ppermute | solution.py:853
  8.3 18.5 %collective-permute-start.3 = (f32[112,4,256]{2,1,0:T(4,128)S(1)}, f32[112,4,256]{2,1,0:T(4,128)S(1)}, u32[]{:S(2)}, u32[]{:S(2)}) collective-permute-start(f32[112,4,256]{2,1,0:T(4,128)S(1)} %get-tuple-element.112), channel_id=1, source_target_pairs={{1,0},{2,1},{3,2},{4,3},{5,4},{6,5},{7,6},{0,7},{9,8},{10,9},{11,1... | collective-permute-start | bytes 1376264 | tf_op jit(solution)/shard_map/ppermute | solution.py:853
  14.7 9.6 %collective-permute-start.6 = (f32[36,16,128]{2,1,0:T(8,128)S(1)}, f32[36,16,128]{2,1,0:T(8,128)S(1)}, u32[]{:S(2)}, u32[]{:S(2)}) collective-permute-start(f32[36,16,128]{2,1,0:T(8,128)S(1)} %get-tuple-element.117), channel_id=1, source_target_pairs={{0,8},{8,0},{16,24},{24,16},{1,9},{9,1},{17,25},{25,17},{2,10},{10... | collective-permute-start | bytes 884744 | tf_op jit(solution)/shard_map/ppermute | solution.py:864
  18.1 8.6 %collective-permute-start.7 = (f32[36,16,128]{2,1,0:T(8,128)S(1)}, f32[36,16,128]{2,1,0:T(8,128)S(1)}, u32[]{:S(2)}, u32[]{:S(2)}) collective-permute-start(f32[36,16,128]{2,1,0:T(8,128)S(1)} %get-tuple-element.118), channel_id=1, source_target_pairs={{0,0},{8,16},{16,8},{24,24},{1,1},{9,17},{17,9},{25,25},{2,2},{10,... | collective-permute-start | bytes 884744 | tf_op jit(solution)/shard_map/ppermute | solution.py:864
  23.0 5.3 %collective-permute-start.4 = (f32[28,4,256]{2,1,0:T(4,128)S(1)}, f32[28,4,256]{2,1,0:T(4,128)S(1)}, u32[]{:S(2)}, u32[]{:S(2)}) collective-permute-start(f32[28,4,256]{2,1,0:T(4,128)S(1)} %get-tuple-element.113), channel_id=1, source_target_pairs={{0,1},{1,2},{2,3},{3,4},{4,5},{5,6},{6,7},{7,0},{8,9},{9,10},{10,1... | collective-permute-start | bytes 344072 | tf_op jit(solution)/shard_map/ppermute | solution.py:853
  28.5 22.0 %collective-permute-start.10 = (f32[168,8,128]{2,1,0:T(8,128)S(1)}, f32[168,8,128]{2,1,0:T(8,128)S(1)}, u32[]{:S(2)}, u32[]{:S(2)}) collective-permute-start(f32[168,8,128]{2,1,0:T(8,128)S(1)} %get-tuple-element.150), channel_id=1, source_target_pairs={{0,1},{1,2},{2,3},{3,4},{4,5},{5,6},{6,7},{7,0},{8,9},{9,10},{10,1... | collective-permute-start | bytes 2064392 | tf_op jit(solution)/shard_map/ppermute | solution.py:853
  29.6 21.0 %collective-permute-start.11 = (f32[168,8,128]{2,1,0:T(8,128)S(1)}, f32[168,8,128]{2,1,0:T(8,128)S(1)}, u32[]{:S(2)}, u32[]{:S(2)}) collective-permute-start(f32[168,8,128]{2,1,0:T(8,128)S(1)} %get-tuple-element.151), channel_id=1, source_target_pairs={{1,0},{2,1},{3,2},{4,3},{5,4},{6,5},{7,6},{0,7},{9,8},{10,9},{11,1... | collective-permute-start | bytes 2064392 | tf_op jit(solution)/shard_map/ppermute | solution.py:853
  42.2 6.5 %collective-permute-start.8 = (f32[2,32,256]{2,1,0:T(8,128)S(1)}, f32[2,32,256]{2,1,0:T(8,128)S(1)}, u32[]{:S(2)}, u32[]{:S(2)}) collective-permute-start(f32[2,32,256]{2,1,0:T(8,128)S(1)} %get-tuple-element.146), channel_id=1, source_target_pairs={{0,8},{8,16},{16,24},{24,0},{1,9},{9,17},{17,25},{25,1},{2,10},{10... | collective-permute-start | bytes 196616 | tf_op jit(solution)/shard_map/ppermute | solution.py:853
  50.6 5.6 %collective-permute-start.12 = (f32[20,4,256]{2,1,0:T(4,128)S(1)}, f32[20,4,256]{2,1,0:T(4,128)S(1)}, u32[]{:S(2)}, u32[]{:S(2)}) collective-permute-start(f32[20,4,256]{2,1,0:T(4,128)S(1)} %get-tuple-element.152), channel_id=1, source_target_pairs={{0,1},{1,2},{2,3},{3,4},{4,5},{5,6},{6,7},{7,0},{8,9},{9,10},{10,1... | collective-permute-start | bytes 245768 | tf_op jit(solution)/shard_map/ppermute | solution.py:853
  50.6 5.6 %collective-permute-start.13 = (f32[20,4,256]{2,1,0:T(4,128)S(1)}, f32[20,4,256]{2,1,0:T(4,128)S(1)}, u32[]{:S(2)}, u32[]{:S(2)}) collective-permute-start(f32[20,4,256]{2,1,0:T(4,128)S(1)} %get-tuple-element.153), channel_id=1, source_target_pairs={{1,0},{2,1},{3,2},{4,3},{5,4},{6,5},{7,6},{0,7},{9,8},{10,9},{11,1... | collective-permute-start | bytes 245768 | tf_op jit(solution)/shard_map/ppermute | solution.py:853
  60.3 6.6 %collective-permute-start.14 = (f32[8,16,128]{2,1,0:T(8,128)S(1)}, f32[8,16,128]{2,1,0:T(8,128)S(1)}, u32[]{:S(2)}, u32[]{:S(2)}) collective-permute-start(f32[8,16,128]{2,1,0:T(8,128)S(1)} %get-tuple-element.165), channel_id=1, source_target_pairs={{0,8},{8,16},{16,24},{24,0},{1,9},{9,17},{17,25},{25,1},{2,10},{10... | collective-permute-start | bytes 196616 | tf_op jit(solution)/shard_map/ppermute | solution.py:853
  60.4 6.5 %collective-permute-start.15 = (f32[8,16,128]{2,1,0:T(8,128)S(1)}, f32[8,16,128]{2,1,0:T(8,128)S(1)}, u32[]{:S(2)}, u32[]{:S(2)}) collective-permute-start(f32[8,16,128]{2,1,0:T(8,128)S(1)} %get-tuple-element.166), channel_id=1, source_target_pairs={{8,0},{16,8},{24,16},{0,24},{9,1},{17,9},{25,17},{1,25},{10,2},{18... | collective-permute-start | bytes 196616 | tf_op jit(solution)/shard_map/ppermute | solution.py:853
  66.9 6.0 %collective-permute-start.16 = (f32[32,8,128]{2,1,0:T(8,128)S(1)}, f32[32,8,128]{2,1,0:T(8,128)S(1)}, u32[]{:S(2)}, u32[]{:S(2)}) collective-permute-start(f32[32,8,128]{2,1,0:T(8,128)S(1)} %get-tuple-element.184), channel_id=1, source_target_pairs={{0,1},{1,2},{2,3},{3,4},{4,5},{5,6},{6,7},{7,0},{8,9},{9,10},{10,1... | collective-permute-start | bytes 393224 | tf_op jit(solution)/shard_map/ppermute | solution.py:853
  67.0 5.9 %collective-permute-start.17 = (f32[32,8,128]{2,1,0:T(8,128)S(1)}, f32[32,8,128]{2,1,0:T(8,128)S(1)}, u32[]{:S(2)}, u32[]{:S(2)}) collective-permute-start(f32[32,8,128]{2,1,0:T(8,128)S(1)} %get-tuple-element.185), channel_id=1, source_target_pairs={{1,0},{2,1},{3,2},{4,3},{5,4},{6,5},{7,6},{0,7},{9,8},{10,9},{11,1... | collective-permute-start | bytes 393224 | tf_op jit(solution)/shard_map/ppermute | solution.py:853
  75.5 5.8 %collective-permute-start.18 = (f32[8,8,128]{2,1,0:T(8,128)S(1)}, f32[8,8,128]{2,1,0:T(8,128)S(1)}, u32[]{:S(2)}, u32[]{:S(2)}) collective-permute-start(f32[8,8,128]{2,1,0:T(8,128)S(1)} %get-tuple-element.187), channel_id=1, source_target_pairs={{0,8},{8,16},{16,24},{24,0},{1,9},{9,17},{17,25},{25,1},{2,10},{10... | collective-permute-start | bytes 98312 | tf_op jit(solution)/shard_map/ppermute | solution.py:853
  75.6 5.7 %collective-permute-start.19 = (f32[8,8,128]{2,1,0:T(8,128)S(1)}, f32[8,8,128]{2,1,0:T(8,128)S(1)}, u32[]{:S(2)}, u32[]{:S(2)}) collective-permute-start(f32[8,8,128]{2,1,0:T(8,128)S(1)} %get-tuple-element.188), channel_id=1, source_target_pairs={{8,0},{16,8},{24,16},{0,24},{9,1},{17,9},{25,17},{1,25},{10,2},{18... | collective-permute-start | bytes 98312 | tf_op jit(solution)/shard_map/ppermute | solution.py:853
  81.3 5.1 %collective-permute-start.20 = (f32[24,8,128]{2,1,0:T(8,128)S(1)}, f32[24,8,128]{2,1,0:T(8,128)S(1)}, u32[]{:S(2)}, u32[]{:S(2)}) collective-permute-start(f32[24,8,128]{2,1,0:T(8,128)S(1)} %get-tuple-element.189), channel_id=1, source_target_pairs={{0,1},{1,2},{2,3},{3,4},{4,5},{5,6},{6,7},{7,0},{8,9},{9,10},{10,1... | collective-permute-start | bytes 294920 | tf_op jit(solution)/shard_map/ppermute | solution.py:853
  81.3 5.0 %collective-permute-start.21 = (f32[24,8,128]{2,1,0:T(8,128)S(1)}, f32[24,8,128]{2,1,0:T(8,128)S(1)}, u32[]{:S(2)}, u32[]{:S(2)}) collective-permute-start(f32[24,8,128]{2,1,0:T(8,128)S(1)} %get-tuple-element.190), channel_id=1, source_target_pairs={{1,0},{2,1},{3,2},{4,3},{5,4},{6,5},{7,6},{0,7},{9,8},{10,9},{11,1... | collective-permute-start | bytes 294920 | tf_op jit(solution)/shard_map/ppermute | solution.py:853
  90.3 6.9 %collective-permute-start.24 = (f32[4,4,128]{2,1,0:T(4,128)S(1)}, f32[4,4,128]{2,1,0:T(4,128)S(1)}, u32[]{:S(2)}, u32[]{:S(2)}) collective-permute-start(f32[4,4,128]{2,1,0:T(4,128)S(1)} %level_2.1), channel_id=1, source_target_pairs={{0,24},{8,0},{16,8},{24,16},{1,25},{9,1},{17,9},{25,17},{2,26},{10... | collective-permute-start | bytes 24584 | tf_op jit(solution)/shard_map/ppermute | solution.py:888
  91.7 5.4 %collective-permute-start.23 = (f32[4,4,128]{2,1,0:T(4,128)S(1)}, f32[4,4,128]{2,1,0:T(4,128)S(1)}, u32[]{:S(2)}, u32[]{:S(2)}) collective-permute-start(f32[4,4,128]{2,1,0:T(4,128)S(1)} %level_2.1), channel_id=1, source_target_pairs={{0,8},{8,16},{16,24},{24,0},{1,9},{9,17},{17,25},{25,1},{2,10},{10... | collective-permute-start | bytes 24584 | tf_op jit(solution)/shard_map/ppermute | solution.py:888
  98.5 4.6 %collective-permute-start.26 = (f32[20,4,128]{2,1,0:T(4,128)S(1)}, f32[20,4,128]{2,1,0:T(4,128)S(1)}, u32[]{:S(2)}, u32[]{:S(2)}) collective-permute-start(f32[20,4,128]{2,1,0:T(4,128)S(1)} %constant_dynamic-update-slice_fusion.refs_2_), channel_id=1, source_target_pairs={{0,1},{1,2},{2,3},{3,4},{4,5},{5,6},{6,7},{7,0},{8,9},{9,10},{10,1... | collective-permute-start | bytes 122888 | tf_op jit(solution)/shard_map/ppermute | solution.py:888
  98.5 4.9 %collective-permute-start.25 = (f32[20,4,128]{2,1,0:T(4,128)S(1)}, f32[20,4,128]{2,1,0:T(4,128)S(1)}, u32[]{:S(2)}, u32[]{:S(2)}) collective-permute-start(f32[20,4,128]{2,1,0:T(4,128)S(1)} %constant_dynamic-update-slice_fusion.refs_2_), channel_id=1, source_target_pairs={{0,2},{1,3},{2,4},{3,5},{4,6},{5,7},{6,0},{7,1},{8,10},{9,11},{10,... | collective-permute-start | bytes 122888 | tf_op jit(solution)/shard_map/ppermute | solution.py:888
  (11 other events, 60.0 us)
